TPU v7x, 32 devices: a whole 2x2x4 slice. The times are simulated.
32 devices in a mesh: dp: 8 (over y, x, core), seq: 4 (over z).
Axes of the slice: x: 2, y: 2, z: 4, core: 2. Of those that a mesh axis runs over, the one named last changes fastest.
Arguments:
- tokens: bfloat16 [8, 512, 6, 768], P('dp', 'seq'), may hold values from -6 to 6
- kind: int32 [8], P('dp'), may hold values from 0 to 1, as said below
- ln1_gain: float32 [768], replicated, may hold values from 0.1 to 1.9
- w_in: bfloat16 [768, 2304], replicated, may hold values from -0.21875 to 0.21875
- short_taps: float32 [3, 2304], replicated, may hold values from -3 to 3
- cond_taps: float32 [3, 768], replicated, may hold values from -3 to 3
- w_cond: bfloat16 [768, 768], replicated, may hold values from -0.21875 to 0.21875
- cond_bias: float32 [768], replicated, may hold values from -3 to 3
- w_out: bfloat16 [768, 768], replicated, may hold values from -0.21875 to 0.21875
- ln2_gain: float32 [768], replicated, may hold values from 0.1 to 1.9
- w_gate: bfloat16 [768, 3072], replicated, may hold values from -0.21875 to 0.21875
- w_up: bfloat16 [768, 3072], replicated, may hold values from -0.21875 to 0.21875
- w_down: bfloat16 [3072, 768], replicated, may hold values from -0.109375 to 0.109375
- cotangent: bfloat16 [8, 512, 6, 768], P('dp', 'seq'), may hold values from -6 to 6
Outputs:
- layer_out: bfloat16 [8, 512, 6, 768], P('dp', 'seq')
- grad_tokens: bfloat16 [8, 512, 6, 768], P('dp', 'seq')
- grad_ln1: float32 [768], P('seq')
- grad_w_in: float32 [768, 2304], P('seq')
- grad_short_taps: float32 [3, 2304], P(None, 'seq')
- grad_cond_taps: float32 [3, 768], P(None, 'seq')
- grad_w_cond: float32 [768, 768], P('seq')
- grad_cond_bias: float32 [768], P('seq')
- grad_w_out: float32 [768, 768], P('seq')
- grad_ln2: float32 [768], P('seq')
- grad_gate: float32 [768, 3072], P('seq')
- grad_up: float32 [768, 3072], P('seq')
- grad_down: float32 [3072, 768], P('seq')
Inputs may be any that keep to these rules, and one draw needn't show every extreme that they name: Exactly 4 groups have kind 1.
All inputs are finite; a program needn't handle non-finite values.
Results may differ from a plain program's by a relative error of at most 0.017.
Values may be sent and summed in bfloat16 or wider, within the bound.
A program may use at most 256 MiB of HBM per device.

v0:
```python
import math

import jax
import jax.numpy as jnp
from jax import lax
from jax.sharding import PartitionSpec as P

highest = lax.Precision.HIGHEST
epsilon = 1e-05


def from_behind(value, axis, by):
    peers = lax.axis_size(axis)
    pairs = [(i, i + by) for i in range(peers) if 0 <= i + by < peers]
    return lax.ppermute(value, axis, pairs)


def norm_rows(values, scale_gain):
    row_mean = jnp.mean(values, axis=-1, keepdims=True)
    centered = values - row_mean
    scale_inv = lax.rsqrt(jnp.mean(centered * centered, axis=-1, keepdims=True) + epsilon)
    normed = centered * scale_inv
    return (normed * scale_gain, normed, scale_inv)


def norm_back(grad_out, normed, scale_inv, scale_gain):
    grad_gain = jnp.sum(grad_out * normed, axis=0)
    grad_normed = grad_out * scale_gain
    inner_mean = jnp.mean(grad_normed, axis=-1, keepdims=True)
    inner_cross = jnp.mean(grad_normed * normed, axis=-1, keepdims=True)
    return (scale_inv * (grad_normed - inner_mean - normed * inner_cross), grad_gain)


def wave_tables(freq_ids, time_ids, span_len):
    fold_freq = freq_ids[:, None] % span_len
    fold_time = time_ids[None, :] % span_len
    same_block = (freq_ids[:, None] // span_len == time_ids[None, :] // span_len).astype(
        jnp.float32
    )
    phase_index = fold_freq * fold_time % span_len
    phase_angle = phase_index.astype(jnp.float32) * (2.0 * math.pi) / span_len.astype(jnp.float32)
    return (jnp.cos(phase_angle) * same_block, jnp.sin(phase_angle) * same_block)


def conv_forward(extended, taps):
    return taps[0] * extended[2:] + taps[1] * extended[1:-1] + taps[2] * extended[:-2]


def conv_backward(grad_out, extended, taps, long_flag):
    count_rows = grad_out.shape[0]
    zero_pad = jnp.zeros((2,) + grad_out.shape[1:], jnp.float32)
    padded = jnp.concatenate([grad_out, zero_pad], axis=0)
    grad_local = (
        taps[0] * padded[:count_rows] + taps[1] * padded[1 : count_rows + 1] + taps[2] * padded[2:]
    )
    grad_rim = (
        jnp.stack([taps[2] * grad_out[0], taps[1] * grad_out[0] + taps[2] * grad_out[1]])
        * long_flag
    )
    grad_taps = jnp.stack(
        [
            jnp.sum(grad_out * extended[2:], axis=(0, 1)),
            jnp.sum(grad_out * extended[1:-1], axis=(0, 1)),
            jnp.sum(grad_out * extended[:-2], axis=(0, 1)),
        ]
    )
    return (grad_local, grad_rim, grad_taps)


def on_device(
    tokens,
    kind,
    ln1_gain,
    w_in,
    short_taps,
    cond_taps,
    w_cond,
    cond_bias,
    w_out,
    ln2_gain,
    w_gate,
    w_up,
    w_down,
    cotangent,
):
    piece_rows = tokens.shape[1]
    slot_count = tokens.shape[2]
    model_width = tokens.shape[3]
    flat_rows = piece_rows * slot_count
    seq_count = lax.axis_size("seq")
    seq_rank = lax.axis_index("seq")
    is_long = kind[0]
    long_flag = is_long.astype(jnp.float32)
    span_len = jnp.where(is_long == 1, piece_rows * seq_count, piece_rows).astype(jnp.int32)
    span_float = span_len.astype(jnp.float32)
    freq_ids = seq_rank * piece_rows + jnp.arange(piece_rows, dtype=jnp.int32)
    token_rows = tokens.reshape(flat_rows, model_width).astype(jnp.float32)
    normed_one, unit_one, inv_one = norm_rows(token_rows, ln1_gain)
    normed_one_low = normed_one.astype(jnp.bfloat16)
    projected = jnp.dot(normed_one_low, w_in, preferred_element_type=jnp.float32)
    proj_low = projected.astype(jnp.bfloat16).reshape(piece_rows, slot_count, 3 * model_width)
    proj_f = proj_low.astype(jnp.float32)
    rim_proj = from_behind(proj_low[piece_rows - 2 :], "seq", 1).astype(jnp.float32) * long_flag
    extended_proj = jnp.concatenate([rim_proj, proj_f], axis=0)
    conv_out = conv_forward(extended_proj, short_taps)
    query_conv = conv_out[:, :, :model_width]
    key_conv = conv_out[:, :, model_width : 2 * model_width]
    value_low = conv_out[:, :, 2 * model_width :].astype(jnp.bfloat16)
    value_f = value_low.astype(jnp.float32)
    rim_value = from_behind(value_low[piece_rows - 2 :], "seq", 1).astype(jnp.float32) * long_flag
    extended_value = jnp.concatenate([rim_value, value_f], axis=0)
    cond_low = conv_forward(extended_value, cond_taps).astype(jnp.bfloat16)
    signal_low = (key_conv * value_f).astype(jnp.bfloat16)
    sig_piece = lax.all_gather(signal_low, "seq", axis=0, tiled=True).astype(jnp.float32)
    cond_piece = lax.all_gather(cond_low, "seq", axis=0, tiled=True).astype(jnp.float32)
    time_ids = jnp.arange(sig_piece.shape[0], dtype=jnp.int32)
    cos_table, sin_table = wave_tables(freq_ids, time_ids, span_len)
    sig_cos = jnp.einsum("ft,tsd->fsd", cos_table, sig_piece, precision=highest)
    sig_sin = jnp.einsum("ft,tsd->fsd", sin_table, sig_piece, precision=highest)
    cond_cos = jnp.einsum("ft,tsd->fsd", cos_table, cond_piece, precision=highest)
    cond_sin = jnp.einsum("ft,tsd->fsd", sin_table, cond_piece, precision=highest)
    power_spec = (cond_cos * cond_cos + cond_sin * cond_sin) / span_float
    features_low = jnp.log1p(power_spec).astype(jnp.bfloat16).reshape(flat_rows, model_width)
    pre_tanh = jnp.dot(features_low, w_cond, preferred_element_type=jnp.float32) + cond_bias
    tanh_value = jnp.tanh(pre_tanh).reshape(piece_rows, slot_count, model_width)
    spectral_gain = 1.0 + tanh_value
    gained_cos = spectral_gain * sig_cos
    gained_sin = spectral_gain * sig_sin
    time_ids = jnp.arange(piece_rows * lax.axis_size("seq"), dtype=jnp.int32)
    cos_table, sin_table = wave_tables(freq_ids, time_ids, span_len)
    term = jnp.einsum("ft,fsd->tsd", cos_table, gained_cos, precision=highest) + jnp.einsum(
        "ft,fsd->tsd", sin_table, gained_sin, precision=highest
    )
    filtered = lax.psum_scatter(
        (term / span_float).astype(jnp.bfloat16), "seq", scatter_dimension=0, tiled=True
    ).astype(jnp.float32)
    mixed_low = (query_conv * filtered).astype(jnp.bfloat16).reshape(flat_rows, model_width)
    hidden_one = token_rows + jnp.dot(mixed_low, w_out, preferred_element_type=jnp.float32)
    normed_two, unit_two, inv_two = norm_rows(hidden_one, ln2_gain)
    normed_two_low = normed_two.astype(jnp.bfloat16)
    gate_pre = jnp.dot(normed_two_low, w_gate, preferred_element_type=jnp.float32)
    up_proj = jnp.dot(normed_two_low, w_up, preferred_element_type=jnp.float32)
    gate_sig = jax.nn.sigmoid(gate_pre)
    gate_act = gate_pre * gate_sig
    hidden_act = (gate_act * up_proj).astype(jnp.bfloat16)
    layer_rows = hidden_one + jnp.dot(hidden_act, w_down, preferred_element_type=jnp.float32)
    layer_out = layer_rows.astype(jnp.bfloat16).reshape(tokens.shape)
    cot_rows = cotangent.reshape(flat_rows, model_width)
    grad_down = jnp.einsum("nf,nd->fd", hidden_act, cot_rows, preferred_element_type=jnp.float32)
    grad_act = jnp.einsum("nd,fd->nf", cot_rows, w_down, preferred_element_type=jnp.float32)
    grad_gate_pre = (grad_act * up_proj * gate_sig * (1.0 + gate_pre * (1.0 - gate_sig))).astype(
        jnp.bfloat16
    )
    grad_up_proj = (grad_act * gate_act).astype(jnp.bfloat16)
    grad_gate = jnp.einsum(
        "nd,nf->df", normed_two_low, grad_gate_pre, preferred_element_type=jnp.float32
    )
    grad_up = jnp.einsum(
        "nd,nf->df", normed_two_low, grad_up_proj, preferred_element_type=jnp.float32
    )
    grad_normed_two = jnp.einsum(
        "nf,df->nd", grad_gate_pre, w_gate, preferred_element_type=jnp.float32
    ) + jnp.einsum("nf,df->nd", grad_up_proj, w_up, preferred_element_type=jnp.float32)
    grad_hidden_part, grad_ln2 = norm_back(grad_normed_two, unit_two, inv_two, ln2_gain)
    grad_hidden = cot_rows.astype(jnp.float32) + grad_hidden_part
    grad_mix_low = grad_hidden.astype(jnp.bfloat16)
    grad_w_out = jnp.einsum(
        "nd,ne->de", mixed_low, grad_mix_low, preferred_element_type=jnp.float32
    )
    grad_mixed = jnp.einsum(
        "ne,de->nd", grad_mix_low, w_out, preferred_element_type=jnp.float32
    ).reshape(piece_rows, slot_count, model_width)
    grad_query = grad_mixed * filtered
    grad_filtered_low = (grad_mixed * query_conv).astype(jnp.bfloat16)
    grad_piece = lax.all_gather(grad_filtered_low, "seq", axis=0, tiled=True).astype(jnp.float32)
    time_ids = jnp.arange(grad_piece.shape[0], dtype=jnp.int32)
    cos_table, sin_table = wave_tables(freq_ids, time_ids, span_len)
    back_cos = jnp.einsum("ft,tsd->fsd", cos_table, grad_piece, precision=highest)
    back_sin = jnp.einsum("ft,tsd->fsd", sin_table, grad_piece, precision=highest)
    back_cos = back_cos / span_float
    back_sin = back_sin / span_float
    grad_gain_spec = back_cos * sig_cos + back_sin * sig_sin
    grad_sig_cos = spectral_gain * back_cos
    grad_sig_sin = spectral_gain * back_sin
    grad_pre_low = (
        (grad_gain_spec * (1.0 - tanh_value * tanh_value))
        .astype(jnp.bfloat16)
        .reshape(flat_rows, model_width)
    )
    grad_w_cond = jnp.einsum(
        "nc,nd->cd", features_low, grad_pre_low, preferred_element_type=jnp.float32
    )
    grad_cond_bias = jnp.sum(grad_pre_low.astype(jnp.float32), axis=0)
    grad_features = jnp.einsum(
        "nd,cd->nc", grad_pre_low, w_cond, preferred_element_type=jnp.float32
    ).reshape(piece_rows, slot_count, model_width)
    grad_power = grad_features / (1.0 + power_spec)
    grad_cond_cos = 2.0 * cond_cos * grad_power / span_float
    grad_cond_sin = 2.0 * cond_sin * grad_power / span_float
    time_ids = jnp.arange(piece_rows * lax.axis_size("seq"), dtype=jnp.int32)
    cos_table, sin_table = wave_tables(freq_ids, time_ids, span_len)
    signal_term = jnp.einsum(
        "ft,fsd->tsd", cos_table, grad_sig_cos, precision=highest
    ) + jnp.einsum("ft,fsd->tsd", sin_table, grad_sig_sin, precision=highest)
    cond_term = jnp.einsum("ft,fsd->tsd", cos_table, grad_cond_cos, precision=highest) + jnp.einsum(
        "ft,fsd->tsd", sin_table, grad_cond_sin, precision=highest
    )
    source_grads = lax.psum_scatter(
        jnp.concatenate([signal_term, cond_term], axis=2).astype(jnp.bfloat16),
        "seq",
        scatter_dimension=0,
        tiled=True,
    ).astype(jnp.float32)
    grad_signal = source_grads[:, :, :model_width]
    grad_cond = source_grads[:, :, model_width:]
    grad_value_cond, grad_value_rim, grad_cond_taps = conv_backward(
        grad_cond, extended_value, cond_taps, long_flag
    )
    grad_value = grad_signal * key_conv + grad_value_cond
    grad_key = grad_signal * value_f
    value_back = from_behind(grad_value_rim.astype(jnp.bfloat16), "seq", -1).astype(
        grad_value_rim.dtype
    )
    grad_value = jnp.concatenate(
        [grad_value[: piece_rows - 2], grad_value[piece_rows - 2 :] + value_back], axis=0
    )
    grad_conv = jnp.concatenate([grad_query, grad_key, grad_value], axis=2)
    grad_proj_local, grad_proj_rim, grad_short_taps = conv_backward(
        grad_conv, extended_proj, short_taps, long_flag
    )
    proj_back = from_behind(grad_proj_rim.astype(jnp.bfloat16), "seq", -1).astype(
        grad_proj_rim.dtype
    )
    grad_proj = jnp.concatenate(
        [grad_proj_local[: piece_rows - 2], grad_proj_local[piece_rows - 2 :] + proj_back], axis=0
    )
    grad_proj_low = grad_proj.astype(jnp.bfloat16).reshape(flat_rows, 3 * model_width)
    grad_w_in = jnp.einsum(
        "nd,ne->de", normed_one_low, grad_proj_low, preferred_element_type=jnp.float32
    )
    grad_normed_one = jnp.einsum(
        "ne,de->nd", grad_proj_low, w_in, preferred_element_type=jnp.float32
    )
    grad_token_part, grad_ln1 = norm_back(grad_normed_one, unit_one, inv_one, ln1_gain)
    grad_tokens = (grad_hidden + grad_token_part).astype(jnp.bfloat16).reshape(tokens.shape)
    whole_sums = lax.psum(
        (
            grad_ln1,
            grad_w_in,
            grad_short_taps,
            grad_cond_taps,
            grad_w_cond,
            grad_cond_bias,
            grad_w_out,
            grad_ln2,
            grad_gate,
            grad_up,
            grad_down,
        ),
        ("dp", "seq"),
    )
    seq_dims = (0, 0, 1, 1, 0, 0, 0, 0, 0, 0, 0)
    summed = tuple(
        (
            lax.dynamic_slice_in_dim(
                whole_sum,
                seq_rank * (whole_sum.shape[axis_dim] // seq_count),
                whole_sum.shape[axis_dim] // seq_count,
                axis_dim,
            )
            for whole_sum, axis_dim in zip(whole_sums, seq_dims)
        )
    )
    return (
        layer_out,
        grad_tokens,
        summed[0],
        summed[1],
        summed[2],
        summed[3],
        summed[4],
        summed[5],
        summed[6],
        summed[7],
        summed[8],
        summed[9],
        summed[10],
    )


def solution(mesh):
    return jax.shard_map(
        on_device,
        mesh=mesh,
        in_specs=(
            P("dp", "seq", None, None),
            P("dp"),
            P(),
            P(),
            P(),
            P(),
            P(),
            P(),
            P(),
            P(),
            P(),
            P(),
            P(),
            P("dp", "seq", None, None),
        ),
        out_specs=(
            P("dp", "seq", None, None),
            P("dp", "seq", None, None),
            P("seq"),
            P("seq", None),
            P(None, "seq"),
            P(None, "seq"),
            P("seq", None),
            P("seq"),
            P("seq", None),
            P("seq"),
            P("seq", None),
            P("seq", None),
            P("seq", None),
        ),
        check_vma=False,
    )
```

profile of v0, /device:TPU:25, one launch (start us, length us, event | category | flops | bytes accessed | tf_op | source)
XLA Modules:
  0.0 1423.5 jit_solution(9233570854723160421)
XLA Ops:
  34.4 6.8 reshape.285
  41.2 6.0 copy.77
  60.3 88.4 %all-gather.4.cloned.1.call-done = bf16[512,6,768]{2,0,1:T(8,128)(2,1)} async-done(((bf16[128,6,768]{2,0,1:T(8,128)(2,1)}), bf16[512,6,768]{2,0,1:T(8,128)(2,1)}) %all-gather.4.cloned.1.call-update) | async-done | bytes 4718608 | tf_op jit(solution)/shard_map/all_gather | solution.py:115
  148.7 8.0 fusion.64
  156.7 8.2 log-plus-one_convert_fusion
  179.6 59.2 %all-gather.6.cloned.1.call-done = bf16[512,6,768]{2,0,1:T(8,128)(2,1)} async-done(((bf16[128,6,768]{2,0,1:T(8,128)(2,1)}), bf16[512,6,768]{2,0,1:T(8,128)(2,1)}) %all-gather.6.cloned.1.call-update) | async-done | bytes 4718608 | tf_op jit(solution)/shard_map/all_gather | solution.py:114
  238.8 7.8 fusion.62
  246.6 11.7 fusion.26
  265.3 14.8 %divide_convert_fusion = bf16[512,6,768]{2,0,1:T(8,128)(2,1)} fusion(f32[512,6,768]{2,0,1:T(8,128)S(1)} %fusion.26, f32[]{:T(128)S(6)} %convert_element_type.160, f32[128,6,768]{2,0,1:T(8,128)S(1)} %fusion.54, f32[128,6,768]{2,1,0:T(8,128)S(1)} %copy-done.2, s32[]{:T(128)S(6)} %select_n.103, s32[512]{0:T(512)S(1)} %get-tuple-element.107, ...), kind=kOutput, calls=%fused_computation.8 | convolution fusion | flops 3632332800 | bytes 18879496 | tf_op jit(solution)/shard_map/ft,fsd->tsd/dot_general | solution.py:131
  286.7 79.4 %reduce-scatter.3.cloned.1.call-done = bf16[128,6,768]{2,0,1:T(8,128)(2,1)} async-done(((bf16[512,6,768]{2,0,1:T(8,128)(2,1)}), bf16[128,6,768]{2,0,1:T(8,128)(2,1)}) %reduce-scatter.3.cloned.1.call-update) | async-done | bytes 1179664 | tf_op jit(solution)/shard_map/reduce_scatter | solution.py:134
  378.0 9.2 fusion.142
  387.3 6.2 fusion.143
  393.5 17.3 %multiply_convert_fusion = (bf16[768,3072]{1,0:T(8,128)(2,1)}, bf16[768,3072]{1,0:T(8,128)(2,1)}, bf16[768,3072]{1,0:T(8,128)(2,1)}) fusion(f32[768,3072]{1,0:T(8,128)} %fusion.142, f32[768,3072]{1,0:T(8,128)} %fusion.143, bf16[768,768]{1,0:T(8,128)(2,1)S(1)} %copy-done.31, bf16[3072,768]{1,0:T(8,128)(2,1)} %param.26), kind=kOutput, calls=%fused_computation.3 | convolution fusion | flops 3659268096 | bytes 38928384 | tf_op jit(solution)/shard_map/nd,fd->nf/dot_general | solution.py:150
  410.8 7.7 fusion.144
  418.6 7.3 multiply_reduce_fusion.2
  434.5 5.7 convert_multiply_fusion
  444.1 84.2 %all-gather.8.cloned.1.call-done = bf16[512,6,768]{2,0,1:T(8,128)(2,1)} async-done(((bf16[128,6,768]{2,0,1:T(8,128)(2,1)}), bf16[512,6,768]{2,0,1:T(8,128)(2,1)}) %all-gather.8.cloned.1.call-update) | async-done | bytes 4718608 | tf_op jit(solution)/shard_map/all_gather | solution.py:175
  528.3 7.9 convolution_divide_fusion.1
  536.3 11.6 fusion.23
  548.0 9.2 convert_reduce_fusion
  561.4 11.2 fusion.18
  572.7 15.4 %add_convert_fusion = bf16[512,6,768]{2,0,1:T(8,128)(2,1)} fusion(f32[512,6,768]{2,0,1:T(8,128)S(1)} %fusion.18, f32[128,6,768]{2,0,1:T(8,128)S(1)} %add_divide_fusion.1, f32[128,6,768]{2,0,1:T(8,128)} %get-tuple-element.101, f32[]{:T(128)S(6)} %convert_element_type.160, s32[]{:T(128)S(6)} %select_n.103, s32[512]{0:T(512)S(1)} %get-tuple-element.107, ...), kind=kOutput, calls=%fused_computation.1 | convolution fusion | flops 3631153152 | bytes 18879496 | tf_op jit(solution)/shard_map/ft,fsd->tsd/dot_general | solution.py:205
  588.0 15.3 %add_convert_fusion.1 = bf16[512,6,768]{2,0,1:T(8,128)(2,1)S(1)} fusion(f32[512,6,768]{2,0,1:T(8,128)S(1)} %fusion.23, f32[128,6,768]{2,0,1:T(8,128)} %get-tuple-element.105, f32[128,6,768]{2,1,0:T(8,128)S(1)} %copy-done.3, f32[]{:T(128)S(6)} %convert_element_type.160, s32[]{:T(128)S(6)} %select_n.103, s32[512]{0:T(512)S(1)} %get-tuple-element.107, ...), kind=kOutput, calls=%fused_computation.2 | convolution fusion | flops 3629973504 | bytes 18879496 | tf_op jit(solution)/shard_map/ft,fsd->tsd/dot_general | solution.py:204
  620.5 8.8 fusion.146
  629.3 6.3 fusion.147
  635.7 6.3 fusion.148
  644.6 125.4 %reduce-scatter.5.cloned.1.call-done = bf16[128,6,1536]{2,0,1:T(8,128)(2,1)} async-done(((bf16[512,6,1536]{2,0,1:T(8,128)(2,1)}), bf16[128,6,1536]{2,0,1:T(8,128)(2,1)}) %reduce-scatter.5.cloned.1.call-update) | async-done | bytes 2359312 | tf_op jit(solution)/shard_map/reduce_scatter | solution.py:208
  794.8 6.6 convert_element_type.184
  801.4 8.2 fusion.145
  814.6 9.7 add_convert_fusion.3
  874.5 43.3 %all-reduce.2 = (f32[768]{0:T(1024)}, f32[3,2304]{1,0:T(4,128)}, f32[3,768]{1,0:T(4,128)}, f32[768]{0:T(1024)}, f32[768]{0:T(1024)}) all-reduce(f32[768]{0:T(1024)} %get-tuple-element.58, f32[3,2304]{1,0:T(4,128)} %pad_maximum_fusion.4, f32[3,768]{1,0:T(4,128)S(1)} %copy-done.56, ...), channel_id=1, replica_groups=mesh['dp'=8,'seq'=4] {'dp','seq'}, use_global_device_ids=true, to_apply=%region_11.12 | all-reduce | flops 11520 | bytes 92160 | tf_op jit(solution)/shard_map/psum | solution.py:246
  924.6 475.4 %all-reduce.6.cloned.1.call-done = (f32[768,2304]{1,0:T(8,128)}, f32[768,768]{1,0:T(8,128)}, f32[768,768]{1,0:T(8,128)}, f32[768,3072]{1,0:T(8,128)}, f32[768,3072]{1,0:T(8,128)}, /*index=5*/f32[3072,768]{1,0:T(8,128)}) async-done(((f32[768,2304]{1,0:T(8,128)}, f32[768,768]{1,0:T(8,128)}, f32[768,768]{1,0:T(8,128)}, f32[768,3072]{1,0:T(8,128)}, f32[768,3072]{1,0:T(8,128)}, ...) | async-done | bytes 40108048 | tf_op jit(solution)/shard_map/psum | solution.py:246
  (293 shorter events, 218.7 us)
Async XLA Ops:
  7.2 11.9 copy-start
  7.2 141.5 %all-gather.4.cloned.1.call-start = ((), (), s32[]{:S(2)}) async-start(), calls=%async_computation.2 | async-start | bytes 5898240 | tf_op jit(solution)/shard_map/all_gather | solution.py:115
  30.1 17.7 %collective-permute-start = (bf16[2,6,2304]{2,0,1:T(2,128)(2,1)}, bf16[2,6,2304]{2,0,1:T(2,128)(2,1)}, u32[]{:S(2)}, u32[]{:S(2)}) collective-permute-start(bf16[2,6,2304]{2,0,1:T(2,128)(2,1)} %copy.78), channel_id=1, source_target_pairs={{0,1},{1,2},{2,3},{4,5},{5,6},{6,7},{8,9},{9,10},{10,11},{12,13},{... | collective-permute-start | bytes 165896 | tf_op jit(solution)/shard_map/ppermute | solution.py:15
  33.0 15.8 %copy-start.44 = (f32[2304]{0:T(1024)}, f32[2304]{0:T(1024)S(1)}, u32[]{:S(2)}) copy-start(f32[2304]{0:T(1024)S(1)} %get-tuple-element.64) | copy-start | bytes 27652
  34.4 22.5 %copy-start.52 = (f32[768]{0:T(1024)}, f32[768]{0:T(1024)S(1)}, u32[]{:S(2)}) copy-start(f32[768]{0:T(1024)S(1)} %get-tuple-element.67) | copy-start | bytes 9220
  51.6 5.3 collective-permute-start.1
  59.1 179.7 %all-gather.6.cloned.1.call-start = ((), (), s32[]{:S(2)}) async-start(), calls=%async_computation.3 | async-start | bytes 5898240 | tf_op jit(solution)/shard_map/all_gather | solution.py:114
  59.8 306.2 %reduce-scatter.3.cloned.1.call-start = ((), (), s32[]{:S(2)}) async-start(), calls=%async_computation.4 | async-start | bytes 5898240 | tf_op jit(solution)/shard_map/reduce_scatter | solution.py:134
  238.8 19.6 %slice-start.2 = ((s8[4718592]{0:T(1024)(128)(4,1)}), s8[4194304]{0:T(1024)(128)(4,1)S(1)}, s32[]{:S(2)}) async-start(s8[4718592]{0:T(1024)(128)(4,1)} %bitcast.76), calls=%async_computation.10 | async-start | bytes 8388608
  246.6 11.7 copy-start.7
  246.6 11.7 slice-start.3
  280.1 248.2 %all-gather.8.cloned.1.call-start = ((), (), s32[]{:S(2)}) async-start(), calls=%async_computation.5 | async-start | bytes 5898240 | tf_op jit(solution)/shard_map/all_gather | solution.py:175
  376.9 49.0 %copy-start.5 = (f32[768,768]{1,0:T(8,128)}, f32[768,768]{1,0:T(8,128)S(1)}, u32[]{:S(2)}) copy-start(f32[768,768]{1,0:T(8,128)S(1)} %get-tuple-element.103) | copy-start | bytes 7077892
  377.6 9.6 slice-start.8
  378.0 9.3 copy-start.22
  378.0 9.3 slice-start.9
  440.2 329.7 %reduce-scatter.5.cloned.1.call-start = ((), (), s32[]{:S(2)}) async-start(), calls=%async_computation.6 | async-start | bytes 11796480 | tf_op jit(solution)/shard_map/reduce_scatter | solution.py:208
  528.3 19.6 %slice-start.4 = ((s8[4718592]{0:T(1024)(128)(4,1)}), s8[4194304]{0:T(1024)(128)(4,1)S(1)}, s32[]{:S(2)}) async-start(s8[4718592]{0:T(1024)(128)(4,1)} %bitcast.78), calls=%async_computation.12 | async-start | bytes 8388608
  536.2 11.7 copy-start.8
  536.2 11.7 copy-start.24
  536.3 11.7 copy-start.26
  536.3 11.7 slice-start.5
  548.0 9.2 copy-start.28
  588.0 15.3 %copy-start.18 = (bf16[512,6,768]{2,0,1:T(8,128)(2,1)S(1)}, bf16[512,6,768]{2,0,1:T(8,128)(2,1)}, u32[]{:S(2)}) copy-start(bf16[512,6,768]{2,0,1:T(8,128)(2,1)} %add_convert_fusion) | copy-start | bytes 14155780
  607.7 792.2 %all-reduce.6.cloned.1.call-start = ((), (), s32[]{:S(2)}) async-start(), calls=%async_computation.7 | async-start | bytes 80216064 | tf_op jit(solution)/shard_map/psum | solution.py:246
  615.5 13.8 slice-start.6
  620.5 8.8 slice-start.7
  620.5 15.1 %slice-start.10 = ((s8[4718592]{0:T(1024)(128)(4,1)}), s8[4194304]{0:T(1024)(128)(4,1)S(1)}, s32[]{:S(2)}) async-start(s8[4718592]{0:T(1024)(128)(4,1)} %bitcast.84), calls=%async_computation.18 | async-start | bytes 8388608
  644.6 127.8 %copy-start.53 = (f32[768]{0:T(1024)S(1)}, f32[768]{0:T(1024)}, u32[]{:S(2)}) copy-start(f32[768]{0:T(1024)} %copy-done.52) | copy-start | bytes 9220
  644.6 127.8 %copy-start.55 = (f32[768]{0:T(1024)S(1)}, f32[768]{0:T(1024)}, u32[]{:S(2)}) copy-start(f32[768]{0:T(1024)} %get-tuple-element.68) | copy-start | bytes 9220
  772.6 7.9 collective-permute-start.2
  785.7 4.6 collective-permute-start.3
  (61 other events, 303.0 us)
Sparse Core Ops, SparseCore 0:
  59.2 89.4 all-gather.3
  150.9 87.8 all-gather.5
  280.2 85.7 reduce-scatter.2
  440.4 87.8 all-gather.7
  607.8 162.1 reduce-scatter.4
  809.7 590.1 all-reduce.5
where the time goes:
time: 1440 us; the launch traced here: 1420 us
  waiting for transfers between devices  916 us (64%)
  matrix products  246 us (17%)
  local copies, waits for them, and re-layouts  147 us (10%)
  other arithmetic  46.6 us (3%)
  blocking collectives  43.3 us (3%)
  between operations  16.2 us (1%)
    psum x1, waiting for transfers between devices, on_device(): lax.psum((grad_ln1, grad_w_in, grad_short_taps, grad_cond_taps, grad_w_co...  475 us
    reduce_scatter x1, waiting for transfers between devices, on_device(): lax.psum_scatter(jnp.concatenate([signal_term, cond_term], axis=2).astype...  125 us
    all_gather x1, waiting for transfers between devices, on_device(): lax.all_gather(cond_low, 'seq', axis=0, tiled=True).astype(jnp.float32)  88.4 us
    all_gather x1, waiting for transfers between devices, on_device(): lax.all_gather(grad_filtered_low, 'seq', axis=0, tiled=True)  84.2 us
    reduce_scatter x1, waiting for transfers between devices, on_device(): lax.psum_scatter((term / span_float).astype(jnp.bfloat16), 'seq', scatter...  79.4 us
    all_gather x1, waiting for transfers between devices, on_device(): lax.all_gather(signal_low, 'seq', axis=0, tiled=True).astype(jnp.float32)  59.2 us
    psum x1, blocking collectives, on_device(): lax.psum((grad_ln1, grad_w_in, grad_short_taps, grad_cond_taps, grad_w_co...  43.3 us
  transfers between devices with their start and end apart: 10, of which 7 were waited for; matrix products, arithmetic and copies ran while one was open for 12% of the time, Pallas kernels for 0%

commit v1 on v0

v1 whole, which is shorter than its diff:
```python
import functools
import math

import jax
import jax.numpy as jnp
from jax import lax
from jax.experimental import pallas as pl
from jax.experimental.pallas import tpu as pltpu
from jax.sharding import PartitionSpec as P

BF = jnp.bfloat16
F32 = jnp.float32
MESH = pl.DeviceIdType.MESH
EPS = 1e-05
CB = 256
FC = 384
RB = 256
VMEM_LIMIT = 60 * 2**20


def mm(a, b):
    return jnp.dot(a, b, preferred_element_type=F32)


def mm_nt(a, b):
    return lax.dot_general(a, b, (((1,), (1,)), ((), ())), preferred_element_type=F32)


def mm_tn(a, b):
    return lax.dot_general(a, b, (((0,), (0,)), ((), ())), preferred_element_type=F32)


def unit_rows(x):
    mean = jnp.mean(x, axis=-1, keepdims=True)
    centered = x - mean
    r = lax.rsqrt(jnp.mean(centered * centered, axis=-1, keepdims=True) + EPS)
    return centered * r, r


def unit_back(g, u, r, gain):
    e = g * gain
    return r * (
        e - jnp.mean(e, axis=-1, keepdims=True) - u * jnp.mean(e * u, axis=-1, keepdims=True)
    )


def lanes(ref, width):
    m = ref[...]
    return jnp.concatenate([m] * (width // m.shape[1]), axis=1)


def down(a, j):
    return pltpu.roll(a, j, axis=0)


def up(a, j):
    return pltpu.roll(a, a.shape[0] - j, axis=0)


def conv(a, taps, m1, m2):
    return taps[0:1] * a + taps[1:2] * (down(a, 1) * m1) + taps[2:3] * (down(a, 2) * m2)


def conv_back(g, taps, m1, m2):
    return taps[0:1] * g + taps[1:2] * up(g * m1, 1) + taps[2:3] * up(g * m2, 2)


def tap_sums(g, a, m1, m2):
    return jnp.concatenate(
        [
            jnp.sum(g * a, axis=0, keepdims=True),
            jnp.sum(g * (down(a, 1) * m1), axis=0, keepdims=True),
            jnp.sum(g * (down(a, 2) * m2), axis=0, keepdims=True),
        ],
        axis=0,
    )


def cols_at(c, width, base=0):
    return pl.ds(pl.multiple_of(base + c * width, 128), width)


def wave_tables(is_long, short, span_long, freqs):
    i = jnp.arange(freqs, dtype=jnp.int32)[:, None]
    t = jnp.arange(span_long, dtype=jnp.int32)[None, :]
    blocks, half = span_long // short, short // 2 + 1
    f_short, b_short = i % half, i // half
    phase = jnp.where(
        is_long, (i * t) % span_long, ((f_short * (t % short)) % short) * blocks
    )
    kept = jnp.where(is_long, i <= span_long // 2, (b_short < blocks) & (t // short == b_short))
    angle = phase.astype(F32) * (2.0 * math.pi / span_long)
    kept_f = kept.astype(F32)
    table = jnp.concatenate([jnp.cos(angle) * kept_f, jnp.sin(angle) * kept_f], axis=0)
    once = jnp.where(
        is_long, (i == 0) | (i == span_long // 2), (f_short == 0) | (f_short == short // 2)
    )
    used = jnp.where(is_long, i <= span_long // 2, b_short < blocks)
    mult = jnp.where(used, jnp.where(once, 1.0, 2.0), 0.0).astype(F32)
    table = table.astype(BF)
    return table, table.T, jnp.broadcast_to(mult, (freqs, 128))


def reshard_in_kernel(tok_ref, cot_ref, xs_ref, cs_ref, local_sem, send_sem, recv_sem):
    dp, me = lax.axis_index("dp"), lax.axis_index("seq")
    n = lax.axis_size("seq")
    rows = tok_ref.shape[1]
    barrier = pltpu.get_barrier_semaphore()
    for k in range(1, n):
        pl.semaphore_signal(
            barrier, inc=1, device_id=(dp, lax.rem(me + k, n)), device_id_type=MESH
        )
    pl.semaphore_wait(barrier, n - 1)
    at = pl.ds(pl.multiple_of(me * rows, rows), rows)
    half_at = pl.ds(pl.multiple_of(n * rows + lax.rem(me, 2) * rows, rows), rows)

    def copies(k, peer):
        moves = [
            (tok_ref.at[peer], xs_ref.at[0, at]),
            (tok_ref.at[n + peer // 2], xs_ref.at[1, at]),
            (cot_ref.at[peer], cs_ref.at[at]),
            (cot_ref.at[n + peer // 2], cs_ref.at[half_at]),
        ]
        if k == 0:
            return [
                pltpu.make_async_copy(s, d, local_sem.at[j]) for j, (s, d) in enumerate(moves)
            ]
        return [
            pltpu.make_async_remote_copy(
                src_ref=s,
                dst_ref=d,
                send_sem=send_sem.at[j, k],
                recv_sem=recv_sem.at[j, k],
                device_id=(dp, peer),
                device_id_type=MESH,
            )
            for j, (s, d) in enumerate(moves)
        ]

    peers = [lax.rem(me + k, n) for k in range(n)]
    sources = [lax.rem(me + n - k, n) for k in range(n)]
    sends_half = [lax.rem(p, 2) == me // 2 for p in peers]
    gets_half = [lax.rem(me, 2) == s // 2 for s in sources]
    all_copies = [copies(k, peers[k]) for k in range(n)]
    for j in range(3):
        for k in range(n):
            all_copies[k][j].start()
    for k in range(n):
        pl.when(sends_half[k])(all_copies[k][3].start)
    for j in range(3):
        for k in range(n):
            all_copies[k][j].wait()
    pl.when(sends_half[0])(all_copies[0][3].wait)
    for k in range(1, n):
        pl.when(sends_half[k])(all_copies[k][3].wait_send)
        pl.when(gets_half[k])(all_copies[k][3].wait_recv)


def reshard_in(tok, cot):
    slots, rows, d = tok.shape
    n = lax.axis_size("seq")
    any_spec = pl.BlockSpec(memory_space=pl.ANY)
    return pl.pallas_call(
        reshard_in_kernel,
        name="reshard_in",
        out_shape=(
            jax.ShapeDtypeStruct((2, n * rows, d), BF),
            jax.ShapeDtypeStruct((n * rows + n * rows // 2, d), BF),
        ),
        in_specs=[any_spec] * 2,
        out_specs=(any_spec, any_spec),
        scratch_shapes=[
            pltpu.SemaphoreType.DMA((4,)),
            pltpu.SemaphoreType.DMA((4, n)),
            pltpu.SemaphoreType.DMA((4, n)),
        ],
        compiler_params=pltpu.CompilerParams(collective_id=0, has_side_effects=True),
    )(tok, cot)


def fwd_kernel(
    isp_ref, x_ref, g1_ref, win_ref, st_ref, ct_ref, wc_ref, cb_ref, w_ref, wt_ref,
    m1_ref, m2_ref, mult_ref,
    proj_ref, mixed_ref, filt_ref, xs_ref, xc_ref, th_ref, feat_ref,
    n1_s, q_s,
):
    t, d = n1_s.shape
    f = th_ref.shape[1]
    isp = isp_ref[0]

    @pl.loop(0, t // 128)
    def _(r):
        rows = pl.ds(pl.multiple_of(r * 128, 128), 128)
        u, _ = unit_rows(x_ref[0, rows, :].astype(F32))
        n1_s[rows, :] = (u * g1_ref[...]).astype(BF)

    @pl.loop(0, d // CB)
    def _(c):
        m1, m2 = lanes(m1_ref, CB), lanes(m2_ref, CB)
        own = cols_at(c, CB)

        def part(k):
            cols = cols_at(c, CB, k * d)
            p = mm(n1_s[...], win_ref[:, cols]).astype(BF)
            proj_ref[0, :, cols] = p
            return conv(p.astype(F32), st_ref[:, cols], m1, m2)

        q_s[:, own] = part(0)
        key = part(1)
        value = part(2).astype(BF)
        value_f = value.astype(F32)
        signal = (key * value_f).astype(BF)
        xs_ref[0, :, own] = mm(w_ref[...], signal).astype(BF)
        cond = conv(value_f, ct_ref[:, own], m1, m2).astype(BF)
        xc = mm(w_ref[...], cond)
        xc_ref[0, :, own] = xc.astype(BF)
        power = (xc[:f] * xc[:f] + xc[f:] * xc[f:]) * isp
        feat_ref[0, :, own] = jnp.log1p(power).astype(BF)

    @pl.loop(0, d // CB)
    def _(c):
        own = cols_at(c, CB)
        th = jnp.tanh(mm(feat_ref[0], wc_ref[:, own]) + cb_ref[:, own])
        th_ref[0, :, own] = th
        g = (1.0 + th) * (lanes(mult_ref, CB) * isp)
        xs = xs_ref[0, :, own].astype(F32)
        y = jnp.concatenate([(g * xs[:f]).astype(BF), (g * xs[f:]).astype(BF)], axis=0)
        filt = mm(wt_ref[...], y)
        filt_ref[0, :, own] = filt.astype(BF)
        mixed_ref[0, :, own] = (q_s[:, own] * filt).astype(BF)


def whole(shape):
    return pl.BlockSpec(shape, lambda *_: (0,) * len(shape), pipeline_mode=pl.Buffered(1))


def per_slot(shape):
    return pl.BlockSpec((1,) + shape, lambda s, *_: (s,) + (0,) * len(shape))


def mix_forward(isp, xs, g1, w_in, st, ct, w_cond, cb, table, table_t, m1, m2, mult):
    _, t, d = xs.shape
    f2 = table.shape[0]
    f = f2 // 2
    return pl.pallas_call(
        fwd_kernel,
        name="mix_forward",
        grid=(2,),
        out_shape=(
            jax.ShapeDtypeStruct((2, t, 3 * d), BF),
            jax.ShapeDtypeStruct((2, t, d), BF),
            jax.ShapeDtypeStruct((2, t, d), BF),
            jax.ShapeDtypeStruct((2, f2, d), BF),
            jax.ShapeDtypeStruct((2, f2, d), BF),
            jax.ShapeDtypeStruct((2, f, d), F32),
            jax.ShapeDtypeStruct((2, f, d), BF),
        ),
        in_specs=[
            pl.BlockSpec(memory_space=pltpu.SMEM),
            per_slot((t, d)),
            whole((1, d)),
            whole((d, 3 * d)),
            whole((3, 3 * d)),
            whole((3, d)),
            whole((d, d)),
            whole((1, d)),
            whole((f2, t)),
            whole((t, f2)),
            whole((t, 128)),
            whole((t, 128)),
            whole((f, 128)),
        ],
        out_specs=(
            per_slot((t, 3 * d)),
            per_slot((t, d)),
            per_slot((t, d)),
            per_slot((f2, d)),
            per_slot((f2, d)),
            per_slot((f, d)),
            per_slot((f, d)),
        ),
        scratch_shapes=[pltpu.VMEM((t, d), BF), pltpu.VMEM((t, d), F32)],
        compiler_params=pltpu.CompilerParams(vmem_limit_bytes=VMEM_LIMIT),
    )(isp, xs, g1, w_in, st, ct, w_cond, cb, table, table_t, m1, m2, mult)


def add_into(dst, src):
    dst[...] = (dst[...].astype(F32) + src[...].astype(F32)).astype(dst.dtype)


def back_kernel(side, *refs):
    (
        isp_ref, mixed_h, xs_h, cot_h, wo_h, g2_ref, wg_h, wu_h, wd_h,
        proj_h, filt_h, ss_h, cs_h, th_h, feat_h,
        st_ref, ct_ref, wc_h, tab_h, tabt_h, m1_ref, m2_ref, mult_ref, g1_ref, win_h,
        lay6_h, gtok6_h, odg_h, odu_h, odd_h, ow_h, small_out,
        a_s, b_s, u_s, r_s, n2_s, n2t_s, cot_s, mix_s, gmix_s, gm_s,
        act_s, gg_s, gu_s, wcol_s, wd_s, wo_s, wc_s, tab_s, tabt_s,
        sbg_s, sbu_s, sbd_s, cg_s, cu_s, cd_s, g1g_s, g1u_s, g1d_s, g2g_s, g2u_s, g2d_s,
        g3g_s, g3u_s, g3d_s,
        proj_s, filt_s, ss_s, cs_s, th_s, feat_s, gpre_s, gprem_s,
        c2_s, own2_s, g12_s, g22_s, g32_s, small_s, sgot_s, ssum_s,
        load_sem, w_sem, send_sem, recv_sem, local_sem,
    ) = refs
    n, d = n2_s.shape
    t = gm_s.shape[1]
    f = th_s.shape[0]
    isp = isp_ref[0]
    fc = gg_s.shape[1]
    quarter = d // 4
    step48 = d // 16

    dp, me = lax.axis_index("dp"), lax.axis_index("seq")
    core = lax.rem(dp, 2)
    x = lax.rem(lax.rem(dp // 2, side), 2)
    y = lax.rem(dp // (2 * side), 2)
    at_core = (dp + 1 - 2 * core, me)
    at_x = (dp + 2 - 4 * x, me)
    at_y = (dp + 2 * side - 4 * side * y, me)
    at_xy = (dp + 2 - 4 * x + 2 * side - 4 * side * y, me)
    at_z = [(dp, lax.rem(me + k, 4)) for k in range(1, 4)]
    half = lax.rem(me, 2)
    at_pair = (dp, me + 1 - 2 * half)
    own = core * 4 + x * 2 + y

    row_moves = lambda src, dst: [
        (src.at[0], dst.at[pl.ds(0, t)]),
        (src.at[1, pl.ds(pl.multiple_of(half * RB, RB), RB)], dst.at[pl.ds(t, RB)]),
    ]
    moves = (
        row_moves(mixed_h, mix_s)
        + row_moves(xs_h, gmix_s)
        + [(wo_h, wo_s), (cot_h, cot_s)]
        + [(tab_h, tab_s), (tabt_h, tabt_s), (wc_h, wc_s), (proj_h, proj_s)]
    )
    loads = [
        pltpu.make_async_copy(s, e, load_sem.at[j]) for j, (s, e) in enumerate(moves)
    ]
    slot_moves = [(filt_h, filt_s), (ss_h, ss_s), (th_h, th_s), (cs_h, cs_s), (feat_h, feat_s)]
    slot_load = lambda slot, j: pltpu.make_async_copy(
        slot_moves[j][0].at[slot], slot_moves[j][1], load_sem.at[len(moves) + j]
    )

    def chunk_of(s):
        if isinstance(s, int):
            return 2 * s + 1 - core if s < 4 else 2 * (s - 4) + core
        return jnp.where(s < 4, 2 * s + 1 - core, 2 * (s - 4) + core)

    def weights(s):
        cols = pl.ds(pl.multiple_of(chunk_of(s) * fc, 128), fc)
        b = s % 2 if isinstance(s, int) else lax.rem(s, 2)
        return [
            pltpu.make_async_copy(wg_h.at[:, cols], wcol_s.at[b], w_sem.at[0, b]),
            pltpu.make_async_copy(wu_h.at[:, cols], wcol_s.at[2 + b], w_sem.at[1, b]),
            pltpu.make_async_copy(wd_h.at[cols, :], wd_s.at[b], w_sem.at[2, b]),
        ]

    def win_col(j):
        return 3 * (1 - core) + j if j < 3 else 3 * core + j - 3

    def win_load(j):
        cols = pl.ds(pl.multiple_of(win_col(j) * fc, 128), fc)
        return pltpu.make_async_copy(win_h.at[:, cols], wcol_s.at[j % 4], w_sem.at[3, j % 4])

    for c in loads[:6]:
        c.start()
    for c in weights(0):
        c.start()
    for c in loads[6:]:
        c.start()
    for j in range(5):
        slot_load(0, j).start()

    barrier = pltpu.get_barrier_semaphore()
    everyone = [at_core, at_x, at_y, at_xy] + at_z
    for peer in everyone:
        pl.semaphore_signal(barrier, inc=1, device_id=peer, device_id_type=MESH)
    pl.semaphore_wait(barrier, len(everyone))

    def remote(src, dst, peer, j):
        return pltpu.make_async_remote_copy(
            src_ref=src,
            dst_ref=dst,
            send_sem=send_sem.at[j],
            recv_sem=recv_sem.at[j],
            device_id=peer,
            device_id_type=MESH,
        )

    def each(copies, what):
        for c in copies:
            getattr(c, what)()

    C, X1, X2, Z, G, GC = 0, 12, 36, 48, 57, 66
    C2, X12, X22, Z2, G2, GC2 = 69, 74, 86, 90, 93, 96
    LAY, GTOK, PAIR, SMALL = 97, 103, 109, 110

    def core_copies(s):
        pairs = ((sbg_s, cg_s), (sbu_s, cu_s), (sbd_s, cd_s))
        return [remote(a, b.at[s], at_core, C + 4 * j + s) for j, (a, b) in enumerate(pairs)]

    each(loads[:6], "wait")
    for i in range(n // RB):
        rows = slice(i * RB, (i + 1) * RB)
        hid = gmix_s[rows, :].astype(F32) + mm(mix_s[rows, :], wo_s[...])
        a_s[rows, :] = hid
        u, r = unit_rows(hid)
        u_s[rows, :] = u
        r_s[rows, :] = jnp.broadcast_to(r, (RB, 128))
        n2 = u * g2_ref[...]
        n2_s[rows, :] = n2.astype(BF)
        n2t_s[:, rows] = n2.T.astype(BF)
    b_s[...] = jnp.zeros_like(b_s)

    triples = ((cg_s, g1g_s, g2g_s, g3g_s), (cu_s, g1u_s, g2u_s, g3u_s), (cd_s, g1d_s, g2d_s, g3d_s))

    def x1_sem(j, q, i):
        return X1 + 8 * j + 2 * q + i

    def first_stage(i):
        a, b = i // 2, lax.rem(i, 2)
        for j in range(2):
            held, got = triples[j][:2]
            for q in range(4):
                if q % 2 == 0:
                    copy = remote(held.at[i, q], got.at[q, b], at_x, x1_sem(j, q, b))
                    pl.when(a != x)(copy.start)
                else:
                    copy = remote(held.at[i, q], got.at[q, a], at_y, x1_sem(j, q, a))
                    pl.when(b != y)(copy.start)

        @pl.when(b == 0)
        def _():
            for e in range(2):
                remote(cd_s.at[i, 2 - 2 * x + e], g1d_s.at[i, e], at_x, x1_sem(2, i, e)).start()

        @pl.when(b == 1)
        def _():
            for e in range(2):
                remote(cd_s.at[i, 2 * e + 1 - y], g1d_s.at[i, e], at_y, x1_sem(2, i, e)).start()

    @pl.loop(0, 8)
    def _(s):
        b = lax.rem(s, 2)
        each(weights(s), "wait")

        @pl.when(s < 7)
        def _():
            each(weights(s + 1), "start")

        @pl.loop(0, n // RB)
        def _(i):
            rows = pl.ds(pl.multiple_of(i * RB, RB), RB)
            n2 = n2_s[rows, :]
            pre = mm(n2, wcol_s[b])
            lin = mm(n2, wcol_s[2 + b])
            g_act = mm_nt(cot_s[rows, :], wd_s[b])
            sg = 1.0 / (1.0 + jnp.exp(-pre))
            silu = pre * sg
            act = (silu * lin).astype(BF)
            act_s[rows, :] = act
            g_up = (g_act * silu).astype(BF)
            gu_s[rows, :] = g_up
            g_gate = (g_act * lin * sg * (1.0 + pre * (1.0 - sg))).astype(BF)
            gg_s[rows, :] = g_gate
            a_s[rows, :] += mm(act, wd_s[b])
            b_s[rows, :] += mm_nt(g_gate, wcol_s[b]) + mm_nt(g_up, wcol_s[2 + b])

        @pl.when((s > 0) & (s < 5))
        def _():
            each(core_copies(s - 1), "wait_send")

        @pl.when(s >= 4)
        def _():
            each(core_copies(s - 4), "wait_recv")

        @pl.loop(0, 4)
        def _(q):
            lhs = n2t_s[pl.ds(pl.multiple_of(q * quarter, quarter), quarter), :]
            dg = mm(lhs, gg_s[...])
            du = mm(lhs, gu_s[...])

            @pl.when(s < 4)
            def _():
                sbg_s[q] = dg.astype(BF)
                sbu_s[q] = du.astype(BF)

            @pl.when(s >= 4)
            def _():
                cg_s[s - 4, q] = (cg_s[s - 4, q].astype(F32) + dg).astype(BF)
                cu_s[s - 4, q] = (cu_s[s - 4, q].astype(F32) + du).astype(BF)

        dd = mm_tn(act_s[...], cot_s[...])
        step = fc // 4

        @pl.when(s < 4)
        def _():
            for p in range(4):
                sbd_s[p] = dd[p * step : (p + 1) * step].astype(BF)
            each(core_copies(s), "start")

        @pl.when(s >= 4)
        def _():
            for p in range(4):
                cd_s[s - 4, p] = (
                    cd_s[s - 4, p].astype(F32) + dd[p * step : (p + 1) * step]
                ).astype(BF)
            first_stage(s - 4)

    for j in range(4):
        win_load(j).start()
    small_s[...] = jnp.zeros_like(small_s)
    for i in range(n // RB):
        rows = slice(i * RB, (i + 1) * RB)
        n2_s[rows, :] = a_s[rows, :].astype(BF)
        g, u = b_s[rows, :], u_s[rows, :]
        small_s[14:15, :] += jnp.sum(g * u, axis=0, keepdims=True)
        gh = cot_s[rows, :].astype(F32) + unit_back(g, u, r_s[rows, 0:1], g2_ref[...])
        gmix_s[rows, :] = gh.astype(BF)

    x_loads = [
        pltpu.make_async_copy(a, b, load_sem.at[15 + j])
        for j, (a, b) in enumerate(row_moves(xs_h, cot_s))
    ]
    each(x_loads, "start")
    half_at = pl.ds(pl.multiple_of(half * RB, RB), RB)
    gm_s[1, half_at, :] = mm_nt(gmix_s[t:, :], wo_s[...]).astype(BF)
    pair_copy = remote(gm_s.at[1, half_at], gm_s.at[1, half_at], at_pair, PAIR)
    pair_copy.start()

    rows128 = lay6_h.shape[1]
    peers = [lax.rem(me + k, 4) for k in range(4)]
    sources = [lax.rem(me + 4 - k, 4) for k in range(4)]
    sends_half = [half == p // 2 for p in peers]
    gets_half = [lax.rem(s, 2) == me // 2 for s in sources]

    def home(buf, out, base, k):
        at = pl.ds(pl.multiple_of(peers[k] * rows128, rows128), rows128)
        at2 = pl.ds(pl.multiple_of(t + lax.rem(peers[k], 2) * rows128, rows128), rows128)
        slots = (me, 4 + me // 2)
        if k == 0:
            j = 0 if base == LAY else 2
            return [
                pltpu.make_async_copy(buf.at[at], out.at[slots[0]], local_sem.at[j]),
                pltpu.make_async_copy(buf.at[at2], out.at[slots[1]], local_sem.at[j + 1]),
            ]
        return [
            remote(buf.at[at], out.at[slots[0]], at_z[k - 1], base + 2 * (k - 1)),
            remote(buf.at[at2], out.at[slots[1]], at_z[k - 1], base + 2 * (k - 1) + 1),
        ]

    def home_start(buf, out, base):
        for k in range(4):
            full, part = home(buf, out, base, k)
            full.start()
            pl.when(sends_half[k])(part.start)

    def home_wait(buf, out, base):
        for k in range(4):
            full, part = home(buf, out, base, k)
            full.wait()
            if k == 0:
                pl.when(sends_half[0])(part.wait)
            else:
                pl.when(sends_half[k])(part.wait_send)
                pl.when(gets_half[k])(part.wait_recv)

    home_start(n2_s, lay6_h, LAY)

    for i in range(t // RB):
        rows = slice(i * RB, (i + 1) * RB)
        gm_s[0, rows, :] = mm_nt(gmix_s[rows, :], wo_s[...]).astype(BF)

    def out_half(which):
        cols = pl.ds(pl.multiple_of(which * fc, 128), fc)
        return mm_tn(mix_s[...], gmix_s[:, cols])

    def put_quarters(dst, value):
        for q in range(4):
            dst[q] = value[q * quarter : (q + 1) * quarter].astype(BF)

    def second_core(c, buf):
        return remote(buf, c2_s.at[c], at_core, C2 + c)

    put_quarters(sbg_s, out_half(1 - core))
    second_core(0, sbg_s).start()
    put_quarters(own2_s.at[0], out_half(core))

    def stage_x1_end():
        for j, (held, got, got2, _) in enumerate(triples):
            for q in range(4):
                for i in range(2):
                    remote(got.at[q, i], got.at[q, i], at_x, x1_sem(j, q, i)).wait()

        @pl.loop(0, 4)
        def _(i):
            q, e = 2 * (i // 2), lax.rem(i, 2)
            for held, got, _, _ in triples[:2]:
                add_into(got.at[q, e], held.at[2 * x + e, q])
                add_into(got.at[q + 1, e], held.at[2 * e + y, q + 1])
            add_into(g1d_s.at[q, e], cd_s.at[q, 2 * x + e])
            add_into(g1d_s.at[q + 1, e], cd_s.at[q + 1, 2 * e + y])

    def x2_copies():
        out = []
        for j, (_, got, got2, _) in enumerate(triples):
            for q in range(4):
                if q % 2 == 0:
                    out.append(remote(got.at[q, 1 - y], got2.at[q], at_y, X2 + 4 * j + q))
                else:
                    out.append(remote(got.at[q, 1 - x], got2.at[q], at_x, X2 + 4 * j + q))
        return out

    def stage_x2_end():
        each(x2_copies(), "wait")

        @pl.loop(0, 2)
        def _(i):
            for _, got, got2, _ in triples:
                add_into(got2.at[2 * i], got.at[2 * i, y])
                add_into(got2.at[2 * i + 1], got.at[2 * i + 1, x])

    def z_copies():
        return [
            remote(got2.at[peers[k]], got3.at[k - 1], at_z[k - 1], Z + 3 * j + k - 1)
            for j, (_, _, got2, got3) in enumerate(triples)
            for k in range(1, 4)
        ]

    def stage_z_end():
        each(z_copies(), "wait")
        for _, _, got2, got3 in triples:
            total = got2[me].astype(F32)
            for k in range(3):
                total += got3[k].astype(F32)
            got2[me] = total.astype(BF)

    outs = (odg_h, odu_h, odd_h)

    def gather_copies():
        return [
            remote(got2.at[me], out.at[own], peer, G + 3 * j + k)
            for j, ((_, _, got2, _), out) in enumerate(zip(triples, outs))
            for k, peer in enumerate((at_x, at_y, at_xy))
        ]

    def gather_local():
        return [
            pltpu.make_async_copy(tr[2].at[me], out.at[own], local_sem.at[4 + j])
            for j, (tr, out) in enumerate(zip(triples, outs))
        ]

    here = pl.ds(4 * core, 4)

    def gather_core():
        return [remote(out.at[here], out.at[here], at_core, GC + j) for j, out in enumerate(outs)]

    each(loads[6:], "wait")

    @pl.loop(0, 2)
    def _(slot):
        share = jnp.where(slot == 0, 1.0, 0.5)
        for j in range(3):
            slot_load(slot, j).wait()
        pl.when(slot == 1)(pair_copy.wait)

        @pl.loop(0, d // CB)
        def _(c):
            m1, m2 = lanes(m1_ref, CB), lanes(m2_ref, CB)
            mult = lanes(mult_ref, CB)
            cols = cols_at(c, CB)
            query = conv(proj_s[slot, :, cols].astype(F32), st_ref[:, cols], m1, m2)
            gm = gm_s[slot, :, cols].astype(F32)
            a_s[0:t, cols] = gm * filt_s[:, cols].astype(F32)
            spec = mm(tab_s[...], (gm * query).astype(BF)) * isp
            ss = ss_s[:, cols].astype(F32)
            th = th_s[:, cols]
            g_gain = spec[:f] * ss[:f] + spec[f:] * ss[f:]
            g_pre = (g_gain * (1.0 - th * th)).astype(BF)
            gpre_s[:, cols] = g_pre
            weighted = g_pre.astype(F32) * mult
            gprem_s[:, cols] = weighted.astype(BF)
            small_s[13:14, cols] += share * jnp.sum(weighted, axis=0, keepdims=True)
            g = (1.0 + th) * mult
            yy = jnp.concatenate(
                [(g * spec[:f]).astype(BF), (g * spec[f:]).astype(BF)], axis=0
            )
            b_s[0:t, cols] = mm(tabt_s[...], yy)

        @pl.when(slot == 0)
        def _():
            for j in range(3):
                slot_load(1, j).start()
            stage_x1_end()
            each(x2_copies(), "start")

        for j in range(3, 5):
            slot_load(slot, j).wait()

        @pl.loop(0, d // CB)
        def _(c):
            m1, m2 = lanes(m1_ref, CB), lanes(m2_ref, CB)
            cols = cols_at(c, CB)
            g_feat = mm_nt(gpre_s[...], wc_s[cols, :])
            xc = cs_s[:, cols].astype(F32)
            power = (xc[:f] * xc[:f] + xc[f:] * xc[f:]) * isp
            g_pow = g_feat / (1.0 + power) * (lanes(mult_ref, CB) * (2.0 * isp))
            yy = jnp.concatenate(
                [(g_pow * xc[:f]).astype(BF), (g_pow * xc[f:]).astype(BF)], axis=0
            )
            g_cond = mm(tabt_s[...], yy)
            dwc = share * mm_tn(feat_s[:, cols], gprem_s[...])

            @pl.when(slot == 0)
            def _():
                u_s[cols, :] = dwc

            @pl.when(slot == 1)
            def _():
                u_s[cols, :] += dwc

            def finish(part, g_conv, p):
                at = cols_at(c, CB, part * d)
                sums = share * tap_sums(g_conv, p, m1, m2)
                for j in range(3):
                    row = 1 + 3 * j + part
                    small_s[row : row + 1, cols] += sums[j : j + 1]
                proj_s[slot, :, at] = conv_back(g_conv, st_ref[:, at], m1, m2).astype(BF)

            finish(0, a_s[0:t, cols], proj_s[slot, :, cols].astype(F32))
            key_cols, value_cols = cols_at(c, CB, d), cols_at(c, CB, 2 * d)
            p_value = proj_s[slot, :, value_cols].astype(F32)
            value = conv(p_value, st_ref[:, value_cols], m1, m2).astype(BF).astype(F32)
            g_sig = b_s[0:t, cols]
            p_key = proj_s[slot, :, key_cols].astype(F32)
            key = conv(p_key, st_ref[:, key_cols], m1, m2)
            finish(1, g_sig * value, p_key)
            sums = share * tap_sums(g_cond, value, m1, m2)
            for j in range(3):
                small_s[10 + j : 11 + j, cols] += sums[j : j + 1]
            finish(2, g_sig * key + conv_back(g_cond, ct_ref[:, cols], m1, m2), p_value)

        @pl.when(slot == 0)
        def _():
            for j in range(3, 5):
                slot_load(1, j).start()
            stage_x2_end()
            each(z_copies(), "start")

    def cond_half(dst, which):
        cols = pl.ds(pl.multiple_of(which * fc, 128), fc)
        for q in range(4):
            dst[q] = u_s[q * quarter : (q + 1) * quarter, cols].astype(BF)

    cond_half(sbu_s, 1 - core)
    second_core(1, sbu_s).start()
    cond_half(own2_s.at[1], core)

    each(x_loads, "wait")
    for i in range(n // RB):
        rows = slice(i * RB, (i + 1) * RB)
        u, r = unit_rows(cot_s[rows, :].astype(F32))
        a_s[rows, :] = u
        r_s[rows, :] = jnp.broadcast_to(r, (RB, 128))
        n2t_s[:, rows] = (u * g1_ref[...]).T.astype(BF)
    b_s[...] = jnp.zeros_like(b_s)

    def proj_step(j, put):
        cols = pl.ds(pl.multiple_of(win_col(j) * fc, 128), fc)
        win_load(j).wait()
        w = wcol_s.at[j % 4]
        blocks = [
            proj_s.at[0, pl.ds(0, RB), cols],
            proj_s.at[0, pl.ds(RB, RB), cols],
            proj_s.at[1, half_at, cols],
        ]
        for i, gp in enumerate(blocks):
            b_s[i * RB : (i + 1) * RB, :] += mm_nt(gp[...], w[...])

        @pl.loop(0, 4)
        def _(q):
            rows = pl.ds(pl.multiple_of(q * quarter, quarter), quarter)
            dw = jnp.zeros((quarter, fc), F32)
            for i, gp in enumerate(blocks):
                dw += mm(n2t_s[rows, i * RB : (i + 1) * RB], gp[...])
            put(q, dw)

        if j < 2:
            win_load(j + 4).start()

    second_core(0, sbg_s).wait_send()
    second_core(1, sbu_s).wait_send()

    def put_g(q, dw):
        sbg_s[q] = dw.astype(BF)

    def put_u(q, dw):
        sbu_s[q] = dw.astype(BF)

    def put_own(q, dw):
        own2_s[2, q] = dw.astype(BF)

    proj_step(0, put_g)
    second_core(2, sbg_s).start()
    proj_step(1, put_u)
    second_core(3, sbu_s).start()
    proj_step(2, put_own)
    second_core(4, own2_s.at[2]).start()

    stage_z_end()
    each(gather_copies(), "start")
    each(gather_local(), "start")

    def x12_copies(first, count, base):
        cs = pl.ds(first, count)
        out = []
        for q in range(4):
            if q % 2 == 0:
                rows = pl.ds(pl.multiple_of((2 - 2 * x) * step48, step48), 2 * step48)
                out.append(
                    remote(c2_s.at[cs, q, rows], g12_s.at[cs, q], at_x, base + q)
                )
            else:
                for e in range(2):
                    rows = pl.ds(pl.multiple_of((2 * e + 1 - y) * step48, step48), step48)
                    to = pl.ds(e * step48, step48)
                    out.append(
                        remote(c2_s.at[cs, q, rows], g12_s.at[cs, q, to], at_y, base + (q if e == 0 else 4 + q // 2))
                    )
        return out

    for c in range(2):
        remote(c2_s.at[c], c2_s.at[c], at_core, C2 + c).wait_recv()

        @pl.loop(0, 4)
        def _(q, c=c):
            add_into(c2_s.at[c, q], own2_s.at[c, q])

    each(x12_copies(0, 2, X12), "start")

    def own_put(c):
        def put(q, dw):
            c2_s[c, q] = (c2_s[c, q].astype(F32) + dw).astype(BF)

        return put

    for c in range(3):
        remote(c2_s.at[2 + c], c2_s.at[2 + c], at_core, C2 + 2 + c).wait_recv()
        proj_step(3 + c, own_put(2 + c))
    each(x12_copies(2, 3, X12 + 6), "start")

    each(gather_copies(), "wait")
    each(gather_local(), "wait")
    each(gather_core(), "start")

    for i in range(n // RB):
        rows = slice(i * RB, (i + 1) * RB)
        g, u = b_s[rows, :], a_s[rows, :]
        small_s[0:1, :] += jnp.sum(g * u, axis=0, keepdims=True)
        mix_s[rows, :] = (
            gmix_s[rows, :].astype(F32) + unit_back(g, u, r_s[rows, 0:1], g1_ref[...])
        ).astype(BF)
    home_start(mix_s, gtok6_h, GTOK)

    small_c = remote(small_s, sgot_s.at[0], at_core, SMALL)
    small_c.start()
    each([second_core(2, sbg_s), second_core(3, sbu_s), second_core(4, own2_s.at[2])], "wait_send")

    each(x12_copies(0, 2, X12), "wait")
    each(x12_copies(2, 3, X12 + 6), "wait")

    @pl.loop(0, 5)
    def _(c):
        for q in range(4):
            if q % 2 == 0:
                rows = pl.ds(pl.multiple_of(2 * x * step48, step48), 2 * step48)
                add_into(g12_s.at[c, q], c2_s.at[c, q, rows])
            else:
                for e in range(2):
                    rows = pl.ds(pl.multiple_of((2 * e + y) * step48, step48), step48)
                    add_into(g12_s.at[c, q, pl.ds(e * step48, step48)], c2_s.at[c, q, rows])

    def x22_copies():
        out = []
        for q in range(4):
            e, peer = (1 - y, at_y) if q % 2 == 0 else (1 - x, at_x)
            rows = pl.ds(pl.multiple_of(e * step48, step48), step48)
            out.append(remote(g12_s.at[:, q, rows], g22_s.at[q], peer, X22 + q))
        return out

    each(x22_copies(), "start")
    small_c.wait()
    ssum_s[0] = small_s[...] + sgot_s[0]
    small_x = remote(ssum_s.at[0], sgot_s.at[1], at_x, SMALL + 1)
    small_x.start()
    each(x22_copies(), "wait")

    @pl.loop(0, 5)
    def _(c):
        for q in range(4):
            e = y if q % 2 == 0 else x
            rows = pl.ds(pl.multiple_of(e * step48, step48), step48)
            add_into(g22_s.at[q, c], g12_s.at[c, q, rows])

    z2_copies = [
        remote(g22_s.at[peers[k]], g32_s.at[k - 1], at_z[k - 1], Z2 + k - 1) for k in range(1, 4)
    ]
    each(z2_copies, "start")
    small_x.wait()
    ssum_s[1] = ssum_s[0] + sgot_s[1]
    small_y = remote(ssum_s.at[1], sgot_s.at[2], at_y, SMALL + 2)
    small_y.start()
    small_y.wait()
    ssum_s[2] = ssum_s[1] + sgot_s[2]
    small_z = [
        remote(ssum_s.at[2], sgot_s.at[2 + k], at_z[k - 1], SMALL + 2 + k) for k in range(1, 4)
    ]
    each(small_z, "start")
    each(gather_core(), "wait")
    each(z2_copies, "wait")

    @pl.loop(0, 5)
    def _(c):
        total = g22_s[me, c].astype(F32)
        for k in range(3):
            total += g32_s[k, c].astype(F32)
        g22_s[me, c] = total.astype(BF)

    g2_copies = [
        remote(g22_s.at[me], ow_h.at[own], peer, G2 + k)
        for k, peer in enumerate((at_x, at_y, at_xy))
    ]
    g2_local = pltpu.make_async_copy(g22_s.at[me], ow_h.at[own], local_sem.at[7])
    each(g2_copies, "start")
    g2_local.start()
    each(small_z, "wait")
    small_out[...] = ssum_s[2] + sgot_s[3] + sgot_s[4] + sgot_s[5]
    each(g2_copies, "wait")
    g2_local.wait()
    last = remote(ow_h.at[here], ow_h.at[here], at_core, GC2)
    last.start()
    home_wait(n2_s, lay6_h, LAY)
    home_wait(mix_s, gtok6_h, GTOK)
    last.wait()


def back(
    side, slots, isp, mixed, xs, cot, w_out, g2, w_gate, w_up, w_down,
    proj, filt, ss, cs, th, feat, st, ct, w_cond, table, table_t, m1, m2, mult, g1, w_in,
):
    n, d = cot.shape
    t = xs.shape[1]
    f2 = table.shape[0]
    f = f2 // 2
    hbm = pl.BlockSpec(memory_space=pl.ANY)
    vm = pl.BlockSpec(memory_space=pltpu.VMEM)
    smem = pl.BlockSpec(memory_space=pltpu.SMEM)
    b = lambda *s: pltpu.VMEM(s, BF)
    g = lambda *s: pltpu.VMEM(s, F32)
    q4, fd = d // 4, FC // 4
    return pl.pallas_call(
        functools.partial(back_kernel, side),
        name="back",
        out_shape=(
            jax.ShapeDtypeStruct((slots, t // 4, d), BF),
            jax.ShapeDtypeStruct((slots, t // 4, d), BF),
            jax.ShapeDtypeStruct((8, q4, FC), BF),
            jax.ShapeDtypeStruct((8, q4, FC), BF),
            jax.ShapeDtypeStruct((8, fd, d), BF),
            jax.ShapeDtypeStruct((8, 5, d // 16, FC), BF),
            jax.ShapeDtypeStruct((16, d), F32),
        ),
        in_specs=[smem, hbm, hbm, hbm, hbm, vm] + [hbm] * 9 + [vm, vm, hbm, hbm, hbm]
        + [vm, vm, vm, vm, hbm],
        out_specs=(hbm,) * 6 + (vm,),
        scratch_shapes=[
            g(n, d), g(n, d), g(n, d), g(n, 128),
            b(n, d), b(d, n), b(n, d), b(n, d), b(n, d), b(2, t, d),
            b(n, FC), b(n, FC), b(n, FC), b(4, d, FC), b(2, FC, d), b(d, d), b(d, d),
            b(f2, t), b(t, f2),
            b(4, q4, FC), b(4, q4, FC), b(4, fd, d),
            b(4, 4, q4, FC), b(4, 4, q4, FC), b(4, 4, fd, d),
            b(4, 2, q4, FC), b(4, 2, q4, FC), b(4, 2, fd, d),
            b(4, q4, FC), b(4, q4, FC), b(4, fd, d),
            b(3, q4, FC), b(3, q4, FC), b(3, fd, d),
            b(2, t, 3 * d), b(t, d), b(f2, d), b(f2, d), g(f, d), b(f, d), b(f, d), b(f, d),
            b(5, 4, q4, FC), b(3, 4, q4, FC), b(5, 4, d // 8, FC), b(4, 5, d // 16, FC),
            b(3, 5, d // 16, FC),
            g(16, d), g(6, 16, d), g(3, 16, d),
            pltpu.SemaphoreType.DMA((17,)),
            pltpu.SemaphoreType.DMA((4, 4)),
            pltpu.SemaphoreType.DMA((116,)),
            pltpu.SemaphoreType.DMA((116,)),
            pltpu.SemaphoreType.DMA((8,)),
        ],
        compiler_params=pltpu.CompilerParams(
            collective_id=1, has_side_effects=True, vmem_limit_bytes=65400 * 1024
        ),
    )(
        isp, mixed, xs, cot, w_out, g2, w_gate, w_up, w_down, proj, filt, ss, cs, th, feat,
        st, ct, w_cond, table, table_t, m1, m2, mult, g1, w_in,
    )


def on_device(
    tokens, kind, ln1_gain, w_in, short_taps, cond_taps, w_cond, cond_bias, w_out, ln2_gain,
    w_gate, w_up, w_down, cotangent,
):
    _, rows, slots, d = tokens.shape
    n = lax.axis_size("seq")
    dp_count = lax.axis_size("dp")
    rank = lax.axis_index("seq")
    span_long = rows * n
    is_long = kind[0] == 1

    freqs = -(-max(span_long // 2 + 1, n * (rows // 2 + 1)) // 16) * 16
    table, table_t, mult = wave_tables(is_long, rows, span_long, freqs)
    isp = jnp.where(is_long, 1.0 / span_long, 1.0 / rows).astype(F32).reshape(1)
    place = jnp.arange(span_long, dtype=jnp.int32)
    offset = jnp.where(is_long, place, place % rows)[:, None]
    m1 = jnp.broadcast_to((offset >= 1).astype(F32), (span_long, 128))
    m2 = jnp.broadcast_to((offset >= 2).astype(F32), (span_long, 128))

    tok6 = jnp.transpose(tokens[0], (1, 0, 2))
    cot6 = jnp.transpose(cotangent[0], (1, 0, 2))
    xs, cot = reshard_in(tok6, cot6)

    g1, g2 = ln1_gain.reshape(1, d), ln2_gain.reshape(1, d)
    proj, mixed, filt, sig_spec, cond_spec, th, feat = mix_forward(
        isp, xs, g1, w_in, short_taps, cond_taps, w_cond, cond_bias.reshape(1, d),
        table, table_t, m1, m2, mult,
    )
    side = math.isqrt(dp_count // 2)
    lay6, gtok6, dg, du, dd, dw, small = back(
        side, slots, isp, mixed, xs, cot, w_out, g2, w_gate, w_up, w_down,
        proj, filt, sig_spec, cond_spec, th, feat, short_taps, cond_taps, w_cond,
        table, table_t, m1, m2, mult, g1, w_in,
    )
    layer_out = jnp.transpose(lay6, (1, 0, 2))[None]
    grad_tokens = jnp.transpose(gtok6, (1, 0, 2))[None]

    sums = (dg, du, dd, dw)
    if dp_count > 8:
        groups = [
            [
                (y * side + x) * 2 + core
                for y in range(y0, side, 2)
                for x in range(x0, side, 2)
            ]
            for y0 in range(2)
            for x0 in range(2)
            for core in range(2)
        ]
        sums = [lax.psum(a.astype(F32), "dp", axis_index_groups=groups) for a in sums]
        small = lax.psum(small, "dp", axis_index_groups=groups)
    dg, du, dd, dw = (a.astype(F32) for a in sums)
    by_chunk = lambda a: jnp.transpose(
        a.reshape((2, 4) + a.shape[1:]), (2, 1, 0, 3)
    ).reshape(a.shape[1], -1)
    dw = dw.reshape((2, 4) + dw.shape[1:])
    by_core = lambda a: jnp.transpose(a, (1, 3, 0, 2, 4)).reshape(d // n, -1)
    part = lambda a, width: lax.dynamic_slice_in_dim(a, rank * width, width, a.ndim - 1)
    return (
        layer_out,
        grad_tokens,
        part(small[0], d // n),
        by_core(dw[:, :, 2:]),
        part(small[1:10].reshape(3, 3 * d), 3 * d // n),
        part(small[10:13], d // n),
        by_core(dw[:, :, 1:2]),
        part(small[13], d // n),
        by_core(dw[:, :, 0:1]),
        part(small[14], d // n),
        by_chunk(dg),
        by_chunk(du),
        dd.reshape(-1, d),
    )


def solution(mesh):
    rows = P("dp", "seq", None, None)
    return jax.shard_map(
        on_device,
        mesh=mesh,
        in_specs=(rows, P("dp")) + (P(),) * 11 + (rows,),
        out_specs=(
            rows,
            rows,
            P("seq"),
            P("seq", None),
            P(None, "seq"),
            P(None, "seq"),
            P("seq", None),
            P("seq"),
            P("seq", None),
            P("seq"),
            P("seq", None),
            P("seq", None),
            P("seq", None),
        ),
        check_vma=False,
    )
```

time: 1440 us -> 363 us (0.25)
  waiting for transfers between devices: 916 us -> 0 us
  Pallas kernels: 0 us -> 316 us
  matrix products: 246 us -> 0 us
  local copies, waits for them, and re-layouts: 147 us -> 27.5 us
  blocking collectives: 43.3 us -> 0 us
  other arithmetic: 46.6 us -> 10.3 us
    psum x1 -> x0, waiting for transfers between devices: 475 us -> none  [on_device(): lax.psum((grad_ln1, grad_w_in, grad_short_taps, grad_cond_taps, grad_w_co...]
    pallas_call x0 -> x3, Pallas kernels: none -> 316 us  [the longest x1 233 us: back(): pl.pallas_call(functools.partial(back_kernel, side), name='back', out_sha...]
    dot_general x30 -> x0, matrix products: 246 us -> none  [the longest x1 17.3 us: on_device(): jnp.einsum('nd,fd->nf', cot_rows, w_down, preferred_element_type=jnp.floa...]
    all_gather x3 -> x0, waiting for transfers between devices: 232 us -> none  [the longest x1 88.4 us: on_device(): lax.all_gather(cond_low, 'seq', axis=0, tiled=True).astype(jnp.float32)]
    reduce_scatter x2 -> x0, waiting for transfers between devices: 205 us -> none  [the longest x1 125 us: on_device(): lax.psum_scatter(jnp.concatenate([signal_term, cond_term], axis=2).astype...]
    psum x1 -> x0, blocking collectives: 43.3 us -> none  [on_device(): lax.psum((grad_ln1, grad_w_in, grad_short_taps, grad_cond_taps, grad_w_co...]
    convert_element_type x10 -> x0, local copies, waits for them, and re-layouts: 40.1 us -> none  [the longest x2 12.8 us: on_device(): proj_f = proj_low.astype(jnp.float32)]
    dynamic_slice x11 -> x5, local copies, waits for them, and re-layouts: 23.2 us -> 3.25 us  [on_device(): lax.dynamic_slice_in_dim(a, rank * width, width, a.ndim - 1)]
  transfers between devices with their start and end apart: 10 -> 0, of which waited for: 7 -> 0; matrix products, arithmetic and copies ran while one was open for 12% -> 0% of each run, Pallas kernels for 0% -> 0%
where the time goes in v1:
time: 363 us; the launch traced here: 356 us
  Pallas kernels  316 us (87%)
  local copies, waits for them, and re-layouts  27.5 us (8%)
  other arithmetic  10.3 us (3%)
    pallas_call x1, Pallas kernels, back(): pl.pallas_call(functools.partial(back_kernel, side), name='back', out_sha...  233 us
    pallas_call x1, Pallas kernels, reshard_in(): pl.pallas_call(reshard_in_kernel, name='reshard_in', out_shape=(jax.Shape...  58 us
    pallas_call x1, Pallas kernels, mix_forward(): pl.pallas_call(fwd_kernel, name='mix_forward', grid=(2,), out_shape=(jax....  25.5 us
    reshape x4, local copies, waits for them, and re-layouts, on_device(): by_chunk = lambda a: jnp.transpose(a.reshape((2, 4) + a.shape[1:]), (2, 1...  9.74 us

profile of v1, /device:TPU:25, one launch (start us, length us, event | category | flops | bytes accessed | tf_op | source)
XLA Modules:
  0.0 355.9 jit_solution(16160155234336698544)
XLA Ops:
  1.3 4.2 %select_convert_fusion.1 = (bf16[272,512]{0,1:T(8,128)(2,1)S(1)}, bf16[272,512]{0,1:T(8,128)(2,1)S(1)}) fusion(s32[272]{0:T(512)S(1)} %get-tuple-element.57, s32[512]{0:T(512)S(1)} %get-tuple-element.55, pred[272]{0:T(512)(128)(4,1)S(1)} %get-tuple-element.59, pred[272]{0:T(512)(128)(4,1)S(1)} %get-tuple-element.58, pred[]{:T(512)} %bitcast, ...), kind=kLoop, calls=%fused_computation.19 | loop fusion | flops 4874240 | bytes 563873 | tf_op jit(solution)/shard_map/convert.8
  5.8 1.0 copy.34.w_ref.refs_18_
  6.8 1.1 fusion.26.wt_ref.refs_19_
  7.9 0.8 broadcast_in_dim.45.m1_ref.refs_20_
  8.7 0.8 broadcast_in_dim.46.m2_ref.refs_21_
  9.6 0.8 broadcast_in_dim.50.mult_ref.refs_22_
  10.3 58.0 %reshard_in.1 = (bf16[2,512,768]{2,1,0:T(8,128)(2,1)}, bf16[768,768]{1,0:T(8,128)(2,1)}) custom-call(bf16[6,128,768]{2,1,0:T(8,128)(2,1)} %bitcast.54, bf16[6,128,768]{2,1,0:T(8,128)(2,1)} %bitcast.55), custom_call_target="tpu_custom_call" | custom-call | tf_op jit(solution)/shard_map/reshard_in/pallas_call | solution.py:163
  68.3 0.6 reshape.229.g1_ref.refs_23_
  68.9 0.6 reshape.230.cb_ref
  69.5 25.5 %mix_forward.1 = (bf16[2,512,2304]{2,1,0:T(8,128)(2,1)}, bf16[2,512,768]{2,1,0:T(8,128)(2,1)}, bf16[2,512,768]{2,1,0:T(8,128)(2,1)}, bf16[2,544,768]{2,1,0:T(8,1...) custom-call(f32[1]{0:T(128)} %bitcast.1.isp_ref.refs_0_, ...), custom_call_target="tpu_custom_call" | custom-call | tf_op jit(solution)/shard_map/mix_forward/pallas_call | solution.py:245
  94.9 0.6 reshape.231.refs_5_
  95.5 232.7 %back.1 = (bf16[6,128,768]{2,1,0:T(8,128)(2,1)}, bf16[6,128,768]{2,1,0:T(8,128)(2,1)}, bf16[8,192,384]{2,1,0:T(8,128)(2,1)}, bf16[8,192,384]{2,1,0:T(8,128)(2,1)...) custom-call(f32[1]{0:T(128)} %bitcast.1.isp_ref.refs_0_, ...), custom_call_target="tpu_custom_call" | custom-call | tf_op jit(solution)/shard_map/back/pallas_call | solution.py:961
  328.3 1.4 convert_bitcast_fusion.1
  329.7 1.8 copy.39
  331.5 3.2 reshape.249
  334.9 1.8 copy.40
  336.7 2.9 reshape.251
  339.6 1.3 slice.32
  340.9 0.9 copy.45
  341.9 2.3 reshape.234
  344.1 1.6 convert.16
  345.8 0.5 copy.37
  346.3 0.9 copy.42
  347.6 0.9 copy.43
  348.5 1.7 bitcast_convert_fusion
  350.2 0.7 constant_dynamic-slice_fusion.3
  350.8 0.7 constant_dynamic-slice_fusion.2
  351.5 0.6 constant_dynamic-slice_fusion.4
  352.2 0.6 constant_dynamic-slice_fusion.1
  352.8 0.6 constant_dynamic-slice_fusion
  353.4 1.0 copy.49
  354.5 1.0 copy.50
  (29 shorter events, 1.0 us)
Async XLA Ops:
  7.9 60.4 %copy-start.5 = (f32[768]{0:T(1024)S(1)}, f32[768]{0:T(1024)}, u32[]{:S(2)}) copy-start(f32[768]{0:T(1024)} %param.16) | copy-start | bytes 9220
  7.9 61.0 %copy-start.6 = (f32[768]{0:T(1024)S(1)}, f32[768]{0:T(1024)}, u32[]{:S(2)}) copy-start(f32[768]{0:T(1024)} %param.21) | copy-start | bytes 9220
  69.4 25.5 %copy-start.7 = (f32[768]{0:T(1024)S(1)}, f32[768]{0:T(1024)}, u32[]{:S(2)}) copy-start(f32[768]{0:T(1024)} %param.23) | copy-start | bytes 9220
  331.5 3.2 copy-start.1
  346.3 2.2 copy-start
  348.5 1.7 copy-start.4
  348.5 5.0 %copy-start.3 = (bf16[6,128,768]{2,1,0:T(8,128)(2,1)S(1)}, bf16[6,128,768]{2,1,0:T(8,128)(2,1)}, u32[]{:S(2)}) copy-start(bf16[6,128,768]{2,1,0:T(8,128)(2,1)} %get-tuple-element.38) | copy-start | bytes 3538948
  350.1 4.3 %copy-start.2 = (bf16[6,128,768]{2,1,0:T(8,128)(2,1)S(1)}, bf16[6,128,768]{2,1,0:T(8,128)(2,1)}, u32[]{:S(2)}) copy-start(bf16[6,128,768]{2,1,0:T(8,128)(2,1)} %get-tuple-element.39) | copy-start | bytes 3538948

commit v2 on v1

v2 whole, which is shorter than its diff:
```python
import functools
import math

import jax
import jax.numpy as jnp
from jax import lax
from jax.experimental import pallas as pl
from jax.experimental.pallas import tpu as pltpu
from jax.sharding import PartitionSpec as P

BF = jnp.bfloat16
F32 = jnp.float32
MESH = pl.DeviceIdType.MESH
EPS = 1e-05
CB = 256
FC = 384
RB = 256
VMEM_LIMIT = 60 * 2**20


def mm(a, b):
    return jnp.dot(a, b, preferred_element_type=F32)


def mm_nt(a, b):
    return lax.dot_general(a, b, (((1,), (1,)), ((), ())), preferred_element_type=F32)


def mm_tn(a, b):
    return lax.dot_general(a, b, (((0,), (0,)), ((), ())), preferred_element_type=F32)


def unit_rows(x):
    mean = jnp.mean(x, axis=-1, keepdims=True)
    centered = x - mean
    r = lax.rsqrt(jnp.mean(centered * centered, axis=-1, keepdims=True) + EPS)
    return centered * r, r


def unit_back(g, u, r, gain):
    e = g * gain
    return r * (
        e - jnp.mean(e, axis=-1, keepdims=True) - u * jnp.mean(e * u, axis=-1, keepdims=True)
    )


def lanes(ref, width):
    m = ref[...]
    return jnp.concatenate([m] * (width // m.shape[1]), axis=1)


def down(a, j):
    return pltpu.roll(a, j, axis=0)


def up(a, j):
    return pltpu.roll(a, a.shape[0] - j, axis=0)


def conv(a, taps, m1, m2):
    return taps[0:1] * a + taps[1:2] * (down(a, 1) * m1) + taps[2:3] * (down(a, 2) * m2)


def conv_back(g, taps, m1, m2):
    return taps[0:1] * g + taps[1:2] * up(g * m1, 1) + taps[2:3] * up(g * m2, 2)


def tap_sums(g, a, m1, m2):
    return jnp.concatenate(
        [
            jnp.sum(g * a, axis=0, keepdims=True),
            jnp.sum(g * (down(a, 1) * m1), axis=0, keepdims=True),
            jnp.sum(g * (down(a, 2) * m2), axis=0, keepdims=True),
        ],
        axis=0,
    )


def cols_at(c, width, base=0):
    return pl.ds(pl.multiple_of(base + c * width, 128), width)


def wave_tables(is_long, short, span_long, freqs):
    i = jnp.arange(freqs, dtype=jnp.int32)[:, None]
    t = jnp.arange(span_long, dtype=jnp.int32)[None, :]
    blocks, half = span_long // short, short // 2 + 1
    f_short, b_short = i % half, i // half
    phase = jnp.where(
        is_long, (i * t) % span_long, ((f_short * (t % short)) % short) * blocks
    )
    kept = jnp.where(is_long, i <= span_long // 2, (b_short < blocks) & (t // short == b_short))
    angle = phase.astype(F32) * (2.0 * math.pi / span_long)
    kept_f = kept.astype(F32)
    table = jnp.concatenate([jnp.cos(angle) * kept_f, jnp.sin(angle) * kept_f], axis=0)
    once = jnp.where(
        is_long, (i == 0) | (i == span_long // 2), (f_short == 0) | (f_short == short // 2)
    )
    used = jnp.where(is_long, i <= span_long // 2, b_short < blocks)
    mult = jnp.where(used, jnp.where(once, 1.0, 2.0), 0.0).astype(F32)
    table = table.astype(BF)
    return table, table.T, jnp.broadcast_to(mult, (freqs, 128))


def reshard_in_kernel(tok_ref, cot_ref, xs_ref, cs_ref, local_sem, send_sem, recv_sem):
    dp, me = lax.axis_index("dp"), lax.axis_index("seq")
    n = lax.axis_size("seq")
    rows = tok_ref.shape[1]
    barrier = pltpu.get_barrier_semaphore()
    for k in range(1, n):
        pl.semaphore_signal(
            barrier, inc=1, device_id=(dp, lax.rem(me + k, n)), device_id_type=MESH
        )
    pl.semaphore_wait(barrier, n - 1)
    at = pl.ds(pl.multiple_of(me * rows, rows), rows)
    half_at = pl.ds(pl.multiple_of(n * rows + lax.rem(me, 2) * rows, rows), rows)

    def copies(k, peer):
        moves = [
            (tok_ref.at[peer], xs_ref.at[0, at]),
            (tok_ref.at[n + peer // 2], xs_ref.at[1, at]),
            (cot_ref.at[peer], cs_ref.at[at]),
            (cot_ref.at[n + peer // 2], cs_ref.at[half_at]),
        ]
        if k == 0:
            return [
                pltpu.make_async_copy(s, d, local_sem.at[j]) for j, (s, d) in enumerate(moves)
            ]
        return [
            pltpu.make_async_remote_copy(
                src_ref=s,
                dst_ref=d,
                send_sem=send_sem.at[j, k],
                recv_sem=recv_sem.at[j, k],
                device_id=(dp, peer),
                device_id_type=MESH,
            )
            for j, (s, d) in enumerate(moves)
        ]

    peers = [lax.rem(me + k, n) for k in range(n)]
    sources = [lax.rem(me + n - k, n) for k in range(n)]
    sends_half = [lax.rem(p, 2) == me // 2 for p in peers]
    gets_half = [lax.rem(me, 2) == s // 2 for s in sources]
    all_copies = [copies(k, peers[k]) for k in range(n)]
    for j in range(3):
        for k in range(n):
            all_copies[k][j].start()
    for k in range(n):
        pl.when(sends_half[k])(all_copies[k][3].start)
    for j in range(3):
        for k in range(n):
            all_copies[k][j].wait()
    pl.when(sends_half[0])(all_copies[0][3].wait)
    for k in range(1, n):
        pl.when(sends_half[k])(all_copies[k][3].wait_send)
        pl.when(gets_half[k])(all_copies[k][3].wait_recv)


def reshard_in(tok, cot):
    slots, rows, d = tok.shape
    n = lax.axis_size("seq")
    any_spec = pl.BlockSpec(memory_space=pl.ANY)
    return pl.pallas_call(
        reshard_in_kernel,
        name="reshard_in",
        out_shape=(
            jax.ShapeDtypeStruct((2, n * rows, d), BF),
            jax.ShapeDtypeStruct((n * rows + n * rows // 2, d), BF),
        ),
        in_specs=[any_spec] * 2,
        out_specs=(any_spec, any_spec),
        scratch_shapes=[
            pltpu.SemaphoreType.DMA((4,)),
            pltpu.SemaphoreType.DMA((4, n)),
            pltpu.SemaphoreType.DMA((4, n)),
        ],
        compiler_params=pltpu.CompilerParams(collective_id=0, has_side_effects=True),
    )(tok, cot)


def fwd_kernel(
    isp_ref, x_ref, g1_ref, win_ref, st_ref, ct_ref, wc_ref, cb_ref, w_ref, wt_ref,
    m1_ref, m2_ref, mult_ref,
    proj_ref, mixed_ref, filt_ref, xs_ref, xc_ref, th_ref, feat_ref,
    n1_s, q_s,
):
    t, d = n1_s.shape
    f = th_ref.shape[1]
    isp = isp_ref[0]

    @pl.loop(0, t // 128)
    def _(r):
        rows = pl.ds(pl.multiple_of(r * 128, 128), 128)
        u, _ = unit_rows(x_ref[0, rows, :].astype(F32))
        n1_s[rows, :] = (u * g1_ref[...]).astype(BF)

    @pl.loop(0, d // CB)
    def _(c):
        m1, m2 = lanes(m1_ref, CB), lanes(m2_ref, CB)
        own = cols_at(c, CB)

        def part(k):
            cols = cols_at(c, CB, k * d)
            p = mm(n1_s[...], win_ref[:, cols]).astype(BF)
            proj_ref[0, :, cols] = p
            return conv(p.astype(F32), st_ref[:, cols], m1, m2)

        q_s[:, own] = part(0)
        key = part(1)
        value = part(2).astype(BF)
        value_f = value.astype(F32)
        signal = (key * value_f).astype(BF)
        xs_ref[0, :, own] = mm(w_ref[...], signal).astype(BF)
        cond = conv(value_f, ct_ref[:, own], m1, m2).astype(BF)
        xc = mm(w_ref[...], cond)
        xc_ref[0, :, own] = xc.astype(BF)
        power = (xc[:f] * xc[:f] + xc[f:] * xc[f:]) * isp
        feat_ref[0, :, own] = jnp.log1p(power).astype(BF)

    @pl.loop(0, d // CB)
    def _(c):
        own = cols_at(c, CB)
        th = jnp.tanh(mm(feat_ref[0], wc_ref[:, own]) + cb_ref[:, own])
        th_ref[0, :, own] = th
        g = (1.0 + th) * (lanes(mult_ref, CB) * isp)
        xs = xs_ref[0, :, own].astype(F32)
        y = jnp.concatenate([(g * xs[:f]).astype(BF), (g * xs[f:]).astype(BF)], axis=0)
        filt = mm(wt_ref[...], y)
        filt_ref[0, :, own] = filt.astype(BF)
        mixed_ref[0, :, own] = (q_s[:, own] * filt).astype(BF)


def whole(shape):
    return pl.BlockSpec(shape, lambda *_: (0,) * len(shape), pipeline_mode=pl.Buffered(1))


def per_slot(shape):
    return pl.BlockSpec((1,) + shape, lambda s, *_: (s,) + (0,) * len(shape))


def mix_forward(isp, xs, g1, w_in, st, ct, w_cond, cb, table, table_t, m1, m2, mult):
    _, t, d = xs.shape
    f2 = table.shape[0]
    f = f2 // 2
    return pl.pallas_call(
        fwd_kernel,
        name="mix_forward",
        grid=(2,),
        out_shape=(
            jax.ShapeDtypeStruct((2, t, 3 * d), BF),
            jax.ShapeDtypeStruct((2, t, d), BF),
            jax.ShapeDtypeStruct((2, t, d), BF),
            jax.ShapeDtypeStruct((2, f2, d), BF),
            jax.ShapeDtypeStruct((2, f2, d), BF),
            jax.ShapeDtypeStruct((2, f, d), F32),
            jax.ShapeDtypeStruct((2, f, d), BF),
        ),
        in_specs=[
            pl.BlockSpec(memory_space=pltpu.SMEM),
            per_slot((t, d)),
            whole((1, d)),
            whole((d, 3 * d)),
            whole((3, 3 * d)),
            whole((3, d)),
            whole((d, d)),
            whole((1, d)),
            whole((f2, t)),
            whole((t, f2)),
            whole((t, 128)),
            whole((t, 128)),
            whole((f, 128)),
        ],
        out_specs=(
            per_slot((t, 3 * d)),
            per_slot((t, d)),
            per_slot((t, d)),
            per_slot((f2, d)),
            per_slot((f2, d)),
            per_slot((f, d)),
            per_slot((f, d)),
        ),
        scratch_shapes=[pltpu.VMEM((t, d), BF), pltpu.VMEM((t, d), F32)],
        compiler_params=pltpu.CompilerParams(vmem_limit_bytes=VMEM_LIMIT),
    )(isp, xs, g1, w_in, st, ct, w_cond, cb, table, table_t, m1, m2, mult)


def add_into(dst, src):
    dst[...] = (dst[...].astype(F32) + src[...].astype(F32)).astype(dst.dtype)


def back_kernel(side, *refs):
    (
        isp_ref, isl_ref, mixed_h, xs_h, cot_h, wo_h, g2_ref, wg_h, wu_h, wd_h,
        proj_h, filt_h, ss_h, cs_h, th_h, feat_h,
        st_ref, ct_ref, wc_h, tab_h, tabt_h, mult_ref, g1_ref, win_h,
        lay6_h, gtok6_h, odg_h, odu_h, odd_h, owo_h, owc_h, owi_h, small_out,
        a_s, b_s, u_s, r_s, n2_s, n2t_s, cot_s, mg_s, gmix_s,
        act_s, gg_s, gu_s, w0_s, w1_s, w2_s, wo_s, wc_s, tab_s, tabt_s, m1_ref, m2_ref,
        sbg_s, sbu_s, sbd_s, cg_s, cu_s, cd_s,
        dgg_s, dgu_s, xg_s, xu_s, yg_s, yu_s, zg_s, zu_s, d1_s, d2_s, zd_s,
        proj_s, filt_s, ss_s, cs_s, th_s, feat_s, gpre_s, gprem_s,
        c2_s, raw2_s, r2_s, z2_s, cw_s, sbw_s, rw_s, zw_s, small_s, sgot_s, ssum_s,
        load_sem, w_sem, send_sem, recv_sem, local_sem,
    ) = refs
    n, d = n2_s.shape
    t = filt_s.shape[0]
    f = th_s.shape[0]
    isp = isp_ref[0]
    h = d // 2
    quarter = d // 4
    step48 = d // 16
    dr = h // 4

    dp, me = lax.axis_index("dp"), lax.axis_index("seq")
    core = lax.rem(dp, 2)
    x = lax.rem(lax.rem(dp // 2, side), 2)
    y = lax.rem(dp // (2 * side), 2)
    dp_x = dp + 2 - 4 * x
    dp_y = dp + 2 * side - 4 * side * y
    at_core, at_x, at_y = (dp + 1 - 2 * core, me), (dp_x, me), (dp_y, me)
    at_xy = (dp_x + dp_y - dp, me)
    peers = [lax.rem(me + k, 4) for k in range(4)]
    at_z = [(dp, peers[k]) for k in range(4)]
    half = lax.rem(me, 2)
    at_pair = (dp, me + 1 - 2 * half)
    half_at = pl.ds(pl.multiple_of(half * RB, RB), RB)
    xy = 2 * x + y
    diag, by_x, by_y = 3 - xy, 2 * (1 - x) + y, 2 * x + 1 - y

    def owner(s):
        if isinstance(s, int):
            return (diag, by_x, by_y, xy)[s]
        return 2 * jnp.where(s < 2, 1 - x, x) + jnp.where(lax.rem(s, 2) == 0, 1 - y, y)

    def rows_at(i, size, base=0):
        return pl.ds(pl.multiple_of(base + i * size, math.gcd(size, base) if base else size), size)

    def each(copies, what):
        for c in copies:
            getattr(c, what)()

    row_moves = lambda src, dst: [
        (src.at[0], dst.at[pl.ds(0, t)]),
        (src.at[1, half_at], dst.at[pl.ds(t, RB)]),
    ]
    moves = (
        row_moves(mixed_h, mg_s)
        + row_moves(xs_h, gmix_s)
        + [(wo_h, wo_s), (cot_h, cot_s)]
        + [(tab_h, tab_s), (tabt_h, tabt_s), (wc_h, wc_s), (proj_h, proj_s)]
    )
    loads = [pltpu.make_async_copy(s, e, load_sem.at[j]) for j, (s, e) in enumerate(moves)]
    slot_moves = [(filt_h, filt_s), (ss_h, ss_s), (th_h, th_s), (cs_h, cs_s), (feat_h, feat_s)]
    slot_load = lambda slot, j: pltpu.make_async_copy(
        slot_moves[j][0].at[slot], slot_moves[j][1], load_sem.at[10 + j]
    )
    x_loads = [
        pltpu.make_async_copy(a, b, load_sem.at[15 + j])
        for j, (a, b) in enumerate(row_moves(xs_h, cot_s))
    ]

    def weights(s):
        cols = cols_at(owner(s), d)
        return [
            pltpu.make_async_copy(wg_h.at[:, cols], w0_s, w_sem.at[0]),
            pltpu.make_async_copy(wu_h.at[:, cols], w1_s, w_sem.at[1]),
            pltpu.make_async_copy(wd_h.at[cols, :], w2_s, w_sem.at[2]),
        ]

    win_loads = [
        pltpu.make_async_copy(win_h.at[:, k * d : (k + 1) * d], w, w_sem.at[3 + k])
        for k, w in enumerate((w0_s, w1_s, w2_s))
    ]

    each(loads[:6], "start")
    each(weights(0), "start")
    each(loads[6:], "start")
    for j in range(5):
        slot_load(0, j).start()

    barrier = pltpu.get_barrier_semaphore()
    everyone = [at_core, at_x, at_y, at_xy] + at_z[1:]
    for peer in everyone:
        pl.semaphore_signal(barrier, inc=1, device_id=peer, device_id_type=MESH)
    pl.semaphore_wait(barrier, len(everyone))

    place = lax.broadcasted_iota(jnp.int32, m1_ref.shape, 0)
    short = place & (t // 4 - 1)
    place = short + isl_ref[0] * (place - short)
    m1_ref[...] = (place >= 1).astype(F32)
    m2_ref[...] = (place >= 2).astype(F32)

    def remote(src, dst, peer, j):
        return pltpu.make_async_remote_copy(
            src_ref=src,
            dst_ref=dst,
            send_sem=send_sem.at[j],
            recv_sem=recv_sem.at[j],
            device_id=peer,
            device_id_type=MESH,
        )

    C, DG, XS, YS, ZD, ZG, GA, GC, DX, DY = 0, 12, 20, 22, 24, 27, 36, 45, 130, 138
    C2, D2, XS2, YS2, Z2, GA2, GC2 = 57, 59, 67, 69, 71, 77, 83
    CW, DW, XW, YW, ZW, GW, GCW = 91, 95, 99, 100, 101, 104, 107
    LAY, GT0, GT1, PAIR, SMALL = 111, 117, 120, 123, 124

    each(loads[:6], "wait")

    @pl.loop(0, n // RB)
    def _(i):
        rows = rows_at(i, RB)
        hid = gmix_s[rows, :].astype(F32) + mm(mg_s[rows, :], wo_s[...])
        a_s[rows, :] = hid
        b_s[rows, :] = jnp.zeros_like(hid)
        u, r = unit_rows(hid)
        u_s[rows, :] = u
        r_s[rows, :] = jnp.broadcast_to(r, (RB, 128))
        n2 = u * g2_ref[...]
        n2_s[rows, :] = n2.astype(BF)
        n2t_s[:, rows] = n2.T.astype(BF)

    pairs = ((sbg_s, cg_s, dgg_s, xg_s, yg_s, zg_s), (sbu_s, cu_s, dgu_s, xu_s, yu_s, zu_s))
    rank_rows = lambda q: pl.ds(q * quarter, quarter)

    def core_copies(s):
        bufs = ((sbg_s, cg_s.at[s]), (sbu_s, cu_s.at[s]), (sbd_s, cd_s.at[owner(s)]))
        return [remote(a, b, at_core, C + 4 * j + s) for j, (a, b) in enumerate(bufs)]

    def diag_copies(odd):
        return [
            remote(p[1].at[0, rank_rows(q)], p[2].at[rank_rows(q)], at_y if odd else at_x, DG + 4 * j + q)
            for j, p in enumerate(pairs)
            for q in ((1, 3) if odd else (0, 2))
        ]

    x_copies = lambda: [remote(p[1].at[1], p[3], at_x, XS + j) for j, p in enumerate(pairs)]
    y_copies = lambda: [remote(p[1].at[2], p[4], at_y, YS + j) for j, p in enumerate(pairs)]

    def add_ranks(s, first):
        for p in pairs:
            for q in (first, first + 2):
                add_into(p[1].at[s, rank_rows(q)], p[2].at[rank_rows(q)])

    def down_first(q, peer, k, e):
        return remote(cd_s.at[q, rows_at(k, dr)], d1_s.at[q, e], peer, DX + 2 * q + e)

    def step_sums(s):
        q = owner(s)

        @pl.when(lax.rem(q, 2) == 0)
        def _():
            down_first(q, at_x, diag, 0).start()
            down_first(q, at_x, by_x, 1).start()

        @pl.when(lax.rem(q, 2) == 1)
        def _():
            down_first(q, at_y, diag, 0).start()
            down_first(q, at_y, by_y, 1).start()

        @pl.when(s == 0)
        def _():
            each(diag_copies(False), "start")
            each(diag_copies(True), "start")

        @pl.when(s == 1)
        def _():
            each(diag_copies(True), "wait_recv")
            add_ranks(1, 1)
            each(x_copies(), "start")

        @pl.when(s == 2)
        def _():
            each(diag_copies(False), "wait_recv")
            add_ranks(2, 0)
            each(y_copies(), "start")

    @pl.loop(0, 4)
    def _(s):
        each(weights(s), "wait")

        @pl.loop(0, n // RB)
        def _(i):
            rows = rows_at(i, RB)
            n2 = n2_s[rows, :]
            pre = mm(n2, w0_s[...])
            lin = mm(n2, w1_s[...])
            g_act = mm_nt(cot_s[rows, :], w2_s[...])
            sg = 1.0 / (1.0 + jnp.exp(-pre))
            silu = pre * sg
            act = (silu * lin).astype(BF)
            act_s[rows, :] = act
            g_up = (g_act * silu).astype(BF)
            gu_s[rows, :] = g_up
            g_gate = (g_act * lin * sg * (1.0 + pre * (1.0 - sg))).astype(BF)
            gg_s[rows, :] = g_gate
            a_s[rows, :] += mm(act, w2_s[...])
            b_s[rows, :] += mm_nt(g_gate, w0_s[...]) + mm_nt(g_up, w1_s[...])

        @pl.when(s < 3)
        def _():
            each(weights(s + 1), "start")

        @pl.when(s > 0)
        def _():
            each(core_copies(s - 1), "wait_send")

        def product(which, j, put):
            cols = cols_at(which, h)

            @pl.loop(0, d // RB)
            def _(i):
                rows, out = rows_at(i, RB), cols_at(i, RB)
                if j == 2:
                    put(slice(None), out, mm_tn(act_s[:, cols], cot_s[:, out]))
                else:
                    put(rows, slice(None), mm(n2t_s[rows, :], (gg_s, gu_s)[j][:, cols]))

        for j, buf in enumerate((sbg_s, sbu_s, sbd_s)):

            def put(rows, cols, value, buf=buf):
                buf[rows, cols] = value.astype(BF)

            product(1 - core, j, put)
            core_copies(s)[j].start()
        for j, (buf, at) in enumerate(((cg_s, s), (cu_s, s), (cd_s, owner(s)))):
            core_copies(s)[j].wait_recv()

            def put(rows, cols, value, buf=buf, at=at):
                buf[at, rows, cols] = (buf[at, rows, cols].astype(F32) + value).astype(BF)

            product(core, j, put)
        step_sums(s)

    each(win_loads, "start")
    small_s[...] = jnp.zeros_like(small_s)

    @pl.loop(0, n // RB)
    def _(i):
        rows = rows_at(i, RB)
        n2_s[rows, :] = a_s[rows, :].astype(BF)
        g, u = b_s[rows, :], u_s[rows, :]
        small_s[14:15, :] += jnp.sum(g * u, axis=0, keepdims=True)
        gh = cot_s[rows, :].astype(F32) + unit_back(g, u, r_s[rows, 0:1], g2_ref[...])
        gmix_s[rows, :] = gh.astype(BF)

    each(x_loads, "start")
    pair_at = rows_at(half, RB, n)
    mg_s[pair_at, :] = mm_nt(gmix_s[t:, :], wo_s[...]).astype(BF)
    pair_copy = remote(mg_s.at[pair_at], mg_s.at[pair_at], at_pair, PAIR)
    pair_copy.start()

    each(core_copies(3), "wait_send")

    def out_half(which, dst):
        cols = cols_at(which, h)

        @pl.loop(0, d // RB)
        def _(i):
            dst[rows_at(i, RB), :] = mm_tn(mg_s[0:n, cols_at(i, RB)], gmix_s[:, cols]).astype(BF)

    second = lambda c, buf: remote(buf, c2_s.at[c], at_core, C2 + c)
    out_half(1 - core, sbg_s)
    second(0, sbg_s).start()
    out_half(core, raw2_s.at[0])

    each(x_copies(), "wait_recv")
    for p in pairs:

        @pl.loop(0, 4)
        def _(q, p=p):
            add_into(p[1].at[3, rows_at(q, quarter)], p[3].at[rows_at(q, quarter)])

    @pl.loop(0, t // RB)
    def _(i):
        rows = rows_at(i, RB)
        mg_s[rows, :] = mm_nt(gmix_s[rows, :], wo_s[...]).astype(BF)

    each(y_copies(), "wait_recv")
    for p in pairs:

        @pl.loop(0, 4)
        def _(q, p=p):
            add_into(p[1].at[3, rows_at(q, quarter)], p[4].at[rows_at(q, quarter)])

    z_copies = [
        remote(p[1].at[3, rows_at(peers[k], quarter)], p[5].at[k - 1], at_z[k], ZG + 3 * j + k - 1)
        for j, p in enumerate(pairs)
        for k in range(1, 4)
    ]
    each(z_copies, "start")

    rows128 = lay6_h.shape[1]
    sources = [lax.rem(me + 4 - k, 4) for k in range(4)]
    sends_half = [half == p // 2 for p in peers]
    gets_half = [lax.rem(s, 2) == me // 2 for s in sources]

    def home(buf, out, part, base, k):
        if part == 0:
            src, dst = buf.at[rows_at(peers[k], rows128)], out.at[me]
        else:
            src, dst = buf.at[rows_at(lax.rem(peers[k], 2), rows128, t)], out.at[4 + me // 2]
        if k == 0:
            return pltpu.make_async_copy(src, dst, local_sem.at[base])
        return remote(src, dst, at_z[k], base + k - 1)

    def home_start(buf, out, part, base, local):
        for k in range(4):
            copy = home(buf, out, part, base if k else local, k)
            if part == 0:
                copy.start()
            else:
                pl.when(sends_half[k])(copy.start)

    def home_wait(buf, out, part, base, local):
        for k in range(4):
            copy = home(buf, out, part, base if k else local, k)
            if part == 0:
                copy.wait()
            elif k == 0:
                pl.when(sends_half[0])(copy.wait)
            else:
                pl.when(sends_half[k])(copy.wait_send)
                pl.when(gets_half[k])(copy.wait_recv)

    for q in range(4):
        for e in range(2):
            remote(d1_s.at[q, e], d1_s.at[q, e], at_x, DX + 2 * q + e).wait()
        add_into(d1_s.at[q, 0], cd_s.at[q, rows_at(by_x if q % 2 else by_y, dr)])
        add_into(d1_s.at[q, 1], cd_s.at[q, rows_at(xy, dr)])
    down_second = [
        remote(d1_s.at[q, 0], d2_s.at[q], at_x if q % 2 else at_y, DY + q) for q in range(4)
    ]
    each(down_second, "start")
    down_z = [
        remote(d1_s.at[peers[k], 1], zd_s.at[k - 1], at_z[k], ZD + k - 1) for k in range(1, 4)
    ]

    def gather(src, view, base, first_local):
        return [
            remote(src, view(xy, core), peer, base + k)
            for k, peer in enumerate((at_x, at_y, at_xy))
        ], pltpu.make_async_copy(src, view(xy, core), local_sem.at[first_local])

    def gather_core(view, base):
        return [remote(view(k, core), view(k, core), at_core, base + k) for k in range(4)]

    view_dg = lambda k, c: odg_h.at[:, cols_at(2 * k + c, h)]
    view_du = lambda k, c: odu_h.at[:, cols_at(2 * k + c, h)]
    view_dd = lambda k, c: odd_h.at[rows_at(4 * c + k, dr)]
    view_wo = lambda k, c: owo_h.at[rows_at(k, step48), cols_at(c, h)]
    view_wc = lambda k, c: owc_h.at[rows_at(k, step48), cols_at(c, h)]
    view_wi = lambda k, c: owi_h.at[rows_at(k, step48), cols_at(c, 3 * h)]
    gathers = [
        gather(cg_s.at[3, rows_at(me, quarter)], view_dg, GA, 4),
        gather(cu_s.at[3, rows_at(me, quarter)], view_du, GA + 3, 5),
        gather(d1_s.at[me, 1], view_dd, GA + 6, 6),
    ]
    core_gathers = (
        gather_core(view_dg, GC) + gather_core(view_du, GC + 4) + gather_core(view_dd, GC + 8)
    )

    each(loads[6:], "wait")
    each(x_loads, "wait")

    @pl.loop(0, 2)
    def _(slot):
        share = jnp.where(slot == 0, 1.0, 0.5)
        for j in range(3):
            slot_load(slot, j).wait()
        pl.when(slot == 1)(pair_copy.wait)
        gm_at = pl.ds(pl.multiple_of(slot * n, RB), t)

        @pl.loop(0, d // CB)
        def _(c):
            m1, m2 = lanes(m1_ref, CB), lanes(m2_ref, CB)
            mult = lanes(mult_ref, CB)
            cols = cols_at(c, CB)
            query = conv(proj_s[slot, :, cols].astype(F32), st_ref[:, cols], m1, m2)
            gm = mg_s[gm_at, cols].astype(F32)
            a_s[0:t, cols] = gm * filt_s[:, cols].astype(F32)
            spec = mm(tab_s[...], (gm * query).astype(BF)) * isp
            ss = ss_s[:, cols].astype(F32)
            th = th_s[:, cols]
            g_gain = spec[:f] * ss[:f] + spec[f:] * ss[f:]
            g_pre = (g_gain * (1.0 - th * th)).astype(BF)
            gpre_s[:, cols] = g_pre
            weighted = g_pre.astype(F32) * mult
            gprem_s[:, cols] = weighted.astype(BF)
            small_s[13:14, cols] += share * jnp.sum(weighted, axis=0, keepdims=True)
            g = (1.0 + th) * mult
            yy = jnp.concatenate(
                [(g * spec[:f]).astype(BF), (g * spec[f:]).astype(BF)], axis=0
            )
            b_s[0:t, cols] = mm(tabt_s[...], yy)

        @pl.when(slot == 0)
        def _():
            for j in range(3):
                slot_load(1, j).start()
            each(down_second, "wait")
            for q in range(4):
                add_into(d1_s.at[q, 1], d2_s.at[q])
            each(down_z, "start")
            home_start(n2_s, lay6_h, 0, LAY, 0)
            home_start(n2_s, lay6_h, 1, LAY + 3, 1)

        @pl.when(slot == 1)
        def _():
            each(z_copies, "wait")
            for p in pairs:
                rows = rows_at(me, quarter)
                total = p[1][3, rows, :].astype(F32)
                for k in range(3):
                    total += p[5][k].astype(F32)
                p[1][3, rows, :] = total.astype(BF)
            each(down_z, "wait")
            total = d1_s[me, 1].astype(F32)
            for k in range(3):
                total += zd_s[k].astype(F32)
            d1_s[me, 1] = total.astype(BF)
            for copies, local in gathers:
                each(copies, "start")
                local.start()

        for j in range(3, 5):
            slot_load(slot, j).wait()

        @pl.loop(0, d // CB)
        def _(c):
            m1, m2 = lanes(m1_ref, CB), lanes(m2_ref, CB)
            cols = cols_at(c, CB)
            g_feat = mm_nt(gpre_s[...], wc_s[cols, :])
            xc = cs_s[:, cols].astype(F32)
            power = (xc[:f] * xc[:f] + xc[f:] * xc[f:]) * isp
            g_pow = g_feat / (1.0 + power) * (lanes(mult_ref, CB) * (2.0 * isp))
            yy = jnp.concatenate(
                [(g_pow * xc[:f]).astype(BF), (g_pow * xc[f:]).astype(BF)], axis=0
            )
            g_cond = mm(tabt_s[...], yy)
            dwc = share * mm_tn(feat_s[:, cols], gprem_s[...])

            @pl.when(slot == 0)
            def _():
                u_s[cols, :] = dwc

            @pl.when(slot == 1)
            def _():
                u_s[cols, :] += dwc

            def finish(part, g_conv, p):
                at = cols_at(c, CB, part * d)
                sums = share * tap_sums(g_conv, p, m1, m2)
                for j in range(3):
                    row = 1 + 3 * j + part
                    small_s[row : row + 1, cols] += sums[j : j + 1]
                proj_s[slot, :, at] = conv_back(g_conv, st_ref[:, at], m1, m2).astype(BF)

            finish(0, a_s[0:t, cols], proj_s[slot, :, cols].astype(F32))
            key_cols, value_cols = cols_at(c, CB, d), cols_at(c, CB, 2 * d)
            p_value = proj_s[slot, :, value_cols].astype(F32)
            value = conv(p_value, st_ref[:, value_cols], m1, m2).astype(BF).astype(F32)
            g_sig = b_s[0:t, cols]
            p_key = proj_s[slot, :, key_cols].astype(F32)
            key = conv(p_key, st_ref[:, key_cols], m1, m2)
            finish(1, g_sig * value, p_key)
            sums = share * tap_sums(g_cond, value, m1, m2)
            for j in range(3):
                small_s[10 + j : 11 + j, cols] += sums[j : j + 1]
            finish(2, g_sig * key + conv_back(g_cond, ct_ref[:, cols], m1, m2), p_value)

        @pl.when(slot == 0)
        def _():
            for j in range(3, 5):
                slot_load(1, j).start()
            each(win_loads, "wait")

        first = jnp.where(slot == 0, 0, half)

        @pl.loop(0, 2 - slot)
        def _(i):
            rows = pl.ds(pl.multiple_of((2 * slot + i) * RB, RB), RB)
            at = pl.ds(pl.multiple_of((first + i) * RB, RB), RB)
            g = mm_nt(proj_s[slot, at, 0:d], w0_s[...])
            g += mm_nt(proj_s[slot, at, d : 2 * d], w1_s[...])
            g += mm_nt(proj_s[slot, at, 2 * d : 3 * d], w2_s[...])
            u, r = unit_rows(cot_s[rows, :].astype(F32))
            n1t = (u * g1_ref[...]).T.astype(BF)
            for q in range(4):
                for p in range(4):
                    to, fr = (4 * p + q) * step48, (4 * q + p) * step48
                    n2t_s[to : to + step48, rows] = n1t[fr : fr + step48]
            small_s[0:1, :] += jnp.sum(g * u, axis=0, keepdims=True)
            gmix_s[rows, :] = (
                gmix_s[rows, :].astype(F32) + unit_back(g, u, r, g1_ref[...])
            ).astype(BF)

        @pl.when(slot == 0)
        def _():
            home_start(gmix_s, gtok6_h, 0, GT0, 2)

        @pl.when(slot == 1)
        def _():
            home_start(gmix_s, gtok6_h, 1, GT1, 3)

    def cond_half(which, dst):
        cols = cols_at(which, h)

        @pl.loop(0, d // RB)
        def _(i):
            dst[rows_at(i, RB), :] = u_s[rows_at(i, RB), cols].astype(BF)

    cond_half(1 - core, sbu_s)
    second(1, sbu_s).start()
    cond_half(core, raw2_s.at[1])

    def win_product(s, which, add):
        rows = rows_at(owner(s), quarter)
        for c in range(3):
            cols = cols_at(3 * which + c, h)
            dw = mm(n2t_s[rows, 0:RB], proj_s[0, 0:RB, cols])
            dw += mm(n2t_s[rows, RB : 2 * RB], proj_s[0, RB : 2 * RB, cols])
            dw += mm(n2t_s[rows, 2 * RB : 3 * RB], proj_s[1, half_at, cols])
            add(slice(c * h, (c + 1) * h), dw)

    win_core = lambda s: remote(sbw_s.at[s % 2], cw_s.at[s], at_core, CW + s)
    for s in range(4):
        if s > 1:
            win_core(s - 2).wait_send()

        def put(cols, dw, s=s):
            sbw_s[s % 2, :, cols] = dw.astype(BF)

        win_product(s, 1 - core, put)
        win_core(s).start()

    def second_rows(q, k):
        return rows_at(4 * q + k, step48)

    for c in range(2):
        remote(c2_s.at[c], c2_s.at[c], at_core, C2 + c).wait_recv()

        @pl.loop(0, 4)
        def _(q, c=c):
            add_into(c2_s.at[c, rows_at(q, quarter)], raw2_s.at[c, rows_at(q, quarter)])

    d2_copies = [
        remote(
            c2_s.at[c, second_rows(q, diag)],
            r2_s.at[0, c, pl.ds(q * step48, step48)],
            at_y if q % 2 else at_x,
            D2 + 4 * c + q,
        )
        for c in range(2)
        for q in range(4)
    ]
    each(d2_copies, "start")

    def own_put(s):
        def put(cols, dw):
            cw_s[s, :, cols] = (cw_s[s, :, cols].astype(F32) + dw).astype(BF)

        return put

    def wait_core(s):
        remote(cw_s.at[s], cw_s.at[s], at_core, CW + s).wait_recv()

    q48 = lambda q: pl.ds(q * step48, step48)
    win_diag = [
        remote(cw_s.at[0, q48(q)], rw_s.at[0, q48(q)], at_y if q % 2 else at_x, DW + q)
        for q in range(4)
    ]
    wait_core(0)
    win_product(0, core, own_put(0))
    each(win_diag, "start")
    wait_core(1)
    win_product(1, core, own_put(1))
    wait_core(2)
    win_product(2, core, own_put(2))

    each(d2_copies, "wait")
    for c in range(2):
        for q in range(4):
            to = by_x if q % 2 else by_y
            add_into(c2_s.at[c, second_rows(q, to)], r2_s.at[0, c, q48(q)])

    def pack_second(k, dst):
        for c in range(2):
            for q in range(4):
                dst[c, q48(q), :] = c2_s[c, second_rows(q, k), :]

    pack_second(by_x, raw2_s.at[:, pl.ds(0, quarter)])
    pack_second(by_y, raw2_s.at[:, pl.ds(quarter, quarter)])
    x2_copy = remote(raw2_s.at[:, pl.ds(0, quarter)], r2_s.at[1], at_x, XS2)
    y2_copy = remote(raw2_s.at[:, pl.ds(quarter, quarter)], r2_s.at[2], at_y, YS2)
    x2_copy.start()
    y2_copy.start()

    win_x = remote(cw_s.at[1], rw_s.at[1], at_x, XW)
    win_y = remote(cw_s.at[2], rw_s.at[2], at_y, YW)
    each(win_diag, "wait")
    for q in range(4):
        add_into(cw_s.at[1 if q % 2 else 2, q48(q)], rw_s.at[0, q48(q)])
    win_x.start()
    win_y.start()
    small_c = remote(small_s, sgot_s.at[0], at_core, SMALL)
    small_c.start()
    wait_core(3)
    win_product(3, core, own_put(3))

    each([c for copies, _ in gathers for c in copies], "wait")
    each([local for _, local in gathers], "wait")
    each(core_gathers, "start")

    x2_copy.wait()
    y2_copy.wait()
    fin2 = raw2_s.at[:, pl.ds(2 * quarter, quarter)]
    pack_second(xy, fin2)
    for c in range(2):
        add_into(fin2.at[c], r2_s.at[1, c])
        add_into(fin2.at[c], r2_s.at[2, c])
    z2_copies = [
        remote(
            raw2_s.at[:, rows_at(peers[k], step48, 2 * quarter)],
            z2_s.at[k - 1],
            at_z[k],
            Z2 + k - 1,
        )
        for k in range(1, 4)
    ]
    each(z2_copies, "start")
    small_c.wait()
    ssum_s[0] = small_s[...] + sgot_s[0]
    small_x = remote(ssum_s.at[0], sgot_s.at[1], at_x, SMALL + 1)
    small_x.start()

    win_x.wait()
    win_y.wait()
    for q in range(4):
        add_into(cw_s.at[3, q48(q)], rw_s.at[1, q48(q)])
        add_into(cw_s.at[3, q48(q)], rw_s.at[2, q48(q)])
    zw_copies = [
        remote(cw_s.at[3, rows_at(peers[k], step48)], zw_s.at[k - 1], at_z[k], ZW + k - 1)
        for k in range(1, 4)
    ]
    each(zw_copies, "start")
    small_x.wait()
    ssum_s[1] = ssum_s[0] + sgot_s[1]
    small_y = remote(ssum_s.at[1], sgot_s.at[2], at_y, SMALL + 2)
    small_y.start()

    def rank_total(ref, got):
        total = ref[...].astype(F32)
        for k in range(3):
            total += got(k).astype(F32)
        ref[...] = total.astype(BF)

    each(z2_copies, "wait")
    mine2 = rows_at(me, step48, 2 * quarter)
    views2 = (view_wo, view_wc)
    gathers2 = []
    for c in range(2):
        rank_total(raw2_s.at[c, mine2], lambda k, c=c: z2_s[k, c])
        gathers2.append(gather(raw2_s.at[c, mine2], views2[c], GA2 + 3 * c, 7 + c))
    for copies, local in gathers2:
        each(copies, "start")
        local.start()
    small_y.wait()
    ssum_s[2] = ssum_s[1] + sgot_s[2]
    small_z = [
        remote(ssum_s.at[2], sgot_s.at[2 + k], at_z[k], SMALL + 2 + k) for k in range(1, 4)
    ]
    each(small_z, "start")
    for copies, local in gathers2:
        each(copies, "wait")
        local.wait()
    core_gathers2 = gather_core(view_wo, GC2) + gather_core(view_wc, GC2 + 4)
    each(core_gathers2, "start")

    each(zw_copies, "wait")
    minew = rows_at(me, step48)
    rank_total(cw_s.at[3, minew], lambda k: zw_s[k])
    copies, local = gather(cw_s.at[3, minew], view_wi, GW, 9)
    each(copies, "start")
    local.start()
    each(small_z, "wait")
    small_out[...] = ssum_s[2] + sgot_s[3] + sgot_s[4] + sgot_s[5]
    each(copies, "wait")
    local.wait()
    core_gathers3 = gather_core(view_wi, GCW)
    each(core_gathers3, "start")

    each(diag_copies(False) + diag_copies(True) + x_copies() + y_copies(), "wait_send")
    second(0, sbg_s).wait_send()
    second(1, sbu_s).wait_send()
    win_core(2).wait_send()
    win_core(3).wait_send()
    each(core_gathers + core_gathers2, "wait")
    home_wait(n2_s, lay6_h, 0, LAY, 0)
    home_wait(n2_s, lay6_h, 1, LAY + 3, 1)
    home_wait(gmix_s, gtok6_h, 0, GT0, 2)
    home_wait(gmix_s, gtok6_h, 1, GT1, 3)
    each(core_gathers3, "wait")


def back(
    side, slots, isp, isl, mixed, xs, cot, w_out, g2, w_gate, w_up, w_down,
    proj, filt, ss, cs, th, feat, st, ct, w_cond, table, table_t, mult, g1, w_in,
):
    n, d = cot.shape
    t = xs.shape[1]
    f2 = table.shape[0]
    f = f2 // 2
    h, q4, dr, s48 = d // 2, d // 4, d // 8, d // 16
    hbm = pl.BlockSpec(memory_space=pl.ANY)
    vm = pl.BlockSpec(memory_space=pltpu.VMEM)
    smem = pl.BlockSpec(memory_space=pltpu.SMEM)
    b = lambda *s: pltpu.VMEM(s, BF)
    g = lambda *s: pltpu.VMEM(s, F32)
    return pl.pallas_call(
        functools.partial(back_kernel, side),
        name="back",
        out_shape=tuple(
            jax.ShapeDtypeStruct(s, BF)
            for s in (
                (slots, t // 4, d), (slots, t // 4, d), (q4, 4 * d), (q4, 4 * d), (d, d),
                (q4, d), (q4, d), (q4, 3 * d),
            )
        )
        + (jax.ShapeDtypeStruct((16, d), F32),),
        in_specs=[smem, smem] + [hbm] * 4 + [vm] + [hbm] * 9 + [vm, vm, hbm, hbm, hbm]
        + [vm, vm, hbm],
        out_specs=(hbm,) * 8 + (vm,),
        scratch_shapes=[
            g(n, d), g(n, d), g(n, d), g(n, 128),
            b(n, d), b(d, n), b(n, d), b(n + t, d), b(n, d),
            b(n, d), b(n, d), b(n, d), b(d, d), b(d, d), b(d, d), b(d, d), b(d, d),
            b(f2, t), b(t, f2), g(t, 128), g(t, 128),
            b(d, h), b(d, h), b(h, d),
            b(4, d, h), b(4, d, h), b(4, h, d),
            b(d, h), b(d, h), b(d, h), b(d, h), b(d, h), b(d, h),
            b(3, q4, h), b(3, q4, h), b(4, 2, dr, d), b(4, dr, d), b(3, dr, d),
            b(2, t, 3 * d), b(t, d), b(f2, d), b(f2, d), g(f, d), b(f, d), b(f, d), b(f, d),
            b(2, d, h), b(2, d, h), b(3, 2, q4, h), b(3, 2, s48, h),
            b(4, q4, 3 * h), b(2, q4, 3 * h), b(3, q4, 3 * h), b(3, s48, 3 * h),
            g(16, d), g(6, 16, d), g(3, 16, d),
            pltpu.SemaphoreType.DMA((17,)),
            pltpu.SemaphoreType.DMA((6,)),
            pltpu.SemaphoreType.DMA((142,)),
            pltpu.SemaphoreType.DMA((142,)),
            pltpu.SemaphoreType.DMA((10,)),
        ],
        compiler_params=pltpu.CompilerParams(
            collective_id=1, has_side_effects=True, vmem_limit_bytes=65400 * 1024
        ),
    )(
        isp, isl, mixed, xs, cot, w_out, g2, w_gate, w_up, w_down, proj, filt, ss, cs, th, feat,
        st, ct, w_cond, table, table_t, mult, g1, w_in,
    )


def on_device(
    tokens, kind, ln1_gain, w_in, short_taps, cond_taps, w_cond, cond_bias, w_out, ln2_gain,
    w_gate, w_up, w_down, cotangent,
):
    _, rows, slots, d = tokens.shape
    n = lax.axis_size("seq")
    dp_count = lax.axis_size("dp")
    rank = lax.axis_index("seq")
    span_long = rows * n
    is_long = kind[0] == 1

    freqs = -(-max(span_long // 2 + 1, n * (rows // 2 + 1)) // 16) * 16
    table, table_t, mult = wave_tables(is_long, rows, span_long, freqs)
    isp = jnp.where(is_long, 1.0 / span_long, 1.0 / rows).astype(F32).reshape(1)
    place = jnp.arange(span_long, dtype=jnp.int32)
    offset = jnp.where(is_long, place, place % rows)[:, None]
    m1 = jnp.broadcast_to((offset >= 1).astype(F32), (span_long, 128))
    m2 = jnp.broadcast_to((offset >= 2).astype(F32), (span_long, 128))

    tok6 = jnp.transpose(tokens[0], (1, 0, 2))
    cot6 = jnp.transpose(cotangent[0], (1, 0, 2))
    xs, cot = reshard_in(tok6, cot6)

    g1, g2 = ln1_gain.reshape(1, d), ln2_gain.reshape(1, d)
    proj, mixed, filt, sig_spec, cond_spec, th, feat = mix_forward(
        isp, xs, g1, w_in, short_taps, cond_taps, w_cond, cond_bias.reshape(1, d),
        table, table_t, m1, m2, mult,
    )
    side = math.isqrt(dp_count // 2)
    lay6, gtok6, *sums, small = back(
        side, slots, isp, is_long.astype(jnp.int32).reshape(1), mixed, xs, cot, w_out, g2,
        w_gate, w_up, w_down, proj, filt, sig_spec, cond_spec, th, feat, short_taps, cond_taps,
        w_cond, table, table_t, mult, g1, w_in,
    )
    layer_out = jnp.transpose(lay6, (1, 0, 2))[None]
    grad_tokens = jnp.transpose(gtok6, (1, 0, 2))[None]

    sums = [a.astype(F32) for a in sums]
    if dp_count > 8:
        groups = [
            [
                (y * side + x) * 2 + core
                for y in range(y0, side, 2)
                for x in range(x0, side, 2)
            ]
            for y0 in range(2)
            for x0 in range(2)
            for core in range(2)
        ]
        sums = [lax.psum(a, "dp", axis_index_groups=groups) for a in sums]
        small = lax.psum(small, "dp", axis_index_groups=groups)
    grad_gate, grad_up, grad_down, grad_w_out, grad_w_cond, grad_w_in = sums
    part = lambda a, width: lax.dynamic_slice_in_dim(a, rank * width, width, a.ndim - 1)
    return (
        layer_out,
        grad_tokens,
        part(small[0], d // n),
        grad_w_in,
        part(small[1:10].reshape(3, 3 * d), 3 * d // n),
        part(small[10:13], d // n),
        grad_w_cond,
        part(small[13], d // n),
        grad_w_out,
        part(small[14], d // n),
        grad_gate,
        grad_up,
        grad_down,
    )


def solution(mesh):
    rows = P("dp", "seq", None, None)
    return jax.shard_map(
        on_device,
        mesh=mesh,
        in_specs=(rows, P("dp")) + (P(),) * 11 + (rows,),
        out_specs=(
            rows,
            rows,
            P("seq"),
            P("seq", None),
            P(None, "seq"),
            P(None, "seq"),
            P("seq", None),
            P("seq"),
            P("seq", None),
            P("seq"),
            P("seq", None),
            P("seq", None),
            P("seq", None),
        ),
        check_vma=False,
    )
```

time: 363 us -> 317 us (0.87); the launches traced: 356 us -> 317 us
  Pallas kernels: 316 us -> 291 us
  local copies, waits for them, and re-layouts: 27.5 us -> 10.6 us
  other arithmetic: 10.3 us -> 14.8 us
    pallas_call x1, Pallas kernels: 233 us -> 207 us  [back(): pl.pallas_call(functools.partial(back_kernel, side), name='back', out_sha...]
    reshape x5 -> x0, local copies, waits for them, and re-layouts: 12 us -> none  [the longest x4 9.74 us: on_device(): by_chunk = lambda a: jnp.transpose(a.reshape((2, 4) + a.shape[1:]), (2, 1...]
    convert_element_type x0 -> x6, other arithmetic: none -> 9.3 us  [on_device(): sums = [a.astype(F32) for a in sums]]
    reshape x4 -> x0, other arithmetic: 4.82 us -> none  [the longest x1 1.65 us: on_device(): dd.reshape(-1, d)]
where the time goes in v2:
time: 317 us
  Pallas kernels  291 us (92%)
  other arithmetic  14.8 us (5%)
  local copies, waits for them, and re-layouts  10.6 us (3%)
    pallas_call x1, Pallas kernels, back(): pl.pallas_call(functools.partial(back_kernel, side), name='back', out_sha...  207 us
    pallas_call x1, Pallas kernels, reshard_in(): pl.pallas_call(reshard_in_kernel, name='reshard_in', out_shape=(jax.Shape...  58 us
    pallas_call x1, Pallas kernels, mix_forward(): pl.pallas_call(fwd_kernel, name='mix_forward', grid=(2,), out_shape=(jax....  25.5 us
    convert_element_type x6, other arithmetic, on_device(): sums = [a.astype(F32) for a in sums]  9.3 us

profile of v2, /device:TPU:25, one launch (start us, length us, event | category | flops | bytes accessed | tf_op | source)
XLA Modules:
  0.0 317.3 jit_solution(16090253481107405228)
XLA Ops:
  1.3 4.2 %select_convert_fusion.1 = (bf16[272,512]{0,1:T(8,128)(2,1)S(1)}, bf16[272,512]{0,1:T(8,128)(2,1)S(1)}) fusion(s32[272]{0:T(512)S(1)} %get-tuple-element.59, s32[512]{0:T(512)S(1)} %get-tuple-element.57, pred[272]{0:T(512)(128)(4,1)S(1)} %get-tuple-element.61, pred[272]{0:T(512)(128)(4,1)S(1)} %get-tuple-element.60, pred[]{:T(512)} %bitcast, ...), kind=kLoop, calls=%fused_computation.15 | loop fusion | flops 4874240 | bytes 563873 | tf_op jit(solution)/shard_map/convert.1
  5.5 0.2 pad_maximum_fusion
  5.8 1.0 copy.27.w_ref.refs_19_
  6.8 1.1 fusion.26.wt_ref.refs_20_
  7.9 0.8 broadcast_in_dim.45.m1_ref
  8.7 0.8 broadcast_in_dim.46.m2_ref
  9.6 0.8 broadcast_in_dim.50.mult_ref.refs_21_
  10.3 58.0 %reshard_in.1 = (bf16[2,512,768]{2,1,0:T(8,128)(2,1)}, bf16[768,768]{1,0:T(8,128)(2,1)}) custom-call(bf16[6,128,768]{2,1,0:T(8,128)(2,1)} %bitcast.19, bf16[6,128,768]{2,1,0:T(8,128)(2,1)} %bitcast.20), custom_call_target="tpu_custom_call" | custom-call | tf_op jit(solution)/shard_map/reshard_in/pallas_call | solution.py:163
  68.3 0.0 copy-done.8
  68.3 0.6 reshape.193.g1_ref.refs_22_
  68.9 0.0 copy-done.9
  68.9 0.6 reshape.194.cb_ref
  69.5 25.5 %mix_forward.1 = (bf16[2,512,2304]{2,1,0:T(8,128)(2,1)}, bf16[2,512,768]{2,1,0:T(8,128)(2,1)}, bf16[2,512,768]{2,1,0:T(8,128)(2,1)}, bf16[2,544,768]{2,1,0:T(8,1...) custom-call(f32[1]{0:T(128)} %bitcast.1.isp_ref.refs_0_, ...), custom_call_target="tpu_custom_call" | custom-call | tf_op jit(solution)/shard_map/mix_forward/pallas_call | solution.py:245
  95.0 0.0 copy-done.10
  95.0 0.6 reshape.195.refs_6_
  95.5 207.1 %back.1 = (bf16[6,128,768]{2,1,0:T(8,128)(2,1)}, bf16[6,128,768]{2,1,0:T(8,128)(2,1)}, bf16[192,3072]{1,0:T(8,128)(2,1)}, bf16[192,3072]{1,0:T(8,128)(2,1)}, bf1...) custom-call(f32[1]{0:T(128)} %bitcast.1.isp_ref.refs_0_, ...), custom_call_target="tpu_custom_call" | custom-call | tf_op jit(solution)/shard_map/back/pallas_call | solution.py:1020
  302.6 0.0 copy-start.1
  302.6 3.0 convert_element_type.46
  305.7 1.7 convert_element_type.47
  307.3 1.6 convert_element_type.48
  308.9 1.3 convert_element_type.43
  310.2 0.9 convert_element_type.44
  311.1 0.0 copy-done.5
  311.1 0.9 convert_element_type.45
  312.0 0.7 constant_dynamic-slice_fusion.3
  312.7 0.7 constant_dynamic-slice_fusion.2
  313.4 0.6 constant_dynamic-slice_fusion.4
  314.0 0.6 constant_dynamic-slice_fusion.1
  314.6 0.6 constant_dynamic-slice_fusion
  315.3 0.0 copy-done.3
  315.3 1.0 copy.32
  316.3 1.0 copy.33
  (25 shorter events, 0.1 us)
Async XLA Ops:
  9.5 58.7 %copy-start.8 = (f32[768]{0:T(1024)S(1)}, f32[768]{0:T(1024)}, u32[]{:S(2)}) copy-start(f32[768]{0:T(1024)} %param.16) | copy-start | bytes 9220
  9.5 59.3 %copy-start.9 = (f32[768]{0:T(1024)S(1)}, f32[768]{0:T(1024)}, u32[]{:S(2)}) copy-start(f32[768]{0:T(1024)} %param.21) | copy-start | bytes 9220
  69.5 25.5 %copy-start.10 = (f32[768]{0:T(1024)S(1)}, f32[768]{0:T(1024)}, u32[]{:S(2)}) copy-start(f32[768]{0:T(1024)} %param.23) | copy-start | bytes 9220
  302.6 3.0 copy-start.1
  305.7 1.7 copy-start
  307.3 1.6 copy-start.4
  308.9 1.3 copy-start.6
  308.9 2.2 copy-start.5
  310.2 1.7 copy-start.7
  310.2 5.0 %copy-start.3 = (bf16[6,128,768]{2,1,0:T(8,128)(2,1)S(1)}, bf16[6,128,768]{2,1,0:T(8,128)(2,1)}, u32[]{:S(2)}) copy-start(bf16[6,128,768]{2,1,0:T(8,128)(2,1)} %get-tuple-element.40) | copy-start | bytes 3538948
  312.0 4.3 %copy-start.2 = (bf16[6,128,768]{2,1,0:T(8,128)(2,1)S(1)}, bf16[6,128,768]{2,1,0:T(8,128)(2,1)}, u32[]{:S(2)}) copy-start(bf16[6,128,768]{2,1,0:T(8,128)(2,1)} %get-tuple-element.41) | copy-start | bytes 3538948

commit v3 on v2

--- a/solution.py
+++ b/solution.py
@@ -80,208 +80,257 @@
     return pl.ds(pl.multiple_of(base + c * width, 128), width)
 
 
-def wave_tables(is_long, short, span_long, freqs):
-    i = jnp.arange(freqs, dtype=jnp.int32)[:, None]
-    t = jnp.arange(span_long, dtype=jnp.int32)[None, :]
-    blocks, half = span_long // short, short // 2 + 1
-    f_short, b_short = i % half, i // half
-    phase = jnp.where(
-        is_long, (i * t) % span_long, ((f_short * (t % short)) % short) * blocks
-    )
-    kept = jnp.where(is_long, i <= span_long // 2, (b_short < blocks) & (t // short == b_short))
-    angle = phase.astype(F32) * (2.0 * math.pi / span_long)
-    kept_f = kept.astype(F32)
-    table = jnp.concatenate([jnp.cos(angle) * kept_f, jnp.sin(angle) * kept_f], axis=0)
-    once = jnp.where(
-        is_long, (i == 0) | (i == span_long // 2), (f_short == 0) | (f_short == short // 2)
-    )
-    used = jnp.where(is_long, i <= span_long // 2, b_short < blocks)
-    mult = jnp.where(used, jnp.where(once, 1.0, 2.0), 0.0).astype(F32)
-    table = table.astype(BF)
-    return table, table.T, jnp.broadcast_to(mult, (freqs, 128))
-
-
-def reshard_in_kernel(tok_ref, cot_ref, xs_ref, cs_ref, local_sem, send_sem, recv_sem):
+def short_rows(i, t):
+    half = t // 8 + 1
+    block = jnp.zeros_like(i)
+    for k in range(1, 5):
+        block += (i >= k * half).astype(jnp.int32)
+    return block, i - half * block
+
+
+def wave_table(ref, axis, isl, t):
+    freqs = ref.shape[axis] // 2
+    j = lax.broadcasted_iota(jnp.int32, ref.shape, axis)
+    pos = lax.broadcasted_iota(jnp.int32, ref.shape, 1 - axis)
+    sin = (j >= freqs).astype(jnp.int32)
+    i = j - freqs * sin
+    block, f = short_rows(i, t)
+    short = t // 4
+    phase = isl * (i * pos) + (1 - isl) * (4 * f * (pos & (short - 1)))
+    kept_long = (i <= t // 2).astype(jnp.int32)
+    kept_short = ((pos >= block * short) & (pos < (block + 1) * short)).astype(jnp.int32)
+    kept = isl * kept_long + (1 - isl) * kept_short
+    phase = (phase - (t // 4) * sin) & (t - 1)
+    angle = (phase - t // 2).astype(F32) * (2.0 * math.pi / t)
+    z = angle * angle
+    value = jnp.full_like(z, -1.0 / math.factorial(14))
+    for k in range(6, -1, -1):
+        value = value * z + (-1.0) ** k / math.factorial(2 * k)
+    ref[...] = (-value * kept.astype(F32)).astype(ref.dtype)
+
+
+def multiplicity(shape, isl, t):
+    i = lax.broadcasted_iota(jnp.int32, shape, 0)
+    block, f = short_rows(i, t)
+    once_long = ((i == 0) | (i == t // 2)).astype(jnp.int32)
+    once_short = ((f == 0) | (f == t // 8)).astype(jnp.int32)
+    long = (2 - once_long) * (i <= t // 2).astype(jnp.int32)
+    short = (2 - once_short) * (block < 4).astype(jnp.int32)
+    return (isl * long + (1 - isl) * short).astype(F32)
+
+
+def causal_masks(m1_ref, m2_ref, isl):
+    t = m1_ref.shape[0]
+    place = lax.broadcasted_iota(jnp.int32, m1_ref.shape, 0)
+    short = place & (t // 4 - 1)
+    place = short + isl * (place - short)
+    m1_ref[...] = (place >= 1).astype(F32)
+    m2_ref[...] = (place >= 2).astype(F32)
+
+
+def inverse_span(isl, t):
+    long = isl.astype(F32)
+    return long * (1.0 / t) + (1.0 - long) * (4.0 / t)
+
+
+def front_kernel(
+    kind_ref, tok_h, cot_h, g1_ref, win_h, st_ref, ct_ref, wc_h, cb_ref,
+    xs_h, cs_h, proj_h, mixed_h, filt_h, ss_h, sc_h, th_h, feat_h, tab_h, tabt_h,
+    x_s, win_s, wc_s, tab_s, tabt_s, m1_ref, m2_ref, ms_s, n1_s, q_s,
+    proj_s, mixed_s, filt_s, ss_s, sc_s, th_s, feat_s,
+    load_sem, out_sem, send_sem, recv_sem,
+):
+    t, d = n1_s.shape
+    f = ms_s.shape[0]
+    n = 4
+    blk = t // n
     dp, me = lax.axis_index("dp"), lax.axis_index("seq")
-    n = lax.axis_size("seq")
-    rows = tok_ref.shape[1]
+    peers = [lax.rem(me + k, n) for k in range(n)]
+    sources = [lax.rem(me + n - k, n) for k in range(n)]
+    half = lax.rem(me, 2)
+    pair = me + 1 - 2 * half
+    isl = kind_ref[0]
+    isp = inverse_span(isl, t)
+
+    block = lambda i: pl.ds(pl.multiple_of(i * blk, blk), blk)
+    half_block = pl.ds(pl.multiple_of(t + half * blk, blk), blk)
+    loads = [
+        pltpu.make_async_copy(win_h, win_s, load_sem.at[0]),
+        pltpu.make_async_copy(wc_h, wc_s, load_sem.at[1]),
+        pltpu.make_async_copy(tok_h.at[me], x_s.at[0, block(me)], load_sem.at[2]),
+        pltpu.make_async_copy(tok_h.at[n + me // 2], x_s.at[1, block(me)], load_sem.at[3]),
+        pltpu.make_async_copy(cot_h.at[me], cs_h.at[block(me)], load_sem.at[4]),
+    ]
+    half_load = pltpu.make_async_copy(cot_h.at[n + me // 2], cs_h.at[half_block], load_sem.at[5])
+
     barrier = pltpu.get_barrier_semaphore()
     for k in range(1, n):
-        pl.semaphore_signal(
-            barrier, inc=1, device_id=(dp, lax.rem(me + k, n)), device_id_type=MESH
+        pl.semaphore_signal(barrier, inc=1, device_id=(dp, peers[k]), device_id_type=MESH)
+    pl.semaphore_wait(barrier, n - 1)
+
+    def remote(src, dst, peer, j):
+        return pltpu.make_async_remote_copy(
+            src_ref=src,
+            dst_ref=dst,
+            send_sem=send_sem.at[j],
+            recv_sem=recv_sem.at[j],
+            device_id=(dp, peer),
+            device_id_type=MESH,
         )
-    pl.semaphore_wait(barrier, n - 1)
-    at = pl.ds(pl.multiple_of(me * rows, rows), rows)
-    half_at = pl.ds(pl.multiple_of(n * rows + lax.rem(me, 2) * rows, rows), rows)
-
-    def copies(k, peer):
-        moves = [
-            (tok_ref.at[peer], xs_ref.at[0, at]),
-            (tok_ref.at[n + peer // 2], xs_ref.at[1, at]),
-            (cot_ref.at[peer], cs_ref.at[at]),
-            (cot_ref.at[n + peer // 2], cs_ref.at[half_at]),
+
+    whole_slot = [
+        remote(tok_h.at[peers[k]], x_s.at[0, block(me)], peers[k], k - 1) for k in range(1, n)
+    ]
+    to_pair = remote(tok_h.at[n + me // 2], x_s.at[1, block(me)], pair, 3)
+    across = remote(tok_h.at[n + peers[2] // 2], x_s.at[1, block(me)], peers[2], 4)
+    handed = remote(x_s.at[1, block(peers[2])], x_s.at[1, block(peers[2])], pair, 5)
+    cots = [remote(cot_h.at[peers[k]], cs_h.at[block(me)], peers[k], 5 + k) for k in range(1, n)]
+    halves = [
+        remote(cot_h.at[n + peers[k] // 2], cs_h.at[half_block], peers[k], 8 + k)
+        for k in range(1, n)
+    ]
+    sends_half = [lax.rem(p, 2) == me // 2 for p in peers]
+    gets_half = [half == s // 2 for s in sources]
+    for c in whole_slot + [across, to_pair] + cots:
+        c.start()
+    for k in range(1, n):
+        pl.when(sends_half[k])(halves[k - 1].start)
+    for c in loads:
+        c.start()
+    pl.when(sends_half[0])(half_load.start)
+
+    wave_table(tab_s, 0, isl, t)
+    wave_table(tabt_s, 1, isl, t)
+    causal_masks(m1_ref, m2_ref, isl)
+    ms_s[...] = multiplicity(ms_s.shape, isl, t) * isp
+
+    for c in loads[:4]:
+        c.wait()
+    for c in whole_slot:
+        c.wait()
+
+    outs = [
+        (x_s, xs_h), (proj_s, proj_h), (ss_s, ss_h), (sc_s, sc_h), (feat_s, feat_h),
+        (mixed_s, mixed_h), (filt_s, filt_h), (th_s, th_h),
+    ]
+
+    def out_copy(slot, j):
+        return pltpu.make_async_copy(outs[j][0].at[slot], outs[j][1].at[slot], out_sem.at[slot, j])
+
+    tables = [
+        pltpu.make_async_copy(tab_s, tab_h, load_sem.at[6]),
+        pltpu.make_async_copy(tabt_s, tabt_h, load_sem.at[7]),
+    ]
+    for c in tables:
+        c.start()
+
+    @pl.loop(0, 2)
+    def _(slot):
+        @pl.when(slot == 1)
+        def _():
+            to_pair.wait()
+            handed.wait()
+
+        @pl.loop(0, t // 128)
+        def _(r):
+            rows = pl.ds(pl.multiple_of(r * 128, 128), 128)
+            u, _ = unit_rows(x_s[slot, rows, :].astype(F32))
+            n1_s[rows, :] = (u * g1_ref[...]).astype(BF)
+
+        @pl.loop(0, d // CB)
+        def _(c):
+            m1, m2 = lanes(m1_ref, CB), lanes(m2_ref, CB)
+            own = cols_at(c, CB)
+
+            def part(k):
+                cols = cols_at(c, CB, k * d)
+                p = mm(n1_s[...], win_s[:, cols]).astype(BF)
+                proj_s[slot, :, cols] = p
+                return conv(p.astype(F32), st_ref[:, cols], m1, m2)
+
+            q_s[:, own] = part(0)
+            key = part(1)
+            value = part(2).astype(BF)
+            value_f = value.astype(F32)
+            signal = (key * value_f).astype(BF)
+            ss_s[slot, :, own] = mm(tab_s[...], signal).astype(BF)
+            cond = conv(value_f, ct_ref[:, own], m1, m2).astype(BF)
+            xc = mm(tab_s[...], cond)
+            sc_s[slot, :, own] = xc.astype(BF)
+            power = (xc[:f] * xc[:f] + xc[f:] * xc[f:]) * isp
+            feat_s[slot, :, own] = jnp.log1p(power).astype(BF)
+
+        for j in range(5):
+            out_copy(slot, j).start()
+
+        @pl.when(slot == 0)
+        def _():
+            across.wait()
+            handed.start()
+
+        @pl.loop(0, d // CB)
+        def _(c):
+            own = cols_at(c, CB)
+            th = jnp.tanh(mm(feat_s[slot], wc_s[:, own]) + cb_ref[:, own])
+            th_s[slot, :, own] = th
+            g = (1.0 + th) * lanes(ms_s, CB)
+            xs = ss_s[slot, :, own].astype(F32)
+            y = jnp.concatenate([(g * xs[:f]).astype(BF), (g * xs[f:]).astype(BF)], axis=0)
+            filt = mm(tabt_s[...], y)
+            filt_s[slot, :, own] = filt.astype(BF)
+            mixed_s[slot, :, own] = (q_s[:, own] * filt).astype(BF)
+
+        for j in range(5, 8):
+            out_copy(slot, j).start()
+
+    for slot in range(2):
+        for j in range(8):
+            out_copy(slot, j).wait()
+    for c in tables + loads[4:] + cots:
+        c.wait()
+    pl.when(sends_half[0])(half_load.wait)
+    for k in range(1, n):
+        pl.when(sends_half[k])(halves[k - 1].wait_send)
+        pl.when(gets_half[k])(halves[k - 1].wait_recv)
+
+
+def front(kind, tok, cot, g1, w_in, st, ct, w_cond, cb):
+    slots, blk, d = tok.shape
+    t = 4 * blk
+    f = -(-max(t // 2 + 1, 4 * (blk // 2 + 1)) // 16) * 16
+    hbm = pl.BlockSpec(memory_space=pl.ANY)
+    vm = pl.BlockSpec(memory_space=pltpu.VMEM)
+    smem = pl.BlockSpec(memory_space=pltpu.SMEM)
+    per_slot = [
+        ((2, t, d), BF), ((2, t, 3 * d), BF), ((2, t, d), BF), ((2, t, d), BF),
+        ((2, 2 * f, d), BF), ((2, 2 * f, d), BF), ((2, f, d), F32), ((2, f, d), BF),
+    ]
+    xs, *rest = [jax.ShapeDtypeStruct(*s) for s in per_slot]
+    tables = [((2 * f, t), BF), ((t, 2 * f), BF)]
+    return pl.pallas_call(
+        front_kernel,
+        name="front",
+        out_shape=(xs, jax.ShapeDtypeStruct((t + t // 2, d), BF), *rest)
+        + tuple(jax.ShapeDtypeStruct(*s) for s in tables),
+        in_specs=[smem, hbm, hbm, vm, hbm, vm, vm, hbm, vm],
+        out_specs=(hbm,) * 11,
+        scratch_shapes=[
+            pltpu.VMEM((2, t, d), BF), pltpu.VMEM((d, 3 * d), BF), pltpu.VMEM((d, d), BF),
+            pltpu.VMEM(*tables[0]), pltpu.VMEM(*tables[1]),
+            pltpu.VMEM((t, 128), F32), pltpu.VMEM((t, 128), F32), pltpu.VMEM((f, 128), F32),
+            pltpu.VMEM((t, d), BF), pltpu.VMEM((t, d), F32),
         ]
-        if k == 0:
-            return [
-                pltpu.make_async_copy(s, d, local_sem.at[j]) for j, (s, d) in enumerate(moves)
-            ]
-        return [
-            pltpu.make_async_remote_copy(
-                src_ref=s,
-                dst_ref=d,
-                send_sem=send_sem.at[j, k],
-                recv_sem=recv_sem.at[j, k],
-                device_id=(dp, peer),
-                device_id_type=MESH,
-            )
-            for j, (s, d) in enumerate(moves)
-        ]
-
-    peers = [lax.rem(me + k, n) for k in range(n)]
-    sources = [lax.rem(me + n - k, n) for k in range(n)]
-    sends_half = [lax.rem(p, 2) == me // 2 for p in peers]
-    gets_half = [lax.rem(me, 2) == s // 2 for s in sources]
-    all_copies = [copies(k, peers[k]) for k in range(n)]
-    for j in range(3):
-        for k in range(n):
-            all_copies[k][j].start()
-    for k in range(n):
-        pl.when(sends_half[k])(all_copies[k][3].start)
-    for j in range(3):
-        for k in range(n):
-            all_copies[k][j].wait()
-    pl.when(sends_half[0])(all_copies[0][3].wait)
-    for k in range(1, n):
-        pl.when(sends_half[k])(all_copies[k][3].wait_send)
-        pl.when(gets_half[k])(all_copies[k][3].wait_recv)
-
-
-def reshard_in(tok, cot):
-    slots, rows, d = tok.shape
-    n = lax.axis_size("seq")
-    any_spec = pl.BlockSpec(memory_space=pl.ANY)
-    return pl.pallas_call(
-        reshard_in_kernel,
-        name="reshard_in",
-        out_shape=(
-            jax.ShapeDtypeStruct((2, n * rows, d), BF),
-            jax.ShapeDtypeStruct((n * rows + n * rows // 2, d), BF),
+        + [pltpu.VMEM(*s) for s in per_slot[1:]]
+        + [
+            pltpu.SemaphoreType.DMA((8,)),
+            pltpu.SemaphoreType.DMA((2, 8)),
+            pltpu.SemaphoreType.DMA((12,)),
+            pltpu.SemaphoreType.DMA((12,)),
+        ],
+        compiler_params=pltpu.CompilerParams(
+            collective_id=0, has_side_effects=True, vmem_limit_bytes=VMEM_LIMIT
         ),
-        in_specs=[any_spec] * 2,
-        out_specs=(any_spec, any_spec),
-        scratch_shapes=[
-            pltpu.SemaphoreType.DMA((4,)),
-            pltpu.SemaphoreType.DMA((4, n)),
-            pltpu.SemaphoreType.DMA((4, n)),
-        ],
-        compiler_params=pltpu.CompilerParams(collective_id=0, has_side_effects=True),
-    )(tok, cot)
-
-
-def fwd_kernel(
-    isp_ref, x_ref, g1_ref, win_ref, st_ref, ct_ref, wc_ref, cb_ref, w_ref, wt_ref,
-    m1_ref, m2_ref, mult_ref,
-    proj_ref, mixed_ref, filt_ref, xs_ref, xc_ref, th_ref, feat_ref,
-    n1_s, q_s,
-):
-    t, d = n1_s.shape
-    f = th_ref.shape[1]
-    isp = isp_ref[0]
-
-    @pl.loop(0, t // 128)
-    def _(r):
-        rows = pl.ds(pl.multiple_of(r * 128, 128), 128)
-        u, _ = unit_rows(x_ref[0, rows, :].astype(F32))
-        n1_s[rows, :] = (u * g1_ref[...]).astype(BF)
-
-    @pl.loop(0, d // CB)
-    def _(c):
-        m1, m2 = lanes(m1_ref, CB), lanes(m2_ref, CB)
-        own = cols_at(c, CB)
-
-        def part(k):
-            cols = cols_at(c, CB, k * d)
-            p = mm(n1_s[...], win_ref[:, cols]).astype(BF)
-            proj_ref[0, :, cols] = p
-            return conv(p.astype(F32), st_ref[:, cols], m1, m2)
-
-        q_s[:, own] = part(0)
-        key = part(1)
-        value = part(2).astype(BF)
-        value_f = value.astype(F32)
-        signal = (key * value_f).astype(BF)
-        xs_ref[0, :, own] = mm(w_ref[...], signal).astype(BF)
-        cond = conv(value_f, ct_ref[:, own], m1, m2).astype(BF)
-        xc = mm(w_ref[...], cond)
-        xc_ref[0, :, own] = xc.astype(BF)
-        power = (xc[:f] * xc[:f] + xc[f:] * xc[f:]) * isp
-        feat_ref[0, :, own] = jnp.log1p(power).astype(BF)
-
-    @pl.loop(0, d // CB)
-    def _(c):
-        own = cols_at(c, CB)
-        th = jnp.tanh(mm(feat_ref[0], wc_ref[:, own]) + cb_ref[:, own])
-        th_ref[0, :, own] = th
-        g = (1.0 + th) * (lanes(mult_ref, CB) * isp)
-        xs = xs_ref[0, :, own].astype(F32)
-        y = jnp.concatenate([(g * xs[:f]).astype(BF), (g * xs[f:]).astype(BF)], axis=0)
-        filt = mm(wt_ref[...], y)
-        filt_ref[0, :, own] = filt.astype(BF)
-        mixed_ref[0, :, own] = (q_s[:, own] * filt).astype(BF)
-
-
-def whole(shape):
-    return pl.BlockSpec(shape, lambda *_: (0,) * len(shape), pipeline_mode=pl.Buffered(1))
-
-
-def per_slot(shape):
-    return pl.BlockSpec((1,) + shape, lambda s, *_: (s,) + (0,) * len(shape))
-
-
-def mix_forward(isp, xs, g1, w_in, st, ct, w_cond, cb, table, table_t, m1, m2, mult):
-    _, t, d = xs.shape
-    f2 = table.shape[0]
-    f = f2 // 2
-    return pl.pallas_call(
-        fwd_kernel,
-        name="mix_forward",
-        grid=(2,),
-        out_shape=(
-            jax.ShapeDtypeStruct((2, t, 3 * d), BF),
-            jax.ShapeDtypeStruct((2, t, d), BF),
-            jax.ShapeDtypeStruct((2, t, d), BF),
-            jax.ShapeDtypeStruct((2, f2, d), BF),
-            jax.ShapeDtypeStruct((2, f2, d), BF),
-            jax.ShapeDtypeStruct((2, f, d), F32),
-            jax.ShapeDtypeStruct((2, f, d), BF),
-        ),
-        in_specs=[
-            pl.BlockSpec(memory_space=pltpu.SMEM),
-            per_slot((t, d)),
-            whole((1, d)),
-            whole((d, 3 * d)),
-            whole((3, 3 * d)),
-            whole((3, d)),
-            whole((d, d)),
-            whole((1, d)),
-            whole((f2, t)),
-            whole((t, f2)),
-            whole((t, 128)),
-            whole((t, 128)),
-            whole((f, 128)),
-        ],
-        out_specs=(
-            per_slot((t, 3 * d)),
-            per_slot((t, d)),
-            per_slot((t, d)),
-            per_slot((f2, d)),
-            per_slot((f2, d)),
-            per_slot((f, d)),
-            per_slot((f, d)),
-        ),
-        scratch_shapes=[pltpu.VMEM((t, d), BF), pltpu.VMEM((t, d), F32)],
-        compiler_params=pltpu.CompilerParams(vmem_limit_bytes=VMEM_LIMIT),
-    )(isp, xs, g1, w_in, st, ct, w_cond, cb, table, table_t, m1, m2, mult)
+    )(kind, tok, cot, g1, w_in, st, ct, w_cond, cb)
 
 
 def add_into(dst, src):
@@ -290,12 +339,12 @@
 
 def back_kernel(side, *refs):
     (
-        isp_ref, isl_ref, mixed_h, xs_h, cot_h, wo_h, g2_ref, wg_h, wu_h, wd_h,
+        kind_ref, mixed_h, xs_h, cot_h, wo_h, g2_ref, wg_h, wu_h, wd_h,
         proj_h, filt_h, ss_h, cs_h, th_h, feat_h,
-        st_ref, ct_ref, wc_h, tab_h, tabt_h, mult_ref, g1_ref, win_h,
+        st_ref, ct_ref, wc_h, tab_h, tabt_h, g1_ref, win_h,
         lay6_h, gtok6_h, odg_h, odu_h, odd_h, owo_h, owc_h, owi_h, small_out,
         a_s, b_s, u_s, r_s, n2_s, n2t_s, cot_s, mg_s, gmix_s,
-        act_s, gg_s, gu_s, w0_s, w1_s, w2_s, wo_s, wc_s, tab_s, tabt_s, m1_ref, m2_ref,
+        act_s, gg_s, gu_s, w0_s, w1_s, w2_s, wo_s, wc_s, tab_s, tabt_s, m1_ref, m2_ref, mult_ref,
         sbg_s, sbu_s, sbd_s, cg_s, cu_s, cd_s,
         dgg_s, dgu_s, xg_s, xu_s, yg_s, yu_s, zg_s, zu_s, d1_s, d2_s, zd_s,
         proj_s, filt_s, ss_s, cs_s, th_s, feat_s, gpre_s, gprem_s,
@@ -305,7 +354,8 @@
     n, d = n2_s.shape
     t = filt_s.shape[0]
     f = th_s.shape[0]
-    isp = isp_ref[0]
+    isl = kind_ref[0]
+    isp = inverse_span(isl, t)
     h = d // 2
     quarter = d // 4
     step48 = d // 16
@@ -384,11 +434,8 @@
         pl.semaphore_signal(barrier, inc=1, device_id=peer, device_id_type=MESH)
     pl.semaphore_wait(barrier, len(everyone))
 
-    place = lax.broadcasted_iota(jnp.int32, m1_ref.shape, 0)
-    short = place & (t // 4 - 1)
-    place = short + isl_ref[0] * (place - short)
-    m1_ref[...] = (place >= 1).astype(F32)
-    m2_ref[...] = (place >= 2).astype(F32)
+    causal_masks(m1_ref, m2_ref, isl)
+    mult_ref[...] = multiplicity(mult_ref.shape, isl, t)
 
     def remote(src, dst, peer, j):
         return pltpu.make_async_remote_copy(
@@ -1004,8 +1051,8 @@
 
 
 def back(
-    side, slots, isp, isl, mixed, xs, cot, w_out, g2, w_gate, w_up, w_down,
-    proj, filt, ss, cs, th, feat, st, ct, w_cond, table, table_t, mult, g1, w_in,
+    side, slots, kind, mixed, xs, cot, w_out, g2, w_gate, w_up, w_down,
+    proj, filt, ss, cs, th, feat, st, ct, w_cond, table, table_t, g1, w_in,
 ):
     n, d = cot.shape
     t = xs.shape[1]
@@ -1028,14 +1075,13 @@
             )
         )
         + (jax.ShapeDtypeStruct((16, d), F32),),
-        in_specs=[smem, smem] + [hbm] * 4 + [vm] + [hbm] * 9 + [vm, vm, hbm, hbm, hbm]
-        + [vm, vm, hbm],
+        in_specs=[smem] + [hbm] * 4 + [vm] + [hbm] * 9 + [vm, vm, hbm, hbm, hbm, vm, hbm],
         out_specs=(hbm,) * 8 + (vm,),
         scratch_shapes=[
             g(n, d), g(n, d), g(n, d), g(n, 128),
             b(n, d), b(d, n), b(n, d), b(n + t, d), b(n, d),
             b(n, d), b(n, d), b(n, d), b(d, d), b(d, d), b(d, d), b(d, d), b(d, d),
-            b(f2, t), b(t, f2), g(t, 128), g(t, 128),
+            b(f2, t), b(t, f2), g(t, 128), g(t, 128), g(f, 128),
             b(d, h), b(d, h), b(h, d),
             b(4, d, h), b(4, d, h), b(4, h, d),
             b(d, h), b(d, h), b(d, h), b(d, h), b(d, h), b(d, h),
@@ -1054,8 +1100,8 @@
             collective_id=1, has_side_effects=True, vmem_limit_bytes=65400 * 1024
         ),
     )(
-        isp, isl, mixed, xs, cot, w_out, g2, w_gate, w_up, w_down, proj, filt, ss, cs, th, feat,
-        st, ct, w_cond, table, table_t, mult, g1, w_in,
+        kind, mixed, xs, cot, w_out, g2, w_gate, w_up, w_down, proj, filt, ss, cs, th, feat,
+        st, ct, w_cond, table, table_t, g1, w_in,
     )
 
 
@@ -1067,31 +1113,17 @@
     n = lax.axis_size("seq")
     dp_count = lax.axis_size("dp")
     rank = lax.axis_index("seq")
-    span_long = rows * n
-    is_long = kind[0] == 1
-
-    freqs = -(-max(span_long // 2 + 1, n * (rows // 2 + 1)) // 16) * 16
-    table, table_t, mult = wave_tables(is_long, rows, span_long, freqs)
-    isp = jnp.where(is_long, 1.0 / span_long, 1.0 / rows).astype(F32).reshape(1)
-    place = jnp.arange(span_long, dtype=jnp.int32)
-    offset = jnp.where(is_long, place, place % rows)[:, None]
-    m1 = jnp.broadcast_to((offset >= 1).astype(F32), (span_long, 128))
-    m2 = jnp.broadcast_to((offset >= 2).astype(F32), (span_long, 128))
-
     tok6 = jnp.transpose(tokens[0], (1, 0, 2))
     cot6 = jnp.transpose(cotangent[0], (1, 0, 2))
-    xs, cot = reshard_in(tok6, cot6)
-
     g1, g2 = ln1_gain.reshape(1, d), ln2_gain.reshape(1, d)
-    proj, mixed, filt, sig_spec, cond_spec, th, feat = mix_forward(
-        isp, xs, g1, w_in, short_taps, cond_taps, w_cond, cond_bias.reshape(1, d),
-        table, table_t, m1, m2, mult,
+    xs, cot, proj, mixed, filt, sig_spec, cond_spec, th, feat, table, table_t = front(
+        kind, tok6, cot6, g1, w_in, short_taps, cond_taps, w_cond, cond_bias.reshape(1, d)
     )
     side = math.isqrt(dp_count // 2)
     lay6, gtok6, *sums, small = back(
-        side, slots, isp, is_long.astype(jnp.int32).reshape(1), mixed, xs, cot, w_out, g2,
-        w_gate, w_up, w_down, proj, filt, sig_spec, cond_spec, th, feat, short_taps, cond_taps,
-        w_cond, table, table_t, mult, g1, w_in,
+        side, slots, kind, mixed, xs, cot, w_out, g2, w_gate, w_up, w_down,
+        proj, filt, sig_spec, cond_spec, th, feat, short_taps, cond_taps, w_cond,
+        table, table_t, g1, w_in,
     )
     layer_out = jnp.transpose(lay6, (1, 0, 2))[None]
     grad_tokens = jnp.transpose(gtok6, (1, 0, 2))[None]

time: 317 us -> 282 us (0.89)
  Pallas kernels: 291 us -> 261 us
  other arithmetic: 14.8 us -> 9.3 us
    pallas_call x2 -> x1, Pallas kernels: 83.4 us -> 54.7 us  [front(): pl.pallas_call(front_kernel, name='front', out_shape=(xs, jax.ShapeDtypeS...]
    another operation x1 -> x0, other arithmetic: 4.17 us -> none
where the time goes in v3:
time: 282 us; the launch traced here: 280 us
  Pallas kernels  261 us (93%)
  other arithmetic  9.3 us (3%)
  local copies, waits for them, and re-layouts  8.65 us (3%)
    pallas_call x1, Pallas kernels, back(): pl.pallas_call(functools.partial(back_kernel, side), name='back', out_sha...  206 us
    pallas_call x1, Pallas kernels, front(): pl.pallas_call(front_kernel, name='front', out_shape=(xs, jax.ShapeDtypeS...  54.7 us
    convert_element_type x6, other arithmetic, on_device(): sums = [a.astype(F32) for a in sums]  9.3 us

profile of v3, /device:TPU:25, one launch (start us, length us, event | category | flops | bytes accessed | tf_op | source)
XLA Modules:
  0.0 279.9 jit_solution(10129493668100473619)
XLA Ops:
  0.6 1.3 reshape.41.g1_ref.refs_20_
  2.6 1.3 reshape.42.cb_ref
  3.8 0.0 copy-start.8
  3.8 54.7 %front.1 = (bf16[2,512,768]{2,1,0:T(8,128)(2,1)}, bf16[768,768]{1,0:T(8,128)(2,1)}, bf16[2,512,2304]{2,1,0:T(8,128)(2,1)}, bf16[2,512,768]{2,1,0:T(8,128)(2,1)},...) custom-call(s32[1]{0:T(128)S(6)} %copy.29.kind_ref.refs_0_, ...), custom_call_target="tpu_custom_call" | custom-call | tf_op jit(solution)/shard_map/front/pallas_call | solution.py:310
  58.6 0.0 copy-done.8
  58.6 0.6 reshape.43.refs_5_
  59.2 205.8 %back.1 = (bf16[6,128,768]{2,1,0:T(8,128)(2,1)}, bf16[6,128,768]{2,1,0:T(8,128)(2,1)}, bf16[192,3072]{1,0:T(8,128)(2,1)}, bf16[192,3072]{1,0:T(8,128)(2,1)}, bf1...) custom-call(s32[1]{0:T(128)S(6)} %copy.29.kind_ref.refs_0_, ...), custom_call_target="tpu_custom_call" | custom-call | tf_op jit(solution)/shard_map/back/pallas_call | solution.py:1067
  265.0 0.8 fusion
  265.9 0.6 constant_dynamic-slice_fusion
  266.5 0.0 copy-start.1
  266.5 3.0 %convert_element_type.21 = f32[192,3072]{1,0:T(8,128)} convert(bf16[192,3072]{1,0:T(8,128)(2,1)} %get-tuple-element.50) | non-fusion elementwise | flops 589824 | bytes 3538944 | tf_op jit(solution)/shard_map/convert_element_type | solution.py:1131
  269.5 0.0 copy-done.1
  269.5 0.0 copy-start
  269.5 1.7 convert_element_type.22
  271.2 0.0 copy-done
  271.2 1.6 convert_element_type.23
  272.8 0.0 copy-start.6
  272.8 0.0 copy-done.4
  272.8 0.0 copy-start.5
  272.8 1.3 convert_element_type.18
  274.1 0.0 copy-done.6
  274.1 0.9 convert_element_type.19
  275.0 0.0 copy-done.5
  275.0 0.9 convert_element_type.20
  275.8 0.0 copy-done.7
  275.9 0.7 constant_dynamic-slice_fusion.3
  276.6 0.7 constant_dynamic-slice_fusion.2
  277.2 0.6 constant_dynamic-slice_fusion.4
  277.9 0.0 copy-done.3
  277.9 1.0 copy.30
  278.9 0.0 copy-done.2
  278.9 1.0 copy.31
  (7 shorter events, 0.0 us)
Async XLA Ops:
  3.8 54.8 %copy-start.8 = (f32[768]{0:T(1024)S(1)}, f32[768]{0:T(1024)}, u32[]{:S(2)}) copy-start(f32[768]{0:T(1024)} %param.23) | copy-start | bytes 9220
  266.5 3.0 %copy-start.1 = (bf16[192,3072]{1,0:T(8,128)(2,1)S(1)}, bf16[192,3072]{1,0:T(8,128)(2,1)}, u32[]{:S(2)}) copy-start(bf16[192,3072]{1,0:T(8,128)(2,1)} %get-tuple-element.51) | copy-start | bytes 3538948
  269.5 1.7 copy-start
  271.2 1.6 copy-start.4
  272.8 1.3 copy-start.6
  272.8 2.2 copy-start.5
  272.8 3.0 %copy-start.7 = (f32[16,768]{1,0:T(8,128)S(1)}, f32[16,768]{1,0:T(8,128)}, u32[]{:S(2)}) copy-start(f32[16,768]{1,0:T(8,128)} %get-tuple-element.46) | copy-start | bytes 147460
  274.1 3.7 %copy-start.3 = (bf16[6,128,768]{2,1,0:T(8,128)(2,1)S(1)}, bf16[6,128,768]{2,1,0:T(8,128)(2,1)}, u32[]{:S(2)}) copy-start(bf16[6,128,768]{2,1,0:T(8,128)(2,1)} %get-tuple-element.44) | copy-start | bytes 3538948
  275.0 3.9 %copy-start.2 = (bf16[6,128,768]{2,1,0:T(8,128)(2,1)S(1)}, bf16[6,128,768]{2,1,0:T(8,128)(2,1)}, u32[]{:S(2)}) copy-start(bf16[6,128,768]{2,1,0:T(8,128)(2,1)} %get-tuple-element.45) | copy-start | bytes 3538948

commit v4 on v3

v4 whole, which is shorter than its diff:
```python
import functools
import math

import jax
import jax.numpy as jnp
from jax import lax
from jax.experimental import pallas as pl
from jax.experimental.pallas import tpu as pltpu
from jax.sharding import PartitionSpec as P

BF = jnp.bfloat16
F32 = jnp.float32
MESH = pl.DeviceIdType.MESH
EPS = 1e-05
CB = 256
FC = 384
RB = 256
VMEM_LIMIT = 60 * 2**20


def mm(a, b):
    return jnp.dot(a, b, preferred_element_type=F32)


def mm_nt(a, b):
    return lax.dot_general(a, b, (((1,), (1,)), ((), ())), preferred_element_type=F32)


def mm_tn(a, b):
    return lax.dot_general(a, b, (((0,), (0,)), ((), ())), preferred_element_type=F32)


def unit_rows(x):
    mean = jnp.mean(x, axis=-1, keepdims=True)
    centered = x - mean
    r = lax.rsqrt(jnp.mean(centered * centered, axis=-1, keepdims=True) + EPS)
    return centered * r, r


def unit_back(g, u, r, gain):
    e = g * gain
    return r * (
        e - jnp.mean(e, axis=-1, keepdims=True) - u * jnp.mean(e * u, axis=-1, keepdims=True)
    )


def lanes(ref, width):
    m = ref[...]
    return jnp.concatenate([m] * (width // m.shape[1]), axis=1)


def down(a, j):
    return pltpu.roll(a, j, axis=0)


def up(a, j):
    return pltpu.roll(a, a.shape[0] - j, axis=0)


def masked(a, m):
    blk = a.shape[0] // 4
    parts = []
    for b in range(4):
        parts.append(a[b * blk : b * blk + 8] * m[8 * b : 8 * b + 8])
        parts.append(a[b * blk + 8 : (b + 1) * blk])
    return jnp.concatenate(parts, axis=0)


def conv(a, taps, m1, m2):
    return taps[0:1] * a + taps[1:2] * masked(down(a, 1), m1) + taps[2:3] * masked(down(a, 2), m2)


def conv_back(g, a, taps, m1, m2):
    g1, g2 = up(masked(g, m1), 1), up(masked(g, m2), 2)
    sums = [jnp.sum(v * a, axis=0, keepdims=True) for v in (g, g1, g2)]
    return taps[0:1] * g + taps[1:2] * g1 + taps[2:3] * g2, sums


def cols_at(c, width, base=0):
    return pl.ds(pl.multiple_of(base + c * width, 128), width)


def short_rows(i, t):
    half = t // 8 + 1
    block = jnp.zeros_like(i)
    for k in range(1, 5):
        block += (i >= k * half).astype(jnp.int32)
    return block, i - half * block


def wave_table(ref, axis, isl, t):
    freqs = ref.shape[axis] // 2
    j = lax.broadcasted_iota(jnp.int32, ref.shape, axis)
    pos = lax.broadcasted_iota(jnp.int32, ref.shape, 1 - axis)
    sin = (j >= freqs).astype(jnp.int32)
    i = j - freqs * sin
    block, f = short_rows(i, t)
    short = t // 4
    phase = isl * (i * pos) + (1 - isl) * (4 * f * (pos & (short - 1)))
    kept_long = (i <= t // 2).astype(jnp.int32)
    kept_short = ((pos >= block * short) & (pos < (block + 1) * short)).astype(jnp.int32)
    kept = isl * kept_long + (1 - isl) * kept_short
    phase = (phase - (t // 4) * sin) & (t - 1)
    angle = (phase - t // 2).astype(F32) * (2.0 * math.pi / t)
    z = angle * angle
    value = jnp.full_like(z, -1.0 / math.factorial(14))
    for k in range(6, -1, -1):
        value = value * z + (-1.0) ** k / math.factorial(2 * k)
    ref[...] = (-value * kept.astype(F32)).astype(ref.dtype)


def multiplicity(shape, isl, t):
    i = lax.broadcasted_iota(jnp.int32, shape, 0)
    block, f = short_rows(i, t)
    once_long = ((i == 0) | (i == t // 2)).astype(jnp.int32)
    once_short = ((f == 0) | (f == t // 8)).astype(jnp.int32)
    long = (2 - once_long) * (i <= t // 2).astype(jnp.int32)
    short = (2 - once_short) * (block < 4).astype(jnp.int32)
    return (isl * long + (1 - isl) * short).astype(F32)


def causal_masks(m1_ref, m2_ref, isl):
    row = lax.broadcasted_iota(jnp.int32, m1_ref.shape, 0)
    place = (row & 7) + isl * (row - (row & 7))
    m1_ref[...] = (place >= 1).astype(F32)
    m2_ref[...] = (place >= 2).astype(F32)


def inverse_span(isl, t):
    long = isl.astype(F32)
    return long * (1.0 / t) + (1.0 - long) * (4.0 / t)


def front_kernel(
    kind_ref, tok_h, g1_ref, win_h, st_ref, ct_ref, wc_h, cb_ref,
    xs_h, proj_h, mixed_h, filt_h, ss_h, sc_h, th_h, feat_h, q_h, k_h, v_h, tab_h, tabt_h,
    x_s, win_s, wc_s, tab_s, tabt_s, m1_ref, m2_ref, ms_s, n1_s, q_s,
    proj_s, mixed_s, filt_s, ss_s, sc_s, th_s, feat_s, qb_s, k_s, v_s,
    load_sem, out_sem, send_sem, recv_sem,
):
    t, d = n1_s.shape
    f = ms_s.shape[0]
    n = 4
    blk = t // n
    dp, me = lax.axis_index("dp"), lax.axis_index("seq")
    peers = [lax.rem(me + k, n) for k in range(n)]
    half = lax.rem(me, 2)
    pair = me + 1 - 2 * half
    isl = kind_ref[0]
    isp = inverse_span(isl, t)

    block = lambda i: pl.ds(pl.multiple_of(i * blk, blk), blk)
    loads = [
        pltpu.make_async_copy(win_h, win_s, load_sem.at[0]),
        pltpu.make_async_copy(wc_h, wc_s, load_sem.at[1]),
        pltpu.make_async_copy(tok_h.at[me], x_s.at[0, block(me)], load_sem.at[2]),
        pltpu.make_async_copy(tok_h.at[n + me // 2], x_s.at[1, block(me)], load_sem.at[3]),
    ]

    barrier = pltpu.get_barrier_semaphore()
    for k in range(1, n):
        pl.semaphore_signal(barrier, inc=1, device_id=(dp, peers[k]), device_id_type=MESH)
    pl.semaphore_wait(barrier, n - 1)

    def remote(src, dst, peer, j):
        return pltpu.make_async_remote_copy(
            src_ref=src,
            dst_ref=dst,
            send_sem=send_sem.at[j],
            recv_sem=recv_sem.at[j],
            device_id=(dp, peer),
            device_id_type=MESH,
        )

    whole_slot = [
        remote(tok_h.at[peers[k]], x_s.at[0, block(me)], peers[k], k - 1) for k in range(1, n)
    ]
    to_pair = remote(tok_h.at[n + me // 2], x_s.at[1, block(me)], pair, 3)
    across = remote(tok_h.at[n + peers[2] // 2], x_s.at[1, block(me)], peers[2], 4)
    handed = remote(x_s.at[1, block(peers[2])], x_s.at[1, block(peers[2])], pair, 5)
    for c in whole_slot + [across, to_pair]:
        c.start()
    for c in loads:
        c.start()

    wave_table(tab_s, 0, isl, t)
    wave_table(tabt_s, 1, isl, t)
    causal_masks(m1_ref, m2_ref, isl)
    ms_s[...] = multiplicity(ms_s.shape, isl, t) * isp

    for c in loads[:4]:
        c.wait()
    for c in whole_slot:
        c.wait()

    outs = [
        (x_s, xs_h), (proj_s, proj_h), (ss_s, ss_h), (sc_s, sc_h), (feat_s, feat_h),
        (qb_s, q_h), (k_s, k_h), (v_s, v_h),
        (mixed_s, mixed_h), (filt_s, filt_h), (th_s, th_h),
    ]

    def out_copy(slot, j):
        return pltpu.make_async_copy(outs[j][0].at[slot], outs[j][1].at[slot], out_sem.at[slot, j])

    tables = [
        pltpu.make_async_copy(tab_s, tab_h, load_sem.at[4]),
        pltpu.make_async_copy(tabt_s, tabt_h, load_sem.at[5]),
    ]
    for c in tables:
        c.start()

    @pl.loop(0, 2)
    def _(slot):
        @pl.when(slot == 1)
        def _():
            to_pair.wait()
            handed.wait()

        @pl.loop(0, t // 128)
        def _(r):
            rows = pl.ds(pl.multiple_of(r * 128, 128), 128)
            u, _ = unit_rows(x_s[slot, rows, :].astype(F32))
            n1_s[rows, :] = (u * g1_ref[...]).astype(BF)

        @pl.loop(0, d // CB)
        def _(c):
            m1, m2 = lanes(m1_ref, CB), lanes(m2_ref, CB)
            own = cols_at(c, CB)

            def part(k):
                cols = cols_at(c, CB, k * d)
                p = mm(n1_s[...], win_s[:, cols]).astype(BF)
                proj_s[slot, :, cols] = p
                return conv(p.astype(F32), st_ref[:, cols], m1, m2)

            query = part(0)
            q_s[:, own] = query
            qb_s[slot, :, own] = query.astype(BF)
            key = part(1)
            k_s[slot, :, own] = key.astype(BF)
            value = part(2).astype(BF)
            v_s[slot, :, own] = value
            value_f = value.astype(F32)
            signal = (key * value_f).astype(BF)
            ss_s[slot, :, own] = mm(tab_s[...], signal).astype(BF)
            cond = conv(value_f, ct_ref[:, own], m1, m2).astype(BF)
            xc = mm(tab_s[...], cond)
            sc_s[slot, :, own] = xc.astype(BF)
            power = (xc[:f] * xc[:f] + xc[f:] * xc[f:]) * isp
            feat_s[slot, :, own] = jnp.log1p(power).astype(BF)

        for j in range(8):
            out_copy(slot, j).start()

        @pl.when(slot == 0)
        def _():
            across.wait()
            handed.start()

        @pl.loop(0, d // CB)
        def _(c):
            own = cols_at(c, CB)
            th = jnp.tanh(mm(feat_s[slot], wc_s[:, own]) + cb_ref[:, own])
            th_s[slot, :, own] = th
            g = (1.0 + th) * lanes(ms_s, CB)
            xs = ss_s[slot, :, own].astype(F32)
            y = jnp.concatenate([(g * xs[:f]).astype(BF), (g * xs[f:]).astype(BF)], axis=0)
            filt = mm(tabt_s[...], y)
            filt_s[slot, :, own] = filt.astype(BF)
            mixed_s[slot, :, own] = (q_s[:, own] * filt).astype(BF)

        for j in range(8, 11):
            out_copy(slot, j).start()

    for slot in range(2):
        for j in range(11):
            out_copy(slot, j).wait()
    for c in tables:
        c.wait()


def front(kind, tok, g1, w_in, st, ct, w_cond, cb):
    slots, blk, d = tok.shape
    t = 4 * blk
    f = -(-max(t // 2 + 1, 4 * (blk // 2 + 1)) // 16) * 16
    hbm = pl.BlockSpec(memory_space=pl.ANY)
    vm = pl.BlockSpec(memory_space=pltpu.VMEM)
    smem = pl.BlockSpec(memory_space=pltpu.SMEM)
    per_slot = [
        ((2, t, d), BF), ((2, t, 3 * d), BF), ((2, t, d), BF), ((2, t, d), BF),
        ((2, 2 * f, d), BF), ((2, 2 * f, d), BF), ((2, f, d), F32), ((2, f, d), BF),
        ((2, t, d), BF), ((2, t, d), BF), ((2, t, d), BF),
    ]
    xs, *rest = [jax.ShapeDtypeStruct(*s) for s in per_slot]
    tables = [((2 * f, t), BF), ((t, 2 * f), BF)]
    return pl.pallas_call(
        front_kernel,
        name="front",
        out_shape=(xs, *rest)
        + tuple(jax.ShapeDtypeStruct(*s) for s in tables),
        in_specs=[smem, hbm, vm, hbm, vm, vm, hbm, vm],
        out_specs=(hbm,) * 13,
        scratch_shapes=[
            pltpu.VMEM((2, t, d), BF), pltpu.VMEM((d, 3 * d), BF), pltpu.VMEM((d, d), BF),
            pltpu.VMEM(*tables[0]), pltpu.VMEM(*tables[1]),
            pltpu.VMEM((32, 128), F32), pltpu.VMEM((32, 128), F32), pltpu.VMEM((f, 128), F32),
            pltpu.VMEM((t, d), BF), pltpu.VMEM((t, d), F32),
        ]
        + [pltpu.VMEM(*s) for s in per_slot[1:]]
        + [
            pltpu.SemaphoreType.DMA((6,)),
            pltpu.SemaphoreType.DMA((2, 11)),
            pltpu.SemaphoreType.DMA((6,)),
            pltpu.SemaphoreType.DMA((6,)),
        ],
        compiler_params=pltpu.CompilerParams(
            collective_id=0, has_side_effects=True, vmem_limit_bytes=VMEM_LIMIT
        ),
    )(kind, tok, g1, w_in, st, ct, w_cond, cb)


def add_into(dst, src):
    dst[...] = (dst[...].astype(F32) + src[...].astype(F32)).astype(dst.dtype)


def back_kernel(side, *refs):
    (
        kind_ref, mixed_h, xs_h, cot_h, wo_h, g2_ref, wg_h, wu_h, wd_h,
        proj_h, filt_h, ss_h, cs_h, th_h, feat_h, q_h, k_h, v_h,
        st_ref, ct_ref, wc_h, tab_h, tabt_h, g1_ref, win_h,
        lay6_h, gtok6_h, odg_h, odu_h, odd_h, owo_h, owc_h, owi_h, spool_h, small_out,
        a_s, b_s, u_s, r_s, n2_s, n2t_s, cot_s, mg_s, gmix_s,
        act_s, gg_s, gu_s, w0_s, w1_s, w2_s, wo_s, wc_s, tab_s, tabt_s, m1_ref, m2_ref, mult_ref,
        sbg_s, sbu_s, sbd_s, cg_s, cu_s, cd_s,
        dgg_s, dgu_s, xg_s, xu_s, yg_s, yu_s, zg_s, zu_s, d1_s, d2_s, zd_s,
        proj_s, filt_s, ss_s, cs_s, th_s, feat_s, q_s, k_s, v_s, gpre_s,
        c2_s, raw2_s, rd_s, rx_s, ry_s, z2_s, small_s, sgot_s, ssum_s,
        load_sem, w_sem, spool_sem, back_sem, send_sem, recv_sem, local_sem,
    ) = refs
    n, d = n2_s.shape
    t = filt_s.shape[0]
    f = th_s.shape[0]
    isl = kind_ref[0]
    isp = inverse_span(isl, t)
    h = d // 2
    quarter = d // 4
    step48 = d // 16
    dr = h // 4

    dp, me = lax.axis_index("dp"), lax.axis_index("seq")
    core = lax.rem(dp, 2)
    x = lax.rem(lax.rem(dp // 2, side), 2)
    y = lax.rem(dp // (2 * side), 2)
    dp_x = dp + 2 - 4 * x
    dp_y = dp + 2 * side - 4 * side * y
    at_core, at_x, at_y = (dp + 1 - 2 * core, me), (dp_x, me), (dp_y, me)
    at_xy = (dp_x + dp_y - dp, me)
    peers = [lax.rem(me + k, 4) for k in range(4)]
    at_z = [(dp, peers[k]) for k in range(4)]
    half = lax.rem(me, 2)
    at_pair = (dp, me + 1 - 2 * half)
    half_at = pl.ds(pl.multiple_of(half * RB, RB), RB)
    xy = 2 * x + y
    diag, by_x, by_y = 3 - xy, 2 * (1 - x) + y, 2 * x + 1 - y

    def owner(s):
        if isinstance(s, int):
            return (diag, by_x, by_y, xy)[s]
        return 2 * jnp.where(s < 2, 1 - x, x) + jnp.where(lax.rem(s, 2) == 0, 1 - y, y)

    def rows_at(i, size, base=0):
        return pl.ds(pl.multiple_of(base + i * size, math.gcd(size, base) if base else size), size)

    def each(copies, what):
        for c in copies:
            getattr(c, what)()

    row_moves = lambda src, dst: [
        (src.at[0], dst.at[pl.ds(0, t)]),
        (src.at[1, half_at], dst.at[pl.ds(t, RB)]),
    ]
    moves = (
        row_moves(mixed_h, mg_s)
        + row_moves(xs_h, gmix_s)
        + [(wo_h, wo_s)]
        + [(tab_h, tab_s), (tabt_h, tabt_s), (wc_h, wc_s), (proj_h, proj_s)]
    )
    loads = [pltpu.make_async_copy(s, e, load_sem.at[j]) for j, (s, e) in enumerate(moves)]
    slot_moves = [
        (filt_h, filt_s), (ss_h, ss_s), (th_h, th_s), (q_h, q_s),
        (cs_h, cs_s), (feat_h, feat_s), (k_h, k_s), (v_h, v_s),
    ]
    slot_load = lambda slot, j: pltpu.make_async_copy(
        slot_moves[j][0].at[slot], slot_moves[j][1], load_sem.at[11 + j]
    )
    x_loads = [
        pltpu.make_async_copy(a, b, load_sem.at[19 + j])
        for j, (a, b) in enumerate(row_moves(xs_h, cot_s))
    ]

    def weights(s):
        cols = cols_at(owner(s), d)
        return [
            pltpu.make_async_copy(wg_h.at[:, cols], w0_s, w_sem.at[0]),
            pltpu.make_async_copy(wu_h.at[:, cols], w1_s, w_sem.at[1]),
            pltpu.make_async_copy(wd_h.at[cols, :], w2_s, w_sem.at[2]),
        ]

    win_loads = [
        pltpu.make_async_copy(win_h.at[:, k * d : (k + 1) * d], w, w_sem.at[3 + k])
        for k, w in enumerate((w0_s, w1_s, w2_s))
    ]

    each(loads[:5], "start")
    each(weights(3), "start")
    each(loads[5:], "start")
    for j in range(8):
        slot_load(0, j).start()

    barrier = pltpu.get_barrier_semaphore()
    everyone = [at_core, at_x, at_y, at_xy] + at_z[1:]
    for peer in everyone:
        pl.semaphore_signal(barrier, inc=1, device_id=peer, device_id_type=MESH)
    pl.semaphore_wait(barrier, len(everyone))

    causal_masks(m1_ref, m2_ref, isl)
    mult_ref[...] = multiplicity(mult_ref.shape, isl, t)

    def remote(src, dst, peer, j):
        return pltpu.make_async_remote_copy(
            src_ref=src,
            dst_ref=dst,
            send_sem=send_sem.at[j],
            recv_sem=recv_sem.at[j],
            device_id=peer,
            device_id_type=MESH,
        )

    C, DG, XS, YS, ZD, ZG, GA, GC = 0, 12, 20, 22, 24, 27, 36, 45
    LAY, GT0, GT1, PAIR, SMALL, COT, DX, DY, UNIT = 57, 63, 66, 69, 70, 76, 82, 90, 94

    rows128 = lay6_h.shape[1]
    sources = [lax.rem(me + 4 - k, 4) for k in range(4)]
    sends_part = [lax.rem(p, 2) == me // 2 for p in peers]
    gets_part = [half == s // 2 for s in sources]

    def cot_copies(k):
        moves = (
            (cot_h.at[peers[k]], cot_s.at[rows_at(me, rows128)]),
            (cot_h.at[4 + peers[k] // 2], cot_s.at[rows_at(half, rows128, t)]),
        )
        if k == 0:
            return [
                pltpu.make_async_copy(a, b, load_sem.at[9 + j]) for j, (a, b) in enumerate(moves)
            ]
        return [remote(a, b, at_z[k], COT + 2 * (k - 1) + j) for j, (a, b) in enumerate(moves)]

    for k in (1, 2, 3, 0):
        full, part = cot_copies(k)
        full.start()
        pl.when(sends_part[k])(part.start)

    each(loads[:5], "wait")

    @pl.loop(0, n // RB)
    def _(i):
        rows = rows_at(i, RB)
        hid = gmix_s[rows, :].astype(F32) + mm(mg_s[rows, :], wo_s[...])
        a_s[rows, :] = hid
        b_s[rows, :] = jnp.zeros_like(hid)
        u, r = unit_rows(hid)
        u_s[rows, :] = u
        r_s[rows, :] = jnp.broadcast_to(r, (RB, 128))
        n2 = u * g2_ref[...]
        n2_s[rows, :] = n2.astype(BF)
        n2t_s[:, rows] = n2.T.astype(BF)

    pairs = ((sbg_s, cg_s, dgg_s, xg_s, yg_s, zg_s), (sbu_s, cu_s, dgu_s, xu_s, yu_s, zu_s))
    rank_rows = lambda q: pl.ds(q * quarter, quarter)

    def core_copies(s):
        bufs = ((sbg_s, cg_s.at[s]), (sbu_s, cu_s.at[s]), (sbd_s, cd_s.at[owner(s)]))
        return [remote(a, b, at_core, C + 4 * j + s) for j, (a, b) in enumerate(bufs)]

    def diag_copies(odd):
        return [
            remote(p[1].at[0, rank_rows(q)], p[2].at[rank_rows(q)], at_y if odd else at_x, DG + 4 * j + q)
            for j, p in enumerate(pairs)
            for q in ((1, 3) if odd else (0, 2))
        ]

    x_copies = lambda: [remote(p[1].at[1], p[3], at_x, XS + j) for j, p in enumerate(pairs)]
    y_copies = lambda: [remote(p[1].at[2], p[4], at_y, YS + j) for j, p in enumerate(pairs)]

    def down_first(q, peer, k, e):
        return remote(cd_s.at[q, rows_at(k, dr)], d1_s.at[q, e], peer, DX + 2 * q + e)

    def step_sums(s, j):
        p = pairs[j]

        def add_ranks(first):
            for q in (first, first + 2):
                add_into(p[1].at[s, rank_rows(q)], p[2].at[rank_rows(q)])

        @pl.when(s == 0)
        def _():
            each(diag_copies(False)[2 * j : 2 * j + 2], "start")
            each(diag_copies(True)[2 * j : 2 * j + 2], "start")

        @pl.when(s == 1)
        def _():
            each(diag_copies(True)[2 * j : 2 * j + 2], "wait_recv")
            add_ranks(1)
            x_copies()[j].start()

        @pl.when(s == 2)
        def _():
            each(diag_copies(False)[2 * j : 2 * j + 2], "wait_recv")
            add_ranks(0)
            y_copies()[j].start()

    saved = (act_s, gu_s, gg_s)

    def spool(s, i, j):
        rows = rows_at(i, RB)
        return pltpu.make_async_copy(
            saved[j].at[rows], spool_h.at[j, s, rows], spool_sem.at[i, j]
        )

    @pl.loop(0, 4)
    def _(p):
        s = 3 - p
        each(weights(s), "wait")

        @pl.loop(0, n // RB)
        def _(i):
            rows = rows_at(i, RB)

            @pl.when(p > 0)
            def _():
                for j in range(3):
                    spool(s, i, j).wait()

            n2 = n2_s[rows, :]
            pre = mm(n2, w0_s[...])
            lin = mm(n2, w1_s[...])
            sg = 1.0 / (1.0 + jnp.exp(-pre))
            silu = pre * sg
            act = (silu * lin).astype(BF)
            act_s[rows, :] = act
            gu_s[rows, :] = silu.astype(BF)
            gg_s[rows, :] = (lin * sg * (1.0 + pre * (1.0 - sg))).astype(BF)
            a_s[rows, :] += mm(act, w2_s[...])

            @pl.when(p < 3)
            def _():
                for j in range(3):
                    spool(s, i, j).start()

        @pl.when(p < 3)
        def _():
            each(weights(s - 1), "start")

    @pl.loop(0, n // RB)
    def _(i):
        rows = rows_at(i, RB)
        n2_s[rows, :] = a_s[rows, :].astype(BF)

    sends_half = [half == p // 2 for p in peers]
    gets_half = [lax.rem(s, 2) == me // 2 for s in sources]

    def home(buf, out, part, base, k):
        if part == 0:
            src, dst = buf.at[rows_at(peers[k], rows128)], out.at[me]
        else:
            src, dst = buf.at[rows_at(lax.rem(peers[k], 2), rows128, t)], out.at[4 + me // 2]
        if k == 0:
            return pltpu.make_async_copy(src, dst, local_sem.at[base])
        return remote(src, dst, at_z[k], base + k - 1)

    def home_start(buf, out, part, base, local):
        for k in range(4):
            copy = home(buf, out, part, base if k else local, k)
            if part == 0:
                copy.start()
            else:
                pl.when(sends_half[k])(copy.start)

    def home_wait(buf, out, part, base, local):
        for k in range(4):
            copy = home(buf, out, part, base if k else local, k)
            if part == 0:
                copy.wait()
            elif k == 0:
                pl.when(sends_half[0])(copy.wait)
            else:
                pl.when(sends_half[k])(copy.wait_send)
                pl.when(gets_half[k])(copy.wait_recv)

    home_start(n2_s, lay6_h, 0, LAY, 0)
    home_start(n2_s, lay6_h, 1, LAY + 3, 1)

    for k in range(4):
        full, part = cot_copies(k)
        full.wait()
        if k == 0:
            pl.when(sends_part[0])(part.wait)
        else:
            pl.when(sends_part[k])(part.wait_send)
            pl.when(gets_part[k])(part.wait_recv)

    def unspool(s, j):
        return pltpu.make_async_copy(spool_h.at[j, s], saved[j], back_sem.at[j])

    @pl.loop(0, 4)
    def _(s):
        @pl.when(s > 0)
        def _():
            each(weights(s), "wait")
            unspool(s, 1).wait()
            unspool(s, 2).wait()

        @pl.loop(0, n // RB)
        def _(i):
            rows = rows_at(i, RB)
            g_act = mm_nt(cot_s[rows, :], w2_s[...])
            g_up = (g_act * gu_s[rows, :].astype(F32)).astype(BF)
            gu_s[rows, :] = g_up
            g_gate = (g_act * gg_s[rows, :].astype(F32)).astype(BF)
            gg_s[rows, :] = g_gate
            b_s[rows, :] += mm_nt(g_gate, w0_s[...]) + mm_nt(g_up, w1_s[...])

        @pl.when(s < 3)
        def _():
            each(weights(s + 1), "start")

        @pl.when(s > 0)
        def _():
            each(core_copies(s - 1), "wait_send")

        def product(which, j, put):
            cols = cols_at(which, h)

            @pl.loop(0, d // RB)
            def _(i):
                rows, out = rows_at(i, RB), cols_at(i, RB)
                if j == 2:
                    put(slice(None), out, mm_tn(act_s[:, cols], cot_s[:, out]))
                else:
                    put(rows, slice(None), mm(n2t_s[rows, :], (gg_s, gu_s)[j][:, cols]))

        for j, buf in enumerate((sbg_s, sbu_s, sbd_s)):

            def put(rows, cols, value, buf=buf):
                buf[rows, cols] = value.astype(BF)

            if j == 2:
                pl.when(s > 0)(unspool(s, 0).wait)
            product(1 - core, j, put)
            core_copies(s)[j].start()
        for j, (buf, at) in enumerate(((cg_s, s), (cu_s, s), (cd_s, owner(s)))):
            core_copies(s)[j].wait_recv()

            def put(rows, cols, value, buf=buf, at=at):
                buf[at, rows, cols] = (buf[at, rows, cols].astype(F32) + value).astype(BF)

            product(core, j, put)
            pl.when(s < 3)(unspool(s + 1, (2, 1, 0)[j]).start)
            if j < 2:
                step_sums(s, j)

    for q in range(4):
        peer, near = (at_y, by_y) if q % 2 else (at_x, by_x)
        down_first(q, peer, diag, 0).start()
        down_first(q, peer, near, 1).start()

    each(win_loads, "start")
    small_s[...] = jnp.zeros_like(small_s)

    @pl.loop(0, n // RB)
    def _(i):
        rows = rows_at(i, RB)
        g, u = b_s[rows, :], u_s[rows, :]
        small_s[14:15, :] += jnp.sum(g * u, axis=0, keepdims=True)
        gh = cot_s[rows, :].astype(F32) + unit_back(g, u, r_s[rows, 0:1], g2_ref[...])
        gmix_s[rows, :] = gh.astype(BF)

    each(x_loads, "start")
    pair_at = rows_at(half, RB, n)
    mg_s[pair_at, :] = mm_nt(gmix_s[t:, :], wo_s[...]).astype(BF)
    pair_copy = remote(mg_s.at[pair_at], mg_s.at[pair_at], at_pair, PAIR)
    pair_copy.start()

    each(core_copies(3), "wait_send")

    def pos(q):
        return q // 2 + 2 * (q % 2 if isinstance(q, int) else lax.rem(q, 2))

    def reorder(dst, src, which):
        cols = cols_at(which, h)
        for q in range(4):
            for k in range(4):
                to, fr = (4 * k + pos(q)) * step48, (4 * q + k) * step48
                dst[to : to + step48, :] = src[fr : fr + step48, cols].astype(BF)

    def unit_core(u):
        return remote((sbg_s, sbu_s)[u % 2], c2_s.at[u], at_core, UNIT + 15 * u)

    raw_of = lambda u: raw2_s.at[2 if u == 4 else u % 2]
    two = 2 * step48

    def unit_diag(u):
        return [
            remote(
                c2_s.at[u, rows_at(2 * diag + e, two)],
                rd_s.at[u, pl.ds(e * two, two)],
                (at_x, at_y)[e],
                UNIT + 15 * u + 1 + e,
            )
            for e in range(2)
        ]

    def unit_near(u):
        return [
            remote(c2_s.at[u, rows_at(by_x, quarter)], rx_s.at[u], at_x, UNIT + 15 * u + 3),
            remote(c2_s.at[u, rows_at(by_y, quarter)], ry_s.at[u], at_y, UNIT + 15 * u + 4),
        ]

    def unit_rank(q):
        return rows_at(4 * xy + pos(q), step48)

    def unit_z(u):
        return [
            remote(
                c2_s.at[u, unit_rank(peers[k])], z2_s.at[u, k - 1], at_z[k], UNIT + 15 * u + 4 + k
            )
            for k in range(1, 4)
        ]

    def unit_view(u):
        if u in (0, 4):
            out = owc_h if u == 0 else owo_h
            return lambda k, c: out.at[rows_at(k, step48), cols_at(c, h)]
        return lambda k, c: owi_h.at[rows_at(k, step48), cols_at(3 * c + u - 1, h)]

    def unit_gather(u):
        return gather(c2_s.at[u, unit_rank(me)], unit_view(u), UNIT + 15 * u + 8, 5 + u)

    def unit_gather_core(u):
        return gather_core(unit_view(u), UNIT + 15 * u + 11)

    def unit1(u):
        unit_core(u).wait()

        @pl.loop(0, 4)
        def _(k):
            add_into(c2_s.at[u, rows_at(k, quarter)], raw_of(u).at[rows_at(k, quarter)])

        each(unit_diag(u), "start")

    def unit2(u):
        each(unit_diag(u), "wait")
        add_into(c2_s.at[u, rows_at(2 * by_y, two)], rd_s.at[u, 0:two])
        add_into(c2_s.at[u, rows_at(2 * by_x + 1, two)], rd_s.at[u, two : 2 * two])
        each(unit_near(u), "start")

    def unit3(u):
        each(unit_near(u), "wait")
        at = c2_s.at[u, rows_at(xy, quarter)]
        total = at[...].astype(F32) + rx_s[u].astype(F32) + ry_s[u].astype(F32)
        at[...] = total.astype(BF)
        each(unit_z(u), "start")

    def unit4(u):
        each(unit_z(u), "wait")
        at = c2_s.at[u, unit_rank(me)]
        total = at[...].astype(F32)
        for k in range(3):
            total += z2_s[u, k].astype(F32)
        at[...] = total.astype(BF)
        copies, local = unit_gather(u)
        each(copies, "start")
        local.start()

    def unit5(u):
        copies, local = unit_gather(u)
        each(copies, "wait")
        local.wait()
        each(unit_gather_core(u), "start")

    @pl.loop(0, d // RB)
    def _(i):
        a_s[rows_at(i, RB), :] = mm_tn(mg_s[0:n, cols_at(i, RB)], gmix_s[...])

    reorder(sbg_s, a_s, 1 - core)
    unit_core(4).start()
    reorder(raw_of(4), a_s, core)

    each(x_copies(), "wait_recv")
    for p in pairs:

        @pl.loop(0, 4)
        def _(q, p=p):
            add_into(p[1].at[3, rows_at(q, quarter)], p[3].at[rows_at(q, quarter)])

    @pl.loop(0, t // RB)
    def _(i):
        rows = rows_at(i, RB)
        mg_s[rows, :] = mm_nt(gmix_s[rows, :], wo_s[...]).astype(BF)

    def z_copies(j):
        p = pairs[j]
        return [
            remote(p[1].at[3, rows_at(peers[k], quarter)], p[5].at[k - 1], at_z[k], ZG + 3 * j + k - 1)
            for k in range(1, 4)
        ]

    def y_end(j):
        p = pairs[j]
        y_copies()[j].wait_recv()

        @pl.loop(0, 4)
        def _(q):
            add_into(p[1].at[3, rows_at(q, quarter)], p[4].at[rows_at(q, quarter)])

        each(z_copies(j), "start")

    y_end(0)

    down_second = [
        remote(d1_s.at[q, 0], d2_s.at[q], at_x if q % 2 else at_y, DY + q) for q in range(4)
    ]
    down_z = [
        remote(d1_s.at[peers[k], 1], zd_s.at[k - 1], at_z[k], ZD + k - 1) for k in range(1, 4)
    ]

    def down_first_end():
        for q in range(4):
            for e in range(2):
                remote(d1_s.at[q, e], d1_s.at[q, e], at_x, DX + 2 * q + e).wait()
            add_into(d1_s.at[q, 0], cd_s.at[q, rows_at(by_x if q % 2 else by_y, dr)])
            add_into(d1_s.at[q, 1], cd_s.at[q, rows_at(xy, dr)])
        each(down_second, "start")

    def down_second_end():
        each(down_second, "wait")
        for q in range(4):
            add_into(d1_s.at[q, 1], d2_s.at[q])
        each(down_z, "start")

    def gather(src, view, base, first_local):
        return [
            remote(src, view(xy, core), peer, base + k)
            for k, peer in enumerate((at_x, at_y, at_xy))
        ], pltpu.make_async_copy(src, view(xy, core), local_sem.at[first_local])

    def gather_core(view, base):
        return [remote(view(k, core), view(k, core), at_core, base + k) for k in range(4)]

    view_dg = lambda k, c: odg_h.at[:, cols_at(2 * k + c, h)]
    view_du = lambda k, c: odu_h.at[:, cols_at(2 * k + c, h)]
    view_dd = lambda k, c: odd_h.at[rows_at(4 * c + k, dr)]
    gathers = [
        gather(cg_s.at[3, rows_at(me, quarter)], view_dg, GA, 10),
        gather(cu_s.at[3, rows_at(me, quarter)], view_du, GA + 3, 11),
        gather(d1_s.at[me, 1], view_dd, GA + 6, 12),
    ]
    core_gathers = (
        gather_core(view_dg, GC) + gather_core(view_du, GC + 4) + gather_core(view_dd, GC + 8)
    )

    def first_norm(rows):
        u, r = unit_rows(cot_s[rows, :].astype(F32))
        n1t = (u * g1_ref[...]).T.astype(BF)
        for q in range(4):
            for k in range(4):
                to, fr = (4 * k + pos(q)) * step48, (4 * q + k) * step48
                n2t_s[to : to + step48, rows] = n1t[fr : fr + step48]
        return u, r

    def token_rows(slot, rows, at):
        g = mm_nt(proj_s[slot, at, 0:d], w0_s[...])
        g += mm_nt(proj_s[slot, at, d : 2 * d], w1_s[...])
        g += mm_nt(proj_s[slot, at, 2 * d : 3 * d], w2_s[...])
        u, r = first_norm(rows)
        small_s[0:1, :] += jnp.sum(g * u, axis=0, keepdims=True)
        gmix_s[rows, :] = (
            gmix_s[rows, :].astype(F32) + unit_back(g, u, r, g1_ref[...])
        ).astype(BF)

    each(loads[5:], "wait")
    each(x_loads, "wait")

    @pl.loop(0, 2)
    def _(slot):
        share = jnp.where(slot == 0, 1.0, 0.5)
        for j in range(4):
            slot_load(slot, j).wait()
        pl.when(slot == 1)(pair_copy.wait)
        gm_at = pl.ds(pl.multiple_of(slot * n, RB), t)

        @pl.loop(0, d // CB)
        def _(c):
            mult = lanes(mult_ref, CB)
            cols = cols_at(c, CB)
            query = q_s[:, cols].astype(F32)
            gm = mg_s[gm_at, cols].astype(F32)
            a_s[0:t, cols] = gm * filt_s[:, cols].astype(F32)
            spec = mm(tab_s[...], (gm * query).astype(BF)) * isp
            ss = ss_s[:, cols].astype(F32)
            th = th_s[:, cols]
            g_gain = spec[:f] * ss[:f] + spec[f:] * ss[f:]
            g_pre = (g_gain * (1.0 - th * th)).astype(BF)
            gpre_s[:, cols] = g_pre
            weighted = g_pre.astype(F32) * mult
            small_s[13:14, cols] += share * jnp.sum(weighted, axis=0, keepdims=True)
            g = (1.0 + th) * mult
            yy = jnp.concatenate(
                [(g * spec[:f]).astype(BF), (g * spec[f:]).astype(BF)], axis=0
            )
            b_s[0:t, cols] = mm(tabt_s[...], yy)

        @pl.when(slot == 0)
        def _():
            for j in range(4):
                slot_load(1, j).start()
            y_end(1)
            unit1(4)

        @pl.when(slot == 1)
        def _():
            for j, p in enumerate(pairs):
                each(z_copies(j), "wait")
                rows = rows_at(me, quarter)
                total = p[1][3, rows, :].astype(F32)
                for k in range(3):
                    total += p[5][k].astype(F32)
                p[1][3, rows, :] = total.astype(BF)
            for copies, local in gathers[:2]:
                each(copies, "start")
                local.start()
            down_second_end()
            unit3(4)

        for j in range(4, 8):
            slot_load(slot, j).wait()

        @pl.loop(0, d // CB)
        def _(c):
            m1, m2 = lanes(m1_ref, CB), lanes(m2_ref, CB)
            cols = cols_at(c, CB)
            g_feat = mm_nt(gpre_s[...], wc_s[cols, :])
            xc = cs_s[:, cols].astype(F32)
            power = (xc[:f] * xc[:f] + xc[f:] * xc[f:]) * isp
            g_pow = g_feat / (1.0 + power) * (lanes(mult_ref, CB) * (2.0 * isp))
            yy = jnp.concatenate(
                [(g_pow * xc[:f]).astype(BF), (g_pow * xc[f:]).astype(BF)], axis=0
            )
            g_cond = mm(tabt_s[...], yy)
            feat = (feat_s[:, cols].astype(F32) * lanes(mult_ref, CB)).astype(BF)
            dwc = share * mm_tn(feat, gpre_s[...])

            @pl.when(slot == 0)
            def _():
                u_s[cols, :] = dwc

            @pl.when(slot == 1)
            def _():
                u_s[cols, :] += dwc

            def finish(part, g_conv, p):
                at = cols_at(c, CB, part * d)
                back, sums = conv_back(g_conv, p, st_ref[:, at], m1, m2)
                for j in range(3):
                    row = 1 + 3 * j + part
                    small_s[row : row + 1, cols] += share * sums[j]
                proj_s[slot, :, at] = back.astype(BF)

            finish(0, a_s[0:t, cols], proj_s[slot, :, cols].astype(F32))
            key_cols, value_cols = cols_at(c, CB, d), cols_at(c, CB, 2 * d)
            p_value = proj_s[slot, :, value_cols].astype(F32)
            value = v_s[:, cols].astype(F32)
            g_sig = b_s[0:t, cols]
            p_key = proj_s[slot, :, key_cols].astype(F32)
            key = k_s[:, cols].astype(F32)
            finish(1, g_sig * value, p_key)
            back, sums = conv_back(g_cond, value, ct_ref[:, cols], m1, m2)
            for j in range(3):
                small_s[10 + j : 11 + j, cols] += share * sums[j]
            finish(2, g_sig * key + back, p_value)

        @pl.when(slot == 0)
        def _():
            for j in range(4, 8):
                slot_load(1, j).start()
            each(win_loads, "wait")
            down_first_end()
            unit2(4)

            @pl.loop(0, t // RB)
            def _(i):
                token_rows(slot, rows_at(i, RB), rows_at(i, RB))

            home_start(gmix_s, gtok6_h, 0, GT0, 2)

    each(down_z, "wait")
    total = d1_s[me, 1].astype(F32)
    for k in range(3):
        total += zd_s[k].astype(F32)
    d1_s[me, 1] = total.astype(BF)
    each(gathers[2][0], "start")
    gathers[2][1].start()

    def win_product(u, which, dst):
        cols = cols_at(3 * which + u - 1, h)

        @pl.loop(0, d // RB)
        def _(i):
            rows = rows_at(i, RB)
            dw = mm(n2t_s[rows, 0:RB], proj_s[0, 0:RB, cols])
            dw += mm(n2t_s[rows, RB : 2 * RB], proj_s[0, RB : 2 * RB, cols])
            dw += mm(n2t_s[rows, 2 * RB : 3 * RB], proj_s[1, half_at, cols])
            dst[rows, :] = dw.astype(BF)

    reorder(sbg_s, u_s, 1 - core)
    unit_core(0).start()
    reorder(raw_of(0), u_s, core)
    last_rows = slice(t, n)
    first_norm(last_rows)
    unit4(4)
    win_product(1, 1 - core, sbu_s)
    unit_core(1).start()
    win_product(1, core, raw_of(1))
    unit1(0)
    win_product(2, 1 - core, sbg_s)
    unit_core(2).start()
    win_product(2, core, raw_of(2))
    unit1(1)
    unit2(0)
    win_product(3, 1 - core, sbu_s)
    unit_core(3).start()
    win_product(3, core, raw_of(3))
    unit1(2)
    unit2(1)
    unit3(0)
    unit5(4)
    token_rows(1, last_rows, half_at)
    small_c = remote(small_s, sgot_s.at[0], at_core, SMALL)
    small_c.start()
    unit1(3)
    unit2(2)
    unit3(1)
    home_start(gmix_s, gtok6_h, 1, GT1, 3)
    unit4(0)
    small_c.wait()
    ssum_s[0] = small_s[...] + sgot_s[0]
    small_x = remote(ssum_s.at[0], sgot_s.at[1], at_x, SMALL + 1)
    small_x.start()
    unit2(3)
    unit3(2)
    each([c for copies, _ in gathers for c in copies], "wait")
    each([local for _, local in gathers], "wait")
    each(core_gathers, "start")
    unit4(1)
    unit5(0)
    small_x.wait()
    ssum_s[1] = ssum_s[0] + sgot_s[1]
    small_y = remote(ssum_s.at[1], sgot_s.at[2], at_y, SMALL + 2)
    small_y.start()
    unit3(3)
    unit4(2)
    unit5(1)
    small_y.wait()
    ssum_s[2] = ssum_s[1] + sgot_s[2]
    small_z = [
        remote(ssum_s.at[2], sgot_s.at[2 + k], at_z[k], SMALL + 2 + k) for k in range(1, 4)
    ]
    each(small_z, "start")
    unit4(3)
    unit5(2)
    each(small_z, "wait")
    small_out[...] = ssum_s[2] + sgot_s[3] + sgot_s[4] + sgot_s[5]
    unit5(3)

    each(diag_copies(False) + diag_copies(True) + x_copies() + y_copies(), "wait_send")
    each(core_gathers, "wait")
    for u in range(5):
        each(unit_gather_core(u), "wait")
    home_wait(n2_s, lay6_h, 0, LAY, 0)
    home_wait(n2_s, lay6_h, 1, LAY + 3, 1)
    home_wait(gmix_s, gtok6_h, 0, GT0, 2)
    home_wait(gmix_s, gtok6_h, 1, GT1, 3)


def back(
    side, slots, kind, mixed, xs, cot, w_out, g2, w_gate, w_up, w_down,
    proj, filt, ss, cs, th, feat, query, key, value, st, ct, w_cond, table, table_t, g1, w_in,
):
    t, d = xs.shape[1:]
    n = t + t // 2
    f2 = table.shape[0]
    f = f2 // 2
    h, q4, dr, s48 = d // 2, d // 4, d // 8, d // 16
    hbm = pl.BlockSpec(memory_space=pl.ANY)
    vm = pl.BlockSpec(memory_space=pltpu.VMEM)
    smem = pl.BlockSpec(memory_space=pltpu.SMEM)
    b = lambda *s: pltpu.VMEM(s, BF)
    g = lambda *s: pltpu.VMEM(s, F32)
    return pl.pallas_call(
        functools.partial(back_kernel, side),
        name="back",
        out_shape=tuple(
            jax.ShapeDtypeStruct(s, BF)
            for s in (
                (slots, t // 4, d), (slots, t // 4, d), (q4, 4 * d), (q4, 4 * d), (d, d),
                (q4, d), (q4, d), (q4, 3 * d), (3, 4, n, d),
            )
        )
        + (jax.ShapeDtypeStruct((16, d), F32),),
        in_specs=[smem] + [hbm] * 4 + [vm] + [hbm] * 12 + [vm, vm, hbm, hbm, hbm, vm, hbm],
        out_specs=(hbm,) * 9 + (vm,),
        scratch_shapes=[
            g(n, d), g(n, d), g(n, d), g(n, 128),
            b(n, d), b(d, n), b(n, d), b(n + t, d), b(n, d),
            b(n, d), b(n, d), b(n, d), b(d, d), b(d, d), b(d, d), b(d, d), b(d, d),
            b(f2, t), b(t, f2), g(32, 128), g(32, 128), g(f, 128),
            b(d, h), b(d, h), b(h, d),
            b(4, d, h), b(4, d, h), b(4, h, d),
            b(d, h), b(d, h), b(d, h), b(d, h), b(d, h), b(d, h),
            b(3, q4, h), b(3, q4, h), b(4, 2, dr, d), b(4, dr, d), b(3, dr, d),
            b(2, t, 3 * d), b(t, d), b(f2, d), b(f2, d), g(f, d), b(f, d), b(t, d), b(t, d), b(t, d), b(f, d),
            b(5, d, h), b(3, d, h), b(5, q4, h), b(5, q4, h), b(5, q4, h), b(5, 3, s48, h),
            g(16, d), g(6, 16, d), g(3, 16, d),
            pltpu.SemaphoreType.DMA((21,)),
            pltpu.SemaphoreType.DMA((6,)),
            pltpu.SemaphoreType.DMA((3, 3)),
            pltpu.SemaphoreType.DMA((3,)),
            pltpu.SemaphoreType.DMA((169,)),
            pltpu.SemaphoreType.DMA((169,)),
            pltpu.SemaphoreType.DMA((13,)),
        ],
        compiler_params=pltpu.CompilerParams(
            collective_id=1, has_side_effects=True, vmem_limit_bytes=65400 * 1024
        ),
    )(
        kind, mixed, xs, cot, w_out, g2, w_gate, w_up, w_down, proj, filt, ss, cs, th, feat,
        query, key, value, st, ct, w_cond, table, table_t, g1, w_in,
    )


def on_device(
    tokens, kind, ln1_gain, w_in, short_taps, cond_taps, w_cond, cond_bias, w_out, ln2_gain,
    w_gate, w_up, w_down, cotangent,
):
    _, rows, slots, d = tokens.shape
    n = lax.axis_size("seq")
    dp_count = lax.axis_size("dp")
    rank = lax.axis_index("seq")
    tok6 = jnp.transpose(tokens[0], (1, 0, 2))
    cot6 = jnp.transpose(cotangent[0], (1, 0, 2))
    g1, g2 = ln1_gain.reshape(1, d), ln2_gain.reshape(1, d)
    xs, proj, mixed, filt, sig_spec, cond_spec, th, feat, query, key, value, table, table_t = front(
        kind, tok6, g1, w_in, short_taps, cond_taps, w_cond, cond_bias.reshape(1, d)
    )
    side = math.isqrt(dp_count // 2)
    lay6, gtok6, *sums, _, small = back(
        side, slots, kind, mixed, xs, cot6, w_out, g2, w_gate, w_up, w_down,
        proj, filt, sig_spec, cond_spec, th, feat, query, key, value, short_taps, cond_taps, w_cond,
        table, table_t, g1, w_in,
    )
    layer_out = jnp.transpose(lay6, (1, 0, 2))[None]
    grad_tokens = jnp.transpose(gtok6, (1, 0, 2))[None]

    sums = [a.astype(F32) for a in sums]
    if dp_count > 8:
        groups = [
            [
                (y * side + x) * 2 + core
                for y in range(y0, side, 2)
                for x in range(x0, side, 2)
            ]
            for y0 in range(2)
            for x0 in range(2)
            for core in range(2)
        ]
        sums = [lax.psum(a, "dp", axis_index_groups=groups) for a in sums]
        small = lax.psum(small, "dp", axis_index_groups=groups)
    grad_gate, grad_up, grad_down, grad_w_out, grad_w_cond, grad_w_in = sums
    part = lambda a, width: lax.dynamic_slice_in_dim(a, rank * width, width, a.ndim - 1)
    return (
        layer_out,
        grad_tokens,
        part(small[0], d // n),
        grad_w_in,
        part(small[1:10].reshape(3, 3 * d), 3 * d // n),
        part(small[10:13], d // n),
        grad_w_cond,
        part(small[13], d // n),
        grad_w_out,
        part(small[14], d // n),
        grad_gate,
        grad_up,
        grad_down,
    )


def solution(mesh):
    rows = P("dp", "seq", None, None)
    return jax.shard_map(
        on_device,
        mesh=mesh,
        in_specs=(rows, P("dp")) + (P(),) * 11 + (rows,),
        out_specs=(
            rows,
            rows,
            P("seq"),
            P("seq", None),
            P(None, "seq"),
            P(None, "seq"),
            P("seq", None),
            P("seq"),
            P("seq", None),
            P("seq"),
            P("seq", None),
            P("seq", None),
            P("seq", None),
        ),
        check_vma=False,
    )
```

time: 282 us -> 262 us (0.929)
  Pallas kernels: 261 us -> 240 us
    pallas_call x1, Pallas kernels: 206 us -> 194 us  [back(): pl.pallas_call(functools.partial(back_kernel, side), name='back', out_sha...]
    pallas_call x1, Pallas kernels: 54.7 us -> 46.9 us  [front(): pl.pallas_call(front_kernel, name='front', out_shape=(xs, *rest) + tuple(...]
where the time goes in v4:
time: 262 us; the launch traced here: 260 us
  Pallas kernels  240 us (92%)
  other arithmetic  9.3 us (4%)
  local copies, waits for them, and re-layouts  8.65 us (3%)
    pallas_call x1, Pallas kernels, back(): pl.pallas_call(functools.partial(back_kernel, side), name='back', out_sha...  194 us
    pallas_call x1, Pallas kernels, front(): pl.pallas_call(front_kernel, name='front', out_shape=(xs, *rest) + tuple(...  46.9 us
    convert_element_type x6, other arithmetic, on_device(): sums = [a.astype(F32) for a in sums]  9.3 us

profile of v4, /device:TPU:25, one launch (start us, length us, event | category | flops | bytes accessed | tf_op | source)
XLA Modules:
  0.0 259.8 jit_solution(6568377386383395079)
XLA Ops:
  0.6 1.3 reshape.41.g1_ref.refs_23_
  2.6 1.3 reshape.42.cb_ref
  3.8 0.0 copy-start.8
  3.8 46.9 %front.1 = (bf16[2,512,768]{2,1,0:T(8,128)(2,1)}, bf16[2,512,2304]{2,1,0:T(8,128)(2,1)}, bf16[2,512,768]{2,1,0:T(8,128)(2,1)}, bf16[2,512,768]{2,1,0:T(8,128)(2,...) custom-call(s32[1]{0:T(128)S(6)} %copy.29.kind_ref.refs_0_, ...), custom_call_target="tpu_custom_call" | custom-call | tf_op jit(solution)/shard_map/front/pallas_call | solution.py:296
  50.8 0.0 copy-done.8
  50.8 0.6 reshape.43.refs_5_
  51.4 193.6 %back.1 = (bf16[6,128,768]{2,1,0:T(8,128)(2,1)}, bf16[6,128,768]{2,1,0:T(8,128)(2,1)}, bf16[192,3072]{1,0:T(8,128)(2,1)}, bf16[192,3072]{1,0:T(8,128)(2,1)}, bf1...) custom-call(s32[1]{0:T(128)S(6)} %copy.29.kind_ref.refs_0_, ...), custom_call_target="tpu_custom_call" | custom-call | tf_op jit(solution)/shard_map/back/pallas_call | solution.py:1109
  244.9 0.8 fusion
  245.8 0.6 constant_dynamic-slice_fusion
  246.4 3.0 %convert_element_type.21 = f32[192,3072]{1,0:T(8,128)} convert(bf16[192,3072]{1,0:T(8,128)(2,1)} %get-tuple-element.54) | non-fusion elementwise | flops 589824 | bytes 3538944 | tf_op jit(solution)/shard_map/convert_element_type | solution.py:1174
  249.4 0.0 copy-done.1
  249.4 0.0 copy-start
  249.4 1.7 convert_element_type.22
  251.1 0.0 copy-done
  251.1 0.0 copy-start.4
  251.1 1.6 convert_element_type.23
  252.7 0.0 copy-start.6
  252.7 0.0 copy-done.4
  252.7 0.0 copy-start.5
  252.7 1.3 convert_element_type.18
  254.0 0.0 copy-done.6
  254.0 0.9 convert_element_type.19
  254.9 0.0 copy-done.5
  254.9 0.9 convert_element_type.20
  255.7 0.0 copy-done.7
  255.8 0.7 constant_dynamic-slice_fusion.3
  256.5 0.7 constant_dynamic-slice_fusion.2
  257.1 0.6 constant_dynamic-slice_fusion.4
  257.8 0.0 copy-done.3
  257.8 1.0 copy.30
  258.8 0.0 copy-done.2
  258.8 1.0 copy.31
  (7 shorter events, 0.0 us)
Async XLA Ops:
  3.8 46.9 %copy-start.8 = (f32[768]{0:T(1024)S(1)}, f32[768]{0:T(1024)}, u32[]{:S(2)}) copy-start(f32[768]{0:T(1024)} %param.23) | copy-start | bytes 9220
  246.4 3.0 %copy-start.1 = (bf16[192,3072]{1,0:T(8,128)(2,1)S(1)}, bf16[192,3072]{1,0:T(8,128)(2,1)}, u32[]{:S(2)}) copy-start(bf16[192,3072]{1,0:T(8,128)(2,1)} %get-tuple-element.55) | copy-start | bytes 3538948
  249.4 1.7 copy-start
  251.1 1.6 copy-start.4
  252.7 1.3 copy-start.6
  252.7 2.2 copy-start.5
  252.7 3.0 %copy-start.7 = (f32[16,768]{1,0:T(8,128)S(1)}, f32[16,768]{1,0:T(8,128)}, u32[]{:S(2)}) copy-start(f32[16,768]{1,0:T(8,128)} %get-tuple-element.50) | copy-start | bytes 147460
  254.0 3.7 %copy-start.3 = (bf16[6,128,768]{2,1,0:T(8,128)(2,1)S(1)}, bf16[6,128,768]{2,1,0:T(8,128)(2,1)}, u32[]{:S(2)}) copy-start(bf16[6,128,768]{2,1,0:T(8,128)(2,1)} %get-tuple-element.48) | copy-start | bytes 3538948
  254.9 3.9 %copy-start.2 = (bf16[6,128,768]{2,1,0:T(8,128)(2,1)S(1)}, bf16[6,128,768]{2,1,0:T(8,128)(2,1)}, u32[]{:S(2)}) copy-start(bf16[6,128,768]{2,1,0:T(8,128)(2,1)} %get-tuple-element.49) | copy-start | bytes 3538948

commit v5 on v4

--- a/solution.py
+++ b/solution.py
@@ -220,17 +220,17 @@
         def _(r):
             rows = pl.ds(pl.multiple_of(r * 128, 128), 128)
             u, _ = unit_rows(x_s[slot, rows, :].astype(F32))
-            n1_s[rows, :] = (u * g1_ref[...]).astype(BF)
-
-        @pl.loop(0, d // CB)
+            n1_s[rows, :] = (u * g1_ref[...].reshape(1, d)).astype(BF)
+
+        @pl.loop(0, d // d)
         def _(c):
-            m1, m2 = lanes(m1_ref, CB), lanes(m2_ref, CB)
-            own = cols_at(c, CB)
+            m1, m2 = lanes(m1_ref, d), lanes(m2_ref, d)
+            own = cols_at(c, d)
 
             def part(k):
-                cols = cols_at(c, CB, k * d)
+                cols = cols_at(c, d, k * d)
                 p = mm(n1_s[...], win_s[:, cols]).astype(BF)
-                proj_s[slot, :, cols] = p
+                proj_s[slot, k, :, own] = p
                 return conv(p.astype(F32), st_ref[:, cols], m1, m2)
 
             query = part(0)
@@ -257,12 +257,12 @@
             across.wait()
             handed.start()
 
-        @pl.loop(0, d // CB)
+        @pl.loop(0, d // d)
         def _(c):
-            own = cols_at(c, CB)
-            th = jnp.tanh(mm(feat_s[slot], wc_s[:, own]) + cb_ref[:, own])
+            own = cols_at(c, d)
+            th = jnp.tanh(mm(feat_s[slot], wc_s[:, own]) + cb_ref[...].reshape(1, d))
             th_s[slot, :, own] = th
-            g = (1.0 + th) * lanes(ms_s, CB)
+            g = (1.0 + th) * lanes(ms_s, d)
             xs = ss_s[slot, :, own].astype(F32)
             y = jnp.concatenate([(g * xs[:f]).astype(BF), (g * xs[f:]).astype(BF)], axis=0)
             filt = mm(tabt_s[...], y)
@@ -287,7 +287,7 @@
     vm = pl.BlockSpec(memory_space=pltpu.VMEM)
     smem = pl.BlockSpec(memory_space=pltpu.SMEM)
     per_slot = [
-        ((2, t, d), BF), ((2, t, 3 * d), BF), ((2, t, d), BF), ((2, t, d), BF),
+        ((2, t, d), BF), ((2, 3, t, d), BF), ((2, t, d), BF), ((2, t, d), BF),
         ((2, 2 * f, d), BF), ((2, 2 * f, d), BF), ((2, f, d), F32), ((2, f, d), BF),
         ((2, t, d), BF), ((2, t, d), BF), ((2, t, d), BF),
     ]
@@ -330,10 +330,10 @@
         st_ref, ct_ref, wc_h, tab_h, tabt_h, g1_ref, win_h,
         lay6_h, gtok6_h, odg_h, odu_h, odd_h, owo_h, owc_h, owi_h, spool_h, small_out,
         a_s, b_s, u_s, r_s, n2_s, n2t_s, cot_s, mg_s, gmix_s,
-        act_s, gg_s, gu_s, w0_s, w1_s, w2_s, wo_s, wc_s, tab_s, tabt_s, m1_ref, m2_ref, mult_ref,
+        act_s, gg_s, gu_s, wall_s, wo_s, wc_s, tab_s, tabt_s, m1_ref, m2_ref, mult_ref,
         sbg_s, sbu_s, sbd_s, cg_s, cu_s, cd_s,
         dgg_s, dgu_s, xg_s, xu_s, yg_s, yu_s, zg_s, zu_s, d1_s, d2_s, zd_s,
-        proj_s, filt_s, ss_s, cs_s, th_s, feat_s, q_s, k_s, v_s, gpre_s,
+        filt_s, ss_s, cs_s, th_s, feat_s, q_s, k_s, v_s, gpre_s,
         c2_s, raw2_s, rd_s, rx_s, ry_s, z2_s, small_s, sgot_s, ssum_s,
         load_sem, w_sem, spool_sem, back_sem, send_sem, recv_sem, local_sem,
     ) = refs
@@ -383,7 +383,8 @@
         row_moves(mixed_h, mg_s)
         + row_moves(xs_h, gmix_s)
         + [(wo_h, wo_s)]
-        + [(tab_h, tab_s), (tabt_h, tabt_s), (wc_h, wc_s), (proj_h, proj_s)]
+        + [(tab_h, tab_s), (tabt_h, tabt_s), (wc_h, wc_s)]
+        + [(proj_h, wall_s.at[pl.ds(3 * d, 6 * t)])]
     )
     loads = [pltpu.make_async_copy(s, e, load_sem.at[j]) for j, (s, e) in enumerate(moves)]
     slot_moves = [
@@ -398,24 +399,28 @@
         for j, (a, b) in enumerate(row_moves(xs_h, cot_s))
     ]
 
-    def weights(s):
+    def weight(k, b):
+        return pl.ds(pl.multiple_of((3 * b + k) * d, RB), d)
+
+    def weights(s, b):
         cols = cols_at(owner(s), d)
         return [
-            pltpu.make_async_copy(wg_h.at[:, cols], w0_s, w_sem.at[0]),
-            pltpu.make_async_copy(wu_h.at[:, cols], w1_s, w_sem.at[1]),
-            pltpu.make_async_copy(wd_h.at[cols, :], w2_s, w_sem.at[2]),
+            pltpu.make_async_copy(src, wall_s.at[weight(k, b)], w_sem.at[b, k])
+            for k, src in enumerate((wg_h.at[:, cols], wu_h.at[:, cols], wd_h.at[cols, :]))
         ]
 
     win_loads = [
-        pltpu.make_async_copy(win_h.at[:, k * d : (k + 1) * d], w, w_sem.at[3 + k])
-        for k, w in enumerate((w0_s, w1_s, w2_s))
+        pltpu.make_async_copy(
+            win_h.at[:, k * d : (k + 1) * d], wall_s.at[weight(k, 0)], w_sem.at[2, k]
+        )
+        for k in range(3)
     ]
 
+    def proj_rows(slot, part, offset, size):
+        return pl.ds(pl.multiple_of(3 * d + (3 * slot + part) * t + offset, RB), size)
+
     each(loads[:5], "start")
-    each(weights(3), "start")
-    each(loads[5:], "start")
-    for j in range(8):
-        slot_load(0, j).start()
+    each(weights(3, 0), "start")
 
     barrier = pltpu.get_barrier_semaphore()
     everyone = [at_core, at_x, at_y, at_xy] + at_z[1:]
@@ -471,9 +476,13 @@
         u, r = unit_rows(hid)
         u_s[rows, :] = u
         r_s[rows, :] = jnp.broadcast_to(r, (RB, 128))
-        n2 = u * g2_ref[...]
+        n2 = u * g2_ref[...].reshape(1, d)
         n2_s[rows, :] = n2.astype(BF)
         n2t_s[:, rows] = n2.T.astype(BF)
+
+    each(loads[5:-1], "start")
+    for j in range(8):
+        slot_load(0, j).start()
 
     pairs = ((sbg_s, cg_s, dgg_s, xg_s, yg_s, zg_s), (sbu_s, cu_s, dgu_s, xu_s, yu_s, zu_s))
     rank_rows = lambda q: pl.ds(q * quarter, quarter)
@@ -529,8 +538,12 @@
 
     @pl.loop(0, 4)
     def _(p):
-        s = 3 - p
-        each(weights(s), "wait")
+        s, b = 3 - p, lax.rem(p, 2)
+        each(weights(s, b), "wait")
+
+        @pl.when(p < 3)
+        def _():
+            each(weights(s - 1, 1 - b), "start")
 
         @pl.loop(0, n // RB)
         def _(i):
@@ -542,24 +555,20 @@
                     spool(s, i, j).wait()
 
             n2 = n2_s[rows, :]
-            pre = mm(n2, w0_s[...])
-            lin = mm(n2, w1_s[...])
+            pre = mm(n2, wall_s[weight(0, b), :])
+            lin = mm(n2, wall_s[weight(1, b), :])
             sg = 1.0 / (1.0 + jnp.exp(-pre))
             silu = pre * sg
             act = (silu * lin).astype(BF)
             act_s[rows, :] = act
             gu_s[rows, :] = silu.astype(BF)
             gg_s[rows, :] = (lin * sg * (1.0 + pre * (1.0 - sg))).astype(BF)
-            a_s[rows, :] += mm(act, w2_s[...])
+            a_s[rows, :] += mm(act, wall_s[weight(2, b), :])
 
             @pl.when(p < 3)
             def _():
                 for j in range(3):
                     spool(s, i, j).start()
-
-        @pl.when(p < 3)
-        def _():
-            each(weights(s - 1), "start")
 
     @pl.loop(0, n // RB)
     def _(i):
@@ -614,25 +623,34 @@
 
     @pl.loop(0, 4)
     def _(s):
+        b = lax.rem(s + 1, 2)
+
         @pl.when(s > 0)
         def _():
-            each(weights(s), "wait")
+            each(weights(s, b), "wait")
+
+        @pl.when(s < 3)
+        def _():
+            each(weights(s + 1, 1 - b), "start")
+
+        pl.when(s == 3)(loads[-1].start)
+
+        @pl.when(s > 0)
+        def _():
             unspool(s, 1).wait()
             unspool(s, 2).wait()
 
         @pl.loop(0, n // RB)
         def _(i):
             rows = rows_at(i, RB)
-            g_act = mm_nt(cot_s[rows, :], w2_s[...])
+            g_act = mm_nt(cot_s[rows, :], wall_s[weight(2, b), :])
             g_up = (g_act * gu_s[rows, :].astype(F32)).astype(BF)
             gu_s[rows, :] = g_up
             g_gate = (g_act * gg_s[rows, :].astype(F32)).astype(BF)
             gg_s[rows, :] = g_gate
-            b_s[rows, :] += mm_nt(g_gate, w0_s[...]) + mm_nt(g_up, w1_s[...])
-
-        @pl.when(s < 3)
-        def _():
-            each(weights(s + 1), "start")
+            b_s[rows, :] += mm_nt(g_gate, wall_s[weight(0, b), :]) + mm_nt(
+                g_up, wall_s[weight(1, b), :]
+            )
 
         @pl.when(s > 0)
         def _():
@@ -682,7 +700,7 @@
         rows = rows_at(i, RB)
         g, u = b_s[rows, :], u_s[rows, :]
         small_s[14:15, :] += jnp.sum(g * u, axis=0, keepdims=True)
-        gh = cot_s[rows, :].astype(F32) + unit_back(g, u, r_s[rows, 0:1], g2_ref[...])
+        gh = cot_s[rows, :].astype(F32) + unit_back(g, u, r_s[rows, 0:1], g2_ref[...].reshape(1, d))
         gmix_s[rows, :] = gh.astype(BF)
 
     each(x_loads, "start")
@@ -869,23 +887,20 @@
         gather_core(view_dg, GC) + gather_core(view_du, GC + 4) + gather_core(view_dd, GC + 8)
     )
 
-    def first_norm(rows):
-        u, r = unit_rows(cot_s[rows, :].astype(F32))
-        n1t = (u * g1_ref[...]).T.astype(BF)
+    def keep_norm(u, rows):
+        n1t = (u * g1_ref[...].reshape(1, d)).T.astype(BF)
         for q in range(4):
             for k in range(4):
                 to, fr = (4 * k + pos(q)) * step48, (4 * q + k) * step48
                 n2t_s[to : to + step48, rows] = n1t[fr : fr + step48]
-        return u, r
-
-    def token_rows(slot, rows, at):
-        g = mm_nt(proj_s[slot, at, 0:d], w0_s[...])
-        g += mm_nt(proj_s[slot, at, d : 2 * d], w1_s[...])
-        g += mm_nt(proj_s[slot, at, 2 * d : 3 * d], w2_s[...])
-        u, r = first_norm(rows)
+
+    def token_rows(slot, rows, offset, u, r):
+        g = jnp.zeros((RB, d), F32)
+        for part in range(3):
+            g += mm_nt(wall_s[proj_rows(slot, part, offset, RB), :], wall_s[weight(part, 0), :])
         small_s[0:1, :] += jnp.sum(g * u, axis=0, keepdims=True)
         gmix_s[rows, :] = (
-            gmix_s[rows, :].astype(F32) + unit_back(g, u, r, g1_ref[...])
+            gmix_s[rows, :].astype(F32) + unit_back(g, u, r, g1_ref[...].reshape(1, d))
         ).astype(BF)
 
     each(loads[5:], "wait")
@@ -941,6 +956,7 @@
                 local.start()
             down_second_end()
             unit3(4)
+            home_start(gmix_s, gtok6_h, 0, GT0, 2)
 
         for j in range(4, 8):
             slot_load(slot, j).wait()
@@ -974,20 +990,18 @@
                 for j in range(3):
                     row = 1 + 3 * j + part
                     small_s[row : row + 1, cols] += share * sums[j]
-                proj_s[slot, :, at] = back.astype(BF)
-
-            finish(0, a_s[0:t, cols], proj_s[slot, :, cols].astype(F32))
-            key_cols, value_cols = cols_at(c, CB, d), cols_at(c, CB, 2 * d)
-            p_value = proj_s[slot, :, value_cols].astype(F32)
+                wall_s[proj_rows(slot, part, 0, t), cols] = back.astype(BF)
+
+            projected = lambda part: wall_s[proj_rows(slot, part, 0, t), cols].astype(F32)
+            finish(0, a_s[0:t, cols], projected(0))
             value = v_s[:, cols].astype(F32)
             g_sig = b_s[0:t, cols]
-            p_key = proj_s[slot, :, key_cols].astype(F32)
             key = k_s[:, cols].astype(F32)
-            finish(1, g_sig * value, p_key)
+            finish(1, g_sig * value, projected(1))
             back, sums = conv_back(g_cond, value, ct_ref[:, cols], m1, m2)
             for j in range(3):
                 small_s[10 + j : 11 + j, cols] += share * sums[j]
-            finish(2, g_sig * key + back, p_value)
+            finish(2, g_sig * key + back, projected(2))
 
         @pl.when(slot == 0)
         def _():
@@ -999,35 +1013,31 @@
 
             @pl.loop(0, t // RB)
             def _(i):
-                token_rows(slot, rows_at(i, RB), rows_at(i, RB))
-
-            home_start(gmix_s, gtok6_h, 0, GT0, 2)
-
-    each(down_z, "wait")
-    total = d1_s[me, 1].astype(F32)
-    for k in range(3):
-        total += zd_s[k].astype(F32)
-    d1_s[me, 1] = total.astype(BF)
-    each(gathers[2][0], "start")
-    gathers[2][1].start()
+                rows = rows_at(i, RB)
+                u, r = unit_rows(cot_s[rows, :].astype(F32))
+                keep_norm(u, rows)
+                token_rows(0, rows, i * RB, u, r)
 
     def win_product(u, which, dst):
-        cols = cols_at(3 * which + u - 1, h)
+        at = 3 * which + u - 1
+        part, cols = at // 2, cols_at(lax.rem(at, 2), h)
+        blocks = [(0, 0), (0, RB), (1, half * RB)]
 
         @pl.loop(0, d // RB)
         def _(i):
             rows = rows_at(i, RB)
-            dw = mm(n2t_s[rows, 0:RB], proj_s[0, 0:RB, cols])
-            dw += mm(n2t_s[rows, RB : 2 * RB], proj_s[0, RB : 2 * RB, cols])
-            dw += mm(n2t_s[rows, 2 * RB : 3 * RB], proj_s[1, half_at, cols])
+            dw = jnp.zeros((RB, h), F32)
+            for k, (slot, offset) in enumerate(blocks):
+                g = wall_s[proj_rows(slot, part, offset, RB), cols]
+                dw += mm(n2t_s[rows, k * RB : (k + 1) * RB], g)
             dst[rows, :] = dw.astype(BF)
 
     reorder(sbg_s, u_s, 1 - core)
     unit_core(0).start()
     reorder(raw_of(0), u_s, core)
     last_rows = slice(t, n)
-    first_norm(last_rows)
-    unit4(4)
+    u1, r1 = unit_rows(cot_s[last_rows, :].astype(F32))
+    keep_norm(u1, last_rows)
     win_product(1, 1 - core, sbu_s)
     unit_core(1).start()
     win_product(1, core, raw_of(1))
@@ -1043,8 +1053,16 @@
     unit1(2)
     unit2(1)
     unit3(0)
-    unit5(4)
-    token_rows(1, last_rows, half_at)
+    each(down_z, "wait")
+    total = d1_s[me, 1].astype(F32)
+    for k in range(3):
+        total += zd_s[k].astype(F32)
+    d1_s[me, 1] = total.astype(BF)
+    each(gathers[2][0], "start")
+    gathers[2][1].start()
+    unit4(4)
+    u1, r1 = unit_rows(cot_s[last_rows, :].astype(F32))
+    token_rows(1, last_rows, half * RB, u1, r1)
     small_c = remote(small_s, sgot_s.at[0], at_core, SMALL)
     small_c.start()
     unit1(3)
@@ -1063,6 +1081,7 @@
     each(core_gathers, "start")
     unit4(1)
     unit5(0)
+    unit5(4)
     small_x.wait()
     ssum_s[1] = ssum_s[0] + sgot_s[1]
     small_y = remote(ssum_s.at[1], sgot_s.at[2], at_y, SMALL + 2)
@@ -1122,17 +1141,17 @@
         scratch_shapes=[
             g(n, d), g(n, d), g(n, d), g(n, 128),
             b(n, d), b(d, n), b(n, d), b(n + t, d), b(n, d),
-            b(n, d), b(n, d), b(n, d), b(d, d), b(d, d), b(d, d), b(d, d), b(d, d),
+            b(n, d), b(n, d), b(n, d), b(3 * d + 6 * t, d), b(d, d), b(d, d),
             b(f2, t), b(t, f2), g(32, 128), g(32, 128), g(f, 128),
             b(d, h), b(d, h), b(h, d),
             b(4, d, h), b(4, d, h), b(4, h, d),
             b(d, h), b(d, h), b(d, h), b(d, h), b(d, h), b(d, h),
             b(3, q4, h), b(3, q4, h), b(4, 2, dr, d), b(4, dr, d), b(3, dr, d),
-            b(2, t, 3 * d), b(t, d), b(f2, d), b(f2, d), g(f, d), b(f, d), b(t, d), b(t, d), b(t, d), b(f, d),
+            b(t, d), b(f2, d), b(f2, d), g(f, d), b(f, d), b(t, d), b(t, d), b(t, d), b(f, d),
             b(5, d, h), b(3, d, h), b(5, q4, h), b(5, q4, h), b(5, q4, h), b(5, 3, s48, h),
             g(16, d), g(6, 16, d), g(3, 16, d),
             pltpu.SemaphoreType.DMA((21,)),
-            pltpu.SemaphoreType.DMA((6,)),
+            pltpu.SemaphoreType.DMA((3, 3)),
             pltpu.SemaphoreType.DMA((3, 3)),
             pltpu.SemaphoreType.DMA((3,)),
             pltpu.SemaphoreType.DMA((169,)),
@@ -1158,15 +1177,14 @@
     rank = lax.axis_index("seq")
     tok6 = jnp.transpose(tokens[0], (1, 0, 2))
     cot6 = jnp.transpose(cotangent[0], (1, 0, 2))
-    g1, g2 = ln1_gain.reshape(1, d), ln2_gain.reshape(1, d)
     xs, proj, mixed, filt, sig_spec, cond_spec, th, feat, query, key, value, table, table_t = front(
-        kind, tok6, g1, w_in, short_taps, cond_taps, w_cond, cond_bias.reshape(1, d)
+        kind, tok6, ln1_gain, w_in, short_taps, cond_taps, w_cond, cond_bias
     )
     side = math.isqrt(dp_count // 2)
     lay6, gtok6, *sums, _, small = back(
-        side, slots, kind, mixed, xs, cot6, w_out, g2, w_gate, w_up, w_down,
-        proj, filt, sig_spec, cond_spec, th, feat, query, key, value, short_taps, cond_taps, w_cond,
-        table, table_t, g1, w_in,
+        side, slots, kind, mixed, xs, cot6, w_out, ln2_gain, w_gate, w_up, w_down,
+        proj.reshape(-1, d), filt, sig_spec, cond_spec, th, feat, query, key, value, short_taps, cond_taps, w_cond,
+        table, table_t, ln1_gain, w_in,
     )
     layer_out = jnp.transpose(lay6, (1, 0, 2))[None]
     grad_tokens = jnp.transpose(gtok6, (1, 0, 2))[None]

time: 262 us -> 250 us (0.954)
  Pallas kernels: 240 us -> 230 us
  local copies, waits for them, and re-layouts: 8.65 us -> 5.53 us
    pallas_call x1, Pallas kernels: 194 us -> 188 us  [back(): pl.pallas_call(functools.partial(back_kernel, side), name='back', out_sha...]
    pallas_call x1, Pallas kernels: 46.9 us -> 42.1 us  [front(): pl.pallas_call(front_kernel, name='front', out_shape=(xs, *rest) + tuple(...]
    reshape x3 -> x0, local copies, waits for them, and re-layouts: 3.12 us -> none  [the longest x2 1.85 us: on_device(): g1, g2 = (ln1_gain.reshape(1, d), ln2_gain.reshape(1, d))]
where the time goes in v5:
time: 250 us; the launch traced here: 246 us
  Pallas kernels  230 us (92%)
  other arithmetic  9.3 us (4%)
  local copies, waits for them, and re-layouts  5.53 us (2%)
    pallas_call x1, Pallas kernels, back(): pl.pallas_call(functools.partial(back_kernel, side), name='back', out_sha...  188 us
    pallas_call x1, Pallas kernels, front(): pl.pallas_call(front_kernel, name='front', out_shape=(xs, *rest) + tuple(...  42.1 us
    convert_element_type x6, other arithmetic, on_device(): sums = [a.astype(F32) for a in sums]  9.3 us

profile of v5, /device:TPU:25, one launch (start us, length us, event | category | flops | bytes accessed | tf_op | source)
XLA Modules:
  0.0 246.0 jit_solution(7524864632931377921)
XLA Ops:
  1.3 42.1 %front.1 = (bf16[2,512,768]{2,1,0:T(8,128)(2,1)}, bf16[2,3,512,768]{3,2,1,0:T(8,128)(2,1)}, bf16[2,512,768]{2,1,0:T(8,128)(2,1)}, bf16[2,512,768]{2,1,0:T(8,128)...) custom-call(s32[1]{0:T(128)S(6)} %copy.29.kind_ref.refs_0_, ...), custom_call_target="tpu_custom_call" | custom-call | tf_op jit(solution)/shard_map/front/pallas_call | solution.py:296
  43.4 187.8 %back.1 = (bf16[6,128,768]{2,1,0:T(8,128)(2,1)}, bf16[6,128,768]{2,1,0:T(8,128)(2,1)}, bf16[192,3072]{1,0:T(8,128)(2,1)}, bf16[192,3072]{1,0:T(8,128)(2,1)}, bf1...) custom-call(s32[1]{0:T(128)S(6)} %copy.29.kind_ref.refs_0_, ...), custom_call_target="tpu_custom_call" | custom-call | tf_op jit(solution)/shard_map/back/pallas_call | solution.py:1128
  231.2 0.8 fusion
  232.0 0.6 constant_dynamic-slice_fusion
  232.7 0.0 copy-start.1
  232.7 3.0 %convert_element_type.21 = f32[192,3072]{1,0:T(8,128)} convert(bf16[192,3072]{1,0:T(8,128)(2,1)} %get-tuple-element.54) | non-fusion elementwise | flops 589824 | bytes 3538944 | tf_op jit(solution)/shard_map/convert_element_type | solution.py:1192
  235.7 0.0 copy-done.1
  235.7 0.0 copy-start
  235.7 1.7 convert_element_type.22
  237.4 0.0 copy-done
  237.4 0.0 copy-start.4
  237.4 1.6 convert_element_type.23
  238.9 0.0 copy-start.6
  238.9 0.0 copy-done.4
  238.9 0.0 copy-start.5
  238.9 0.0 copy-start.7
  238.9 1.3 convert_element_type.18
  240.3 0.0 copy-start.3
  240.3 0.0 copy-done.6
  240.3 0.9 convert_element_type.19
  241.1 0.0 copy-done.5
  241.1 0.0 copy-start.2
  241.1 0.9 convert_element_type.20
  242.0 0.0 copy-done.7
  242.0 0.7 constant_dynamic-slice_fusion.3
  242.7 0.7 constant_dynamic-slice_fusion.2
  243.4 0.6 constant_dynamic-slice_fusion.4
  244.0 0.0 copy-done.3
  244.0 1.0 copy.30
  245.0 0.0 copy-done.2
  245.0 1.0 copy.31
  (3 shorter events, 0.0 us)
Async XLA Ops:
  232.7 3.0 %copy-start.1 = (bf16[192,3072]{1,0:T(8,128)(2,1)S(1)}, bf16[192,3072]{1,0:T(8,128)(2,1)}, u32[]{:S(2)}) copy-start(bf16[192,3072]{1,0:T(8,128)(2,1)} %get-tuple-element.55) | copy-start | bytes 3538948
  235.7 1.7 copy-start
  237.4 1.6 copy-start.4
  238.9 1.3 copy-start.6
  238.9 2.2 copy-start.5
  238.9 3.0 %copy-start.7 = (f32[16,768]{1,0:T(8,128)S(1)}, f32[16,768]{1,0:T(8,128)}, u32[]{:S(2)}) copy-start(f32[16,768]{1,0:T(8,128)} %get-tuple-element.50) | copy-start | bytes 147460
  240.3 3.7 %copy-start.3 = (bf16[6,128,768]{2,1,0:T(8,128)(2,1)S(1)}, bf16[6,128,768]{2,1,0:T(8,128)(2,1)}, u32[]{:S(2)}) copy-start(bf16[6,128,768]{2,1,0:T(8,128)(2,1)} %get-tuple-element.48) | copy-start | bytes 3538948
  241.1 3.9 %copy-start.2 = (bf16[6,128,768]{2,1,0:T(8,128)(2,1)S(1)}, bf16[6,128,768]{2,1,0:T(8,128)(2,1)}, u32[]{:S(2)}) copy-start(bf16[6,128,768]{2,1,0:T(8,128)(2,1)} %get-tuple-element.49) | copy-start | bytes 3538948

commit v6 on v5

--- a/solution.py
+++ b/solution.py
@@ -606,9 +606,6 @@
                 pl.when(sends_half[k])(copy.wait_send)
                 pl.when(gets_half[k])(copy.wait_recv)
 
-    home_start(n2_s, lay6_h, 0, LAY, 0)
-    home_start(n2_s, lay6_h, 1, LAY + 3, 1)
-
     for k in range(4):
         full, part = cot_copies(k)
         full.wait()
@@ -634,6 +631,11 @@
             each(weights(s + 1, 1 - b), "start")
 
         pl.when(s == 3)(loads[-1].start)
+
+        @pl.when(s == 1)
+        def _():
+            home_start(n2_s, lay6_h, 0, LAY, 0)
+            home_start(n2_s, lay6_h, 1, LAY + 3, 1)
 
         @pl.when(s > 0)
         def _():
@@ -1018,6 +1020,11 @@
                 keep_norm(u, rows)
                 token_rows(0, rows, i * RB, u, r)
 
+    def gathers_end(j):
+        each(gathers[j][0], "wait")
+        gathers[j][1].wait()
+        each(core_gathers[4 * j : 4 * j + 4], "start")
+
     def win_product(u, which, dst):
         at = 3 * which + u - 1
         part, cols = at // 2, cols_at(lax.rem(at, 2), h)
@@ -1052,6 +1059,8 @@
     win_product(3, core, raw_of(3))
     unit1(2)
     unit2(1)
+    gathers_end(0)
+    gathers_end(1)
     unit3(0)
     each(down_z, "wait")
     total = d1_s[me, 1].astype(F32)
@@ -1076,9 +1085,6 @@
     small_x.start()
     unit2(3)
     unit3(2)
-    each([c for copies, _ in gathers for c in copies], "wait")
-    each([local for _, local in gathers], "wait")
-    each(core_gathers, "start")
     unit4(1)
     unit5(0)
     unit5(4)
@@ -1088,6 +1094,7 @@
     small_y.start()
     unit3(3)
     unit4(2)
+    gathers_end(2)
     unit5(1)
     small_y.wait()
     ssum_s[2] = ssum_s[1] + sgot_s[2]

time: 250 us -> 239 us (0.956); the launches traced: 246 us -> 238 us
  Pallas kernels: 230 us -> 222 us
    pallas_call x1, Pallas kernels: 188 us -> 180 us  [back(): pl.pallas_call(functools.partial(back_kernel, side), name='back', out_sha...]
where the time goes in v6:
time: 239 us; the launch traced here: 238 us
  Pallas kernels  222 us (93%)
  other arithmetic  9.3 us (4%)
  local copies, waits for them, and re-layouts  5.53 us (2%)
    pallas_call x1, Pallas kernels, back(): pl.pallas_call(functools.partial(back_kernel, side), name='back', out_sha...  180 us
    pallas_call x1, Pallas kernels, front(): pl.pallas_call(front_kernel, name='front', out_shape=(xs, *rest) + tuple(...  42.1 us
    convert_element_type x6, other arithmetic, on_device(): sums = [a.astype(F32) for a in sums]  9.3 us

profile of v6, /device:TPU:25, one launch (start us, length us, event | category | flops | bytes accessed | tf_op | source)
XLA Modules:
  0.0 238.4 jit_solution(1830080294829360658)
XLA Ops:
  1.3 42.1 %front.1 = (bf16[2,512,768]{2,1,0:T(8,128)(2,1)}, bf16[2,3,512,768]{3,2,1,0:T(8,128)(2,1)}, bf16[2,512,768]{2,1,0:T(8,128)(2,1)}, bf16[2,512,768]{2,1,0:T(8,128)...) custom-call(s32[1]{0:T(128)S(6)} %copy.29.kind_ref.refs_0_, ...), custom_call_target="tpu_custom_call" | custom-call | tf_op jit(solution)/shard_map/front/pallas_call | solution.py:296
  43.4 180.2 %back.1 = (bf16[6,128,768]{2,1,0:T(8,128)(2,1)}, bf16[6,128,768]{2,1,0:T(8,128)(2,1)}, bf16[192,3072]{1,0:T(8,128)(2,1)}, bf16[192,3072]{1,0:T(8,128)(2,1)}, bf1...) custom-call(s32[1]{0:T(128)S(6)} %copy.29.kind_ref.refs_0_, ...), custom_call_target="tpu_custom_call" | custom-call | tf_op jit(solution)/shard_map/back/pallas_call | solution.py:1135
  223.6 0.8 fusion
  224.4 0.6 constant_dynamic-slice_fusion
  225.0 0.0 copy-start.1
  225.0 3.0 %convert_element_type.21 = f32[192,3072]{1,0:T(8,128)} convert(bf16[192,3072]{1,0:T(8,128)(2,1)} %get-tuple-element.54) | non-fusion elementwise | flops 589824 | bytes 3538944 | tf_op jit(solution)/shard_map/convert_element_type | solution.py:1199
  228.1 0.0 copy-done.1
  228.1 0.0 copy-start
  228.1 1.7 convert_element_type.22
  229.7 0.0 copy-done
  229.7 0.0 copy-start.4
  229.7 1.6 convert_element_type.23
  231.3 0.0 copy-start.6
  231.3 0.0 copy-done.4
  231.3 0.0 copy-start.5
  231.3 0.0 copy-start.7
  231.3 1.3 convert_element_type.18
  232.6 0.0 copy-start.3
  232.6 0.0 copy-done.6
  232.6 0.9 convert_element_type.19
  233.5 0.0 copy-done.5
  233.5 0.0 copy-start.2
  233.5 0.9 convert_element_type.20
  234.4 0.0 copy-done.7
  234.4 0.7 constant_dynamic-slice_fusion.3
  235.1 0.7 constant_dynamic-slice_fusion.2
  235.8 0.6 constant_dynamic-slice_fusion.4
  236.4 0.0 copy-done.3
  236.4 1.0 copy.30
  237.4 0.0 copy-done.2
  237.4 1.0 copy.31
  (3 shorter events, 0.0 us)
Async XLA Ops:
  225.0 3.0 %copy-start.1 = (bf16[192,3072]{1,0:T(8,128)(2,1)S(1)}, bf16[192,3072]{1,0:T(8,128)(2,1)}, u32[]{:S(2)}) copy-start(bf16[192,3072]{1,0:T(8,128)(2,1)} %get-tuple-element.55) | copy-start | bytes 3538948
  228.1 1.7 copy-start
  229.7 1.6 copy-start.4
  231.3 1.3 copy-start.6
  231.3 2.2 copy-start.5
  231.3 3.0 %copy-start.7 = (f32[16,768]{1,0:T(8,128)S(1)}, f32[16,768]{1,0:T(8,128)}, u32[]{:S(2)}) copy-start(f32[16,768]{1,0:T(8,128)} %get-tuple-element.50) | copy-start | bytes 147460
  232.6 3.7 %copy-start.3 = (bf16[6,128,768]{2,1,0:T(8,128)(2,1)S(1)}, bf16[6,128,768]{2,1,0:T(8,128)(2,1)}, u32[]{:S(2)}) copy-start(bf16[6,128,768]{2,1,0:T(8,128)(2,1)} %get-tuple-element.48) | copy-start | bytes 3538948
  233.5 3.9 %copy-start.2 = (bf16[6,128,768]{2,1,0:T(8,128)(2,1)S(1)}, bf16[6,128,768]{2,1,0:T(8,128)(2,1)}, u32[]{:S(2)}) copy-start(bf16[6,128,768]{2,1,0:T(8,128)(2,1)} %get-tuple-element.49) | copy-start | bytes 3538948

commit v7 on v6

--- a/solution.py
+++ b/solution.py
@@ -688,11 +688,18 @@
             pl.when(s < 3)(unspool(s + 1, (2, 1, 0)[j]).start)
             if j < 2:
                 step_sums(s, j)
-
-    for q in range(4):
-        peer, near = (at_y, by_y) if q % 2 else (at_x, by_x)
-        down_first(q, peer, diag, 0).start()
-        down_first(q, peer, near, 1).start()
+        mine = owner(s)
+
+        @pl.when(lax.rem(mine, 2) == 0)
+        def _():
+            down_first(mine, at_x, diag, 0).start()
+            down_first(mine, at_x, by_x, 1).start()
+
+        @pl.when(lax.rem(mine, 2) == 1)
+        def _():
+            down_first(mine, at_y, diag, 0).start()
+            down_first(mine, at_y, by_y, 1).start()
+
 
     each(win_loads, "start")
     small_s[...] = jnp.zeros_like(small_s)

time: 239 us -> 239 us (level)
  no operation moved by 1% of the time
where the time goes in v7:
time: 239 us; the launch traced here: 237 us
  Pallas kernels  221 us (92%)
  other arithmetic  9.3 us (4%)
  local copies, waits for them, and re-layouts  5.53 us (2%)
    pallas_call x1, Pallas kernels, back(): pl.pallas_call(functools.partial(back_kernel, side), name='back', out_sha...  179 us
    pallas_call x1, Pallas kernels, front(): pl.pallas_call(front_kernel, name='front', out_shape=(xs, *rest) + tuple(...  42.1 us
    convert_element_type x6, other arithmetic, on_device(): sums = [a.astype(F32) for a in sums]  9.3 us

profile of v7, /device:TPU:25, one launch (start us, length us, event | category | flops | bytes accessed | tf_op | source)
XLA Modules:
  0.0 237.3 jit_solution(7529338223732538137)
XLA Ops:
  1.3 42.1 %front.1 = (bf16[2,512,768]{2,1,0:T(8,128)(2,1)}, bf16[2,3,512,768]{3,2,1,0:T(8,128)(2,1)}, bf16[2,512,768]{2,1,0:T(8,128)(2,1)}, bf16[2,512,768]{2,1,0:T(8,128)...) custom-call(s32[1]{0:T(128)S(6)} %copy.29.kind_ref.refs_0_, ...), custom_call_target="tpu_custom_call" | custom-call | tf_op jit(solution)/shard_map/front/pallas_call | solution.py:296
  43.4 179.1 %back.1 = (bf16[6,128,768]{2,1,0:T(8,128)(2,1)}, bf16[6,128,768]{2,1,0:T(8,128)(2,1)}, bf16[192,3072]{1,0:T(8,128)(2,1)}, bf16[192,3072]{1,0:T(8,128)(2,1)}, bf1...) custom-call(s32[1]{0:T(128)S(6)} %copy.29.kind_ref.refs_0_, ...), custom_call_target="tpu_custom_call" | custom-call | tf_op jit(solution)/shard_map/back/pallas_call | solution.py:1142
  222.5 0.8 fusion
  223.3 0.6 constant_dynamic-slice_fusion
  223.9 0.0 copy-start.1
  223.9 3.0 %convert_element_type.21 = f32[192,3072]{1,0:T(8,128)} convert(bf16[192,3072]{1,0:T(8,128)(2,1)} %get-tuple-element.54) | non-fusion elementwise | flops 589824 | bytes 3538944 | tf_op jit(solution)/shard_map/convert_element_type | solution.py:1206
  227.0 0.0 copy-done.1
  227.0 0.0 copy-start
  227.0 1.7 convert_element_type.22
  228.6 0.0 copy-done
  228.6 0.0 copy-start.4
  228.6 1.6 convert_element_type.23
  230.2 0.0 copy-start.6
  230.2 0.0 copy-done.4
  230.2 0.0 copy-start.5
  230.2 0.0 copy-start.7
  230.2 1.3 convert_element_type.18
  231.6 0.0 copy-start.3
  231.6 0.0 copy-done.6
  231.6 0.9 convert_element_type.19
  232.4 0.0 copy-done.5
  232.4 0.0 copy-start.2
  232.4 0.9 convert_element_type.20
  233.3 0.0 copy-done.7
  233.3 0.7 constant_dynamic-slice_fusion.3
  234.0 0.7 constant_dynamic-slice_fusion.2
  234.7 0.6 constant_dynamic-slice_fusion.4
  235.3 0.0 copy-done.3
  235.3 1.0 copy.30
  236.3 0.0 copy-done.2
  236.3 1.0 copy.31
  (3 shorter events, 0.0 us)
Async XLA Ops:
  223.9 3.0 %copy-start.1 = (bf16[192,3072]{1,0:T(8,128)(2,1)S(1)}, bf16[192,3072]{1,0:T(8,128)(2,1)}, u32[]{:S(2)}) copy-start(bf16[192,3072]{1,0:T(8,128)(2,1)} %get-tuple-element.55) | copy-start | bytes 3538948
  227.0 1.7 copy-start
  228.6 1.6 copy-start.4
  230.2 1.3 copy-start.6
  230.2 2.2 copy-start.5
  230.2 3.0 %copy-start.7 = (f32[16,768]{1,0:T(8,128)S(1)}, f32[16,768]{1,0:T(8,128)}, u32[]{:S(2)}) copy-start(f32[16,768]{1,0:T(8,128)} %get-tuple-element.50) | copy-start | bytes 147460
  231.6 3.7 %copy-start.3 = (bf16[6,128,768]{2,1,0:T(8,128)(2,1)S(1)}, bf16[6,128,768]{2,1,0:T(8,128)(2,1)}, u32[]{:S(2)}) copy-start(bf16[6,128,768]{2,1,0:T(8,128)(2,1)} %get-tuple-element.48) | copy-start | bytes 3538948
  232.4 3.9 %copy-start.2 = (bf16[6,128,768]{2,1,0:T(8,128)(2,1)S(1)}, bf16[6,128,768]{2,1,0:T(8,128)(2,1)}, u32[]{:S(2)}) copy-start(bf16[6,128,768]{2,1,0:T(8,128)(2,1)} %get-tuple-element.49) | copy-start | bytes 3538948
